TPU v7x, 512 devices: a whole 4x4x16 slice. The times are simulated.
512 devices in a mesh: slab: 64 (over z, x_hi, core), band: 8 (over y, x_lo).
Axes of the slice: x: 4 (x_hi: 2, x_lo: 2; x = x_hi * 2 + x_lo), y: 4, z: 16, core: 2. Of those that a mesh axis runs over, the one named last changes fastest.
Arguments:
- hamiltonian: bfloat16 [512, 7, 128, 128], P('slab', None, 'band'), may hold values from -0.1875 to 0.1875
- neighbors: int32 [512, 7], P('slab'), may hold values from 0 to 11, as said below
- orbitals: bfloat16 [65536, 1024], P('slab', 'band'), may hold values from -6 to 6
Outputs:
- residual: bfloat16 [65536, 1024], P(('slab', 'band'))
Inputs may be any that keep to these rules, and one draw needn't show every extreme that they name: `neighbors`: window positions 0 to 1 are the last 2 elements of the slab below (periodic), 2 to 9 the slab's own elements, the rest the first 2 elements of the slab above. A slab's elements are in layers of 2; each block row names, in an order of its own, itself, the element 2 positions below and above it in the window, and four elements of its own layer (repeats possible).
All inputs are finite; a program needn't handle non-finite values.
Results may differ from a plain program's by a relative error of at most 0.012.
Values may be sent and summed in bfloat16 or wider, within the bound.
No kernel may reach another device: no remote copies, remote signals or barrier semaphores. Data moves between devices by JAX's collectives and lax.ppermute only.
A program may use at most 64 MiB of HBM per device.

v0:
```python
import math

import jax
import jax.numpy as jnp
from jax import lax
from jax.sharding import PartitionSpec as P

FACE = 2


def padded(block, sides, width):
    for axis, dim in sides:
        count = lax.axis_size(axis)
        forward = [(i, i + 1) for i in range(count - 1)]
        forward.append((count - 1, 0))
        backward = [(target, source) for source, target in forward]
        low = lax.ppermute(
            lax.slice_in_dim(block, block.shape[dim] - width, None, axis=dim), axis, forward
        )
        high = lax.ppermute(lax.slice_in_dim(block, 0, width, axis=dim), axis, backward)
        block = jnp.concatenate([low, block, high], axis=dim)
    return block


def apply_local(vector, full_tiles, neighbors):
    tile_size = full_tiles.shape[2]
    extended = padded(vector, (("slab", 0),), FACE * tile_size)
    blocks = extended.reshape(-1, tile_size, vector.shape[1])
    picked_blocks = blocks[neighbors]
    product = jnp.einsum(
        "rjab,rjbc->rac", full_tiles, picked_blocks, preferred_element_type=jnp.float32
    )
    return product.reshape(vector.shape[0], vector.shape[1])


def body(hamiltonian, neighbors, orbitals):
    full_tiles = lax.all_gather(hamiltonian, "band", axis=2, tiled=True)
    first = apply_local(orbitals, full_tiles, neighbors).astype(jnp.bfloat16)
    second = (
        2.0 * apply_local(first, full_tiles, neighbors) - orbitals.astype(jnp.float32)
    ).astype(jnp.bfloat16)
    third = (2.0 * apply_local(second, full_tiles, neighbors) - first.astype(jnp.float32)).astype(
        jnp.bfloat16
    )
    applied = apply_local(third, full_tiles, neighbors).astype(jnp.bfloat16)
    rows_all = orbitals.shape[0] * lax.axis_size("slab")
    bands_all = orbitals.shape[1] * lax.axis_size("band")
    gram_scale = 1.0 / math.sqrt(float(rows_all) * float(bands_all))
    strip_third, strip_applied = (
        lax.all_to_all(third, "band", split_axis=0, concat_axis=1, tiled=True),
        lax.all_to_all(applied, "band", split_axis=0, concat_axis=1, tiled=True),
    )
    partial_value = jnp.einsum(
        "rb,rc->bc", strip_third, strip_applied, preferred_element_type=jnp.float32
    )
    summed = lax.psum(partial_value, ("slab", "band"))
    gram_full = (summed * gram_scale).astype(jnp.bfloat16)
    mixed = jnp.dot(strip_third, gram_full, preferred_element_type=jnp.float32)
    return (strip_applied.astype(jnp.float32) - mixed).astype(jnp.bfloat16)


def solution(mesh):
    in_specs = (P("slab", None, "band", None), P("slab", None), P("slab", "band"))
    out_specs = P(("slab", "band"), None)
    return jax.shard_map(body, mesh=mesh, in_specs=in_specs, out_specs=out_specs, check_vma=False)
```

profile of v0, /device:TPU:1, one launch (start us, length us, event | category | flops | bytes accessed | tf_op | source)
XLA Modules:
  0.0 639.2 jit_solution(16940214057220224389)
XLA Ops:
  6.5 0.0 all-gather.2.cloned.1.call-start
  6.5 0.7 all-gather.2.cloned.1.call-update
  7.3 0.9 fusion.16
  8.1 6.0 collective-permute-start
  14.2 4.6 collective-permute-start.1
  18.8 0.7 compare_select_fusion
  19.5 0.1 reshape.35
  19.6 0.0 collective-permute-done
  19.6 1.7 collective-permute-done.1
  21.3 1.0 pad_maximum_fusion
  22.3 0.9 gather_fusion
  23.2 44.6 %all-gather.2.cloned.1.call-done = bf16[8,7,128,128]{3,2,1,0:T(8,128)(2,1)} async-done(((bf16[8,7,16,128]{3,2,1,0:T(8,128)(2,1)}), bf16[8,7,128,128]{3,2,1,0:T(8,128)(2,1)}) %all-gather.2.cloned.1.call-update) | async-done | bytes 1835024 | tf_op jit(solution)/shard_map/all_gather | solution.py:37
  67.7 2.1 fusion.6
  69.9 4.5 collective-permute-start.3
  74.4 4.4 collective-permute-start.2
  78.8 0.0 collective-permute-done.3
  78.8 1.3 collective-permute-done.2
  80.2 0.0 copy-start
  80.2 2.0 gather_fusion.1
  82.2 0.0 copy-done
  82.2 2.2 fusion.3
  84.4 0.0 copy-done.1
  84.4 0.1 fusion.10
  84.5 5.8 collective-permute-start.4
  90.3 3.9 collective-permute-start.5
  94.1 0.0 collective-permute-done.4
  94.1 3.2 collective-permute-done.5
  97.4 2.1 gather_fusion.2
  99.4 2.1 fusion.4
  101.6 0.1 fusion.9
  101.7 1.9 collective-permute-start.6
  103.6 5.9 collective-permute-start.7
  109.5 0.8 fusion.11
  110.3 4.2 all-to-all-start.1
  114.5 0.0 collective-permute-done.6
  114.5 0.0 collective-permute-done.7
  114.6 2.1 gather_fusion.3
  116.6 3.0 fusion.8
  119.6 1.0 all-to-all-done.1
  120.7 4.1 all-to-all-start
  124.8 0.0 all-reduce.2.cloned.1.call-start
  124.8 0.2 copy.7
  125.0 5.9 all-to-all-done
  130.9 2.7 fusion.17
  133.6 0.0 all-reduce.2.cloned.1.call-update
  133.6 0.1 copy.6
  133.8 495.2 %all-reduce.2.cloned.1.call-done = f32[1024,1024]{1,0:T(8,128)} async-done(((f32[1024,1024]{1,0:T(8,128)}), f32[1024,1024]{1,0:T(8,128)}) %all-reduce.2.cloned.1.call-update) | async-done | bytes 4194320 | tf_op jit(solution)/shard_map/psum | solution.py:56
  629.0 3.4 fusion.7
  (8 shorter events, 0.1 us)
Async XLA Ops:
  6.5 61.2 %all-gather.2.cloned.1.call-start = ((), (), s32[]{:S(2)}) async-start(), calls=%async_computation.2 | async-start | bytes 2064384 | tf_op jit(solution)/shard_map/all_gather | solution.py:37
  8.1 11.5 %collective-permute-start = (bf16[256,128]{1,0:T(8,128)(2,1)S(1)}, bf16[256,128]{1,0:T(8,128)(2,1)S(1)}, u32[]{:S(2)}, u32[]{:S(2)}) collective-permute-start(bf16[256,128]{1,0:T(8,128)(2,1)S(1)} %get-tuple-element.11), channel_id=1, source_target_pairs={{0,8},{8,16},{16,24},{24,32},{32,40},{40,48},{48,56},{56,64},{64,7... | collective-permute-start | bytes 196616 | tf_op jit(solution)/shard_map/ppermute | solution.py:17
  14.2 7.1 %collective-permute-start.1 = (bf16[256,128]{1,0:T(8,128)(2,1)S(1)}, bf16[256,128]{1,0:T(8,128)(2,1)S(1)}, u32[]{:S(2)}, u32[]{:S(2)}) collective-permute-start(bf16[256,128]{1,0:T(8,128)(2,1)S(1)} %get-tuple-element.12), channel_id=1, source_target_pairs={{8,0},{16,8},{24,16},{32,24},{40,32},{48,40},{56,48},{64,56},{72,6... | collective-permute-start | bytes 196616 | tf_op jit(solution)/shard_map/ppermute | solution.py:20
  69.9 8.9 %collective-permute-start.3 = (bf16[256,128]{1,0:T(8,128)(2,1)S(1)}, bf16[256,128]{1,0:T(8,128)(2,1)S(1)}, u32[]{:S(2)}, u32[]{:S(2)}) collective-permute-start(bf16[256,128]{1,0:T(8,128)(2,1)S(1)} %bitcast.84), channel_id=1, source_target_pairs={{8,0},{16,8},{24,16},{32,24},{40,32},{48,40},{56,48},{64,56},{72,6... | collective-permute-start | bytes 196616 | tf_op jit(solution)/shard_map/ppermute | solution.py:20
  74.4 5.8 collective-permute-start.2
  80.2 2.0 copy-start
  82.2 2.2 copy-start.1
  84.5 9.7 %collective-permute-start.4 = (bf16[256,128]{1,0:T(8,128)(2,1)S(1)}, bf16[256,128]{1,0:T(8,128)(2,1)S(1)}, u32[]{:S(2)}, u32[]{:S(2)}) collective-permute-start(bf16[256,128]{1,0:T(8,128)(2,1)S(1)} %get-tuple-element.7), channel_id=1, source_target_pairs={{0,8},{8,16},{16,24},{24,32},{32,40},{40,48},{48,56},{56,64},{64,7... | collective-permute-start | bytes 196616 | tf_op jit(solution)/shard_map/ppermute | solution.py:17
  90.3 7.1 %collective-permute-start.5 = (bf16[256,128]{1,0:T(8,128)(2,1)S(1)}, bf16[256,128]{1,0:T(8,128)(2,1)S(1)}, u32[]{:S(2)}, u32[]{:S(2)}) collective-permute-start(bf16[256,128]{1,0:T(8,128)(2,1)S(1)} %get-tuple-element.8), channel_id=1, source_target_pairs={{8,0},{16,8},{24,16},{32,24},{40,32},{48,40},{56,48},{64,56},{72,6... | collective-permute-start | bytes 196616 | tf_op jit(solution)/shard_map/ppermute | solution.py:20
  101.7 12.9 %collective-permute-start.6 = (bf16[256,128]{1,0:T(8,128)(2,1)S(1)}, bf16[256,128]{1,0:T(8,128)(2,1)S(1)}, u32[]{:S(2)}, u32[]{:S(2)}) collective-permute-start(bf16[256,128]{1,0:T(8,128)(2,1)S(1)} %get-tuple-element.5), channel_id=1, source_target_pairs={{0,8},{8,16},{16,24},{24,32},{32,40},{40,48},{48,56},{56,64},{64,7... | collective-permute-start | bytes 196616 | tf_op jit(solution)/shard_map/ppermute | solution.py:17
  103.6 10.9 %collective-permute-start.7 = (bf16[256,128]{1,0:T(8,128)(2,1)S(1)}, bf16[256,128]{1,0:T(8,128)(2,1)S(1)}, u32[]{:S(2)}, u32[]{:S(2)}) collective-permute-start(bf16[256,128]{1,0:T(8,128)(2,1)S(1)} %get-tuple-element.6), channel_id=1, source_target_pairs={{8,0},{16,8},{24,16},{32,24},{40,32},{48,40},{56,48},{64,56},{72,6... | collective-permute-start | bytes 196616 | tf_op jit(solution)/shard_map/ppermute | solution.py:20
  110.3 10.3 %all-to-all-start.1 = ((bf16[8,128,128]{2,1,0:T(8,128)(2,1)}), bf16[8,128,128]{2,1,0:T(8,128)(2,1)S(1)}, u32[]{:S(2)}, u32[]{:S(2)}) async-start(bf16[8,128,128]{2,1,0:T(8,128)(2,1)} %fusion.11), calls=%async_computation.1 | async-start | bytes 524288 | tf_op jit(solution)/shard_map/all_to_all | solution.py:50
  120.7 10.2 %all-to-all-start = ((bf16[8,128,128]{1,2,0:T(8,128)(2,1)}), bf16[8,128,128]{1,2,0:T(8,128)(2,1)S(1)}, u32[]{:S(2)}, u32[]{:S(2)}) async-start(bf16[8,128,128]{1,2,0:T(8,128)(2,1)} %fusion.8), calls=%async_computation | async-start | bytes 524288 | tf_op jit(solution)/shard_map/all_to_all | solution.py:51
  124.8 504.2 %all-reduce.2.cloned.1.call-start = ((), (), s32[]{:S(2)}) async-start(), calls=%async_computation.3 | async-start | bytes 8388608 | tf_op jit(solution)/shard_map/psum | solution.py:56
Sparse Core Ops, SparseCore 0:
  9.3 58.3 all-gather.1
  133.7 495.2 all-reduce.1
where the time goes:
time: 641 us; the launch traced here: 639 us
  waiting for transfers between devices  554 us (86%)
  starting transfers between devices  45.4 us (7%)
  matrix products  15.5 us (2%)
  between operations  13.6 us (2%)
  local copies, waits for them, and re-layouts  8.39 us (1%)
    psum x1, waiting for transfers between devices, body(): summed = lax.psum(partial_value, ('slab', 'band'))  495 us
    all_gather x1, waiting for transfers between devices, body(): full_tiles = lax.all_gather(hamiltonian, 'band', axis=2, tiled=True)  44.6 us
    ppermute x4, starting transfers between devices, padded(): lax.ppermute(lax.slice_in_dim(block, 0, width, axis=dim), axis, backward)  18.9 us
    ppermute x4, starting transfers between devices, padded(): lax.ppermute(lax.slice_in_dim(block, block.shape[dim] - width, None, axis...  18.2 us
  transfers between devices with their start and end apart: 12, of which 7 were waited for; matrix products, arithmetic and copies ran while one was open for 2% of the time, Pallas kernels for 0%

commit v1 on v0

v1 whole, which is shorter than its diff:
```python
import functools
import math

import jax
import jax.numpy as jnp
import numpy as np
from jax import lax
from jax.experimental import pallas as pl
from jax.experimental.pallas import tpu as pltpu
from jax.sharding import Mesh
from jax.sharding import PartitionSpec as P

SLAB = ("z2", "z1", "xh", "core")
BAND = ("y", "xl")
NEAR = ("z1", "xh", "core")
FACE = 2
F32 = jnp.float32
BF16 = jnp.bfloat16

VMEM = pl.BlockSpec(memory_space=pltpu.VMEM)
SMEM = pl.BlockSpec(memory_space=pltpu.SMEM)


def dot(a, b, dims=((1,), (0,))):
    return lax.dot_general(a, b, (dims, ((), ())), preferred_element_type=F32)


def call(kernel, outs, args, scratch=(), smem=0):
    return pl.pallas_call(
        kernel,
        out_shape=[jax.ShapeDtypeStruct(shape, BF16) for shape in outs],
        in_specs=[SMEM] * smem + [VMEM] * (len(args) - smem),
        out_specs=[VMEM] * len(outs),
        scratch_shapes=list(scratch),
    )(*args)


def combine_kernel(nbr, ham, out):
    blocks, slots = ham.shape[0], ham.shape[1]
    width = ham.shape[3]
    for r in range(blocks):
        layer = FACE + r // FACE * FACE
        for k, position in enumerate((r, layer, layer + 1, r + 2 * FACE)):
            total = jnp.zeros(ham.shape[2:], F32)
            for j in range(slots):
                keep = (nbr[r, j] == position).astype(F32)
                total = total + keep * ham[r, j].astype(F32)
            total = total.astype(BF16)
            for copy in range(out.shape[0]):
                out[copy, r, :, k * width : (k + 1) * width] = total


def apply_kernel(prior, copies, core, ham, vec, from_a, from_b, *rest):
    before = rest[0] if prior else None
    rest = rest[1:] if prior else rest
    ext = rest[-1]
    edge = from_a.shape[0]
    rows = vec.shape[0]
    tile = edge // FACE
    c = core[0]
    ext[edge : edge + rows] = vec[...]
    ext[pl.ds(pl.multiple_of((1 - c) * (edge + rows), edge), edge)] = from_a[...]
    ext[pl.ds(pl.multiple_of(c * (edge + rows), edge), edge)] = from_b[...]
    out = rest[0]
    for r in range(rows // tile):
        layer = FACE + r // FACE * FACE
        lhs = ham[:, r].reshape(tile, 4 * tile)
        rhs = jnp.concatenate(
            [
                ext[r * tile : (r + 1) * tile],
                ext[layer * tile : (layer + FACE) * tile],
                ext[(r + 2 * FACE) * tile : (r + 2 * FACE + 1) * tile],
            ],
            axis=0,
        )
        value = dot(lhs, rhs)
        here = slice(r * tile, (r + 1) * tile)
        if prior:
            value = 2.0 * value - before[here].astype(F32)
        value = value.astype(BF16)
        out[here] = value
        if copies:
            for copy in range(copies):
                rest[3][copy, here] = value
    if len(rest) > 2:
        rest[1][...] = out[pl.ds(pl.multiple_of((1 - c) * (rows - edge), edge), edge)]
        rest[2][...] = out[pl.ds(pl.multiple_of(c * (rows - edge), edge), edge)]


def gram_kernel(third, own, other, out):
    right = jnp.concatenate([own[...], other[...]], axis=1)
    share = out.shape[1]
    per = third.shape[2] // share
    for y in range(third.shape[0]):
        block = dot(third[y], right, ((0,), (0,))).astype(BF16)
        for i in range(per):
            out[y * per + i] = block[i * share : (i + 1) * share]


def sum_kernel(scale, parts, out):
    total = parts[0].astype(F32)
    for i in range(1, parts.shape[0]):
        total = total + parts[i].astype(F32)
    if scale is not None:
        total = total * scale
    total = total.astype(BF16)
    for copy in range(out.shape[0]):
        out[copy] = total


def mixed_kernel(third, gram, applied, out):
    strips, height = out.shape[0], out.shape[1]
    width = third.shape[2]
    depth = third.shape[0] * width
    weights = gram[...].reshape(depth, gram.shape[2])
    for s in range(strips):
        here = slice(s * height, (s + 1) * height)
        left = jnp.concatenate([third[y, here] for y in range(third.shape[0])], axis=1)
        value = dot(left, weights)
        out[s, :, :width] = (applied[here].astype(F32) - value[:, :width]).astype(BF16)
        out[s, :, width:] = (-value[:, width:]).astype(BF16)


def final_kernel(parts, out):
    width = parts.shape[2] // 2
    for b in range(parts.shape[0]):
        value = parts[b, :, :width].astype(F32) + parts[b ^ 1, :, width:].astype(F32)
        out[:, b * width : (b + 1) * width] = value.astype(BF16)


def gather(copies, axes):
    return lax.all_to_all(copies, axes, 0, 0, tiled=True)


def swap(near, far):
    count = lax.axis_size(SLAB)
    pairs = [(s, (s + 1) % count if s % 2 else (s - 1) % count) for s in range(count)]
    return (
        lax.ppermute(near, "core", [(0, 1), (1, 0)]),
        lax.ppermute(far, SLAB, pairs),
    )


def body(hamiltonian, neighbors, orbitals):
    blocks, _, strip, tile = hamiltonian.shape
    rows, width = orbitals.shape
    edge = FACE * tile
    ny, nband, near, far = (lax.axis_size(a) for a in ("y", BAND, NEAR, "z2"))
    core = lax.axis_index("core")
    scalar = core.astype(jnp.int32).reshape(1)

    (shares,) = call(
        combine_kernel, [(nband, blocks, strip, 4 * tile)], (neighbors, hamiltonian), smem=1
    )
    tiles = gather(shares, BAND)
    received = swap(
        lax.dynamic_slice_in_dim(orbitals, (1 - core) * (rows - edge), edge, 0),
        lax.dynamic_slice_in_dim(orbitals, core * (rows - edge), edge, 0),
    )

    def apply(vec, received, before=None, copies=0, edges=True):
        args = (scalar, tiles, vec, *received) + (() if before is None else (before,))
        outs = [(rows, width)] + [(edge, width)] * (2 if edges else 0)
        if copies:
            outs.append((copies, rows, width))
        return call(
            functools.partial(apply_kernel, before is not None, copies),
            outs,
            args,
            (pltpu.VMEM((rows + 2 * edge, width), BF16),),
            smem=1,
        )

    first, *edges = apply(orbitals, received)
    second, *edges = apply(first, swap(*edges), orbitals)
    third, *edges, copies = apply(second, swap(*edges), first, copies=ny)
    third_all = gather(copies, "y")
    (applied,) = apply(third, swap(*edges), edges=False)
    other = lax.ppermute(applied, "xl", [(0, 1), (1, 0)])

    rows_all = rows * lax.axis_size(SLAB)
    scale = 1.0 / math.sqrt(float(rows_all) * float(width * nband))
    share = ny * width // near
    (partial_gram,) = call(gram_kernel, [(near, share, 2 * width)], (third_all, applied, other))
    (summed,) = call(
        functools.partial(sum_kernel, None),
        [(far, share, 2 * width)],
        (gather(partial_gram, NEAR),),
    )
    (scaled,) = call(
        functools.partial(sum_kernel, scale),
        [(near, share, 2 * width)],
        (gather(summed, "z2"),),
    )
    gram = gather(scaled, NEAR)
    (partial_out,) = call(
        mixed_kernel, [(nband, rows // nband, 2 * width)], (third_all, gram, applied)
    )
    (out,) = call(final_kernel, [(rows // nband, nband * width)], (gather(partial_out, BAND),))
    return out


def solution(mesh):
    slabs = mesh.shape["slab"]
    fine = Mesh(
        np.asarray(mesh.devices).reshape(slabs // 16, 4, 2, 2, mesh.shape["band"] // 2, 2),
        SLAB + BAND,
    )
    in_specs = (P(SLAB, None, BAND, None), P(SLAB, None), P(SLAB, BAND))
    out_specs = P(SLAB + BAND, None)
    return jax.shard_map(body, mesh=fine, in_specs=in_specs, out_specs=out_specs, check_vma=False)
```

time: 641 us -> 172 us (0.27)
  waiting for transfers between devices: 554 us -> 28.5 us
  blocking collectives: 0 us -> 70.8 us
  Pallas kernels: 0 us -> 22.9 us
  matrix products: 15.5 us -> 0 us
  between operations: 13.6 us -> 0.2 us
    psum x1 -> x0, waiting for transfers between devices: 495 us -> none  [body(): summed = lax.psum(partial_value, ('slab', 'band'))]
    all_to_all x0 -> x4, blocking collectives: none -> 70.8 us  [gather(): return lax.all_to_all(copies, axes, 0, 0, tiled=True)]
    all_gather x1 -> x0, waiting for transfers between devices: 44.6 us -> none  [body(): full_tiles = lax.all_gather(hamiltonian, 'band', axis=2, tiled=True)]
    pallas_call x0 -> x10, Pallas kernels: none -> 22.9 us  [call(): pl.pallas_call(kernel, out_shape=[jax.ShapeDtypeStruct(shape, BF16) for s...]
    ppermute x8 -> x9, waiting for transfers between devices: 6.17 us -> 28.5 us  [the longest x4 22.6 us: swap(): lax.ppermute(far, SLAB, pairs)]
    dot_general x6 -> x0, matrix products: 15.5 us -> none  [the longest x4 9.39 us: apply_local(): jnp.einsum('rjab,rjbc->rac', full_tiles, picked_blocks, preferred_element...]
    gather x4 -> x0, local copies, waits for them, and re-layouts: 7.06 us -> none  [apply_local(): picked_blocks = blocks[neighbors]]
    all_to_all x2, waiting for transfers between devices: 6.94 us -> 0.01 us  [gather(): return lax.all_to_all(copies, axes, 0, 0, tiled=True)]
  transfers between devices with their start and end apart: 12 -> 11, of which waited for: 7 -> 5; matrix products, arithmetic and copies ran while one was open for 2% -> 0% of each run, Pallas kernels for 0% -> 1%
where the time goes in v1:
time: 172 us; the launch traced here: 171 us
  blocking collectives  70.8 us (41%)
  starting transfers between devices  44.3 us (26%)
  waiting for transfers between devices  28.5 us (17%)
  Pallas kernels  22.9 us (13%)
  local copies, waits for them, and re-layouts  4.59 us (3%)
    all_to_all x4, blocking collectives, gather(): return lax.all_to_all(copies, axes, 0, 0, tiled=True)  70.8 us
    ppermute x4, starting transfers between devices, swap(): lax.ppermute(near, 'core', [(0, 1), (1, 0)])  24.6 us
    pallas_call x10, Pallas kernels, call(): pl.pallas_call(kernel, out_shape=[jax.ShapeDtypeStruct(shape, BF16) for s...  22.9 us
    ppermute x4, waiting for transfers between devices, swap(): lax.ppermute(far, SLAB, pairs)  22.6 us
    all_to_all x2, starting transfers between devices, gather(): return lax.all_to_all(copies, axes, 0, 0, tiled=True)  9.72 us
    ppermute x4, starting transfers between devices, swap(): lax.ppermute(far, SLAB, pairs)  8.13 us
    ppermute x1, waiting for transfers between devices, body(): other = lax.ppermute(applied, 'xl', [(0, 1), (1, 0)])  5.92 us
    unnamed x28, local copies, waits for them, and re-layouts  4.58 us
  transfers between devices with their start and end apart: 11, of which 5 were waited for; matrix products, arithmetic and copies ran while one was open for 0% of the time, Pallas kernels for 1%

profile of v1, /device:TPU:1, one launch (start us, length us, event | category | flops | bytes accessed | tf_op | source)
XLA Modules:
  0.0 171.3 jit_solution(10779126346326121295)
XLA Ops:
  0.0 2.2 %shard_map.37 = bf16[8,8,16,512]{3,2,1,0:T(8,128)(2,1)} custom-call(s32[8,7]{1,0:T(8,128)} %nbr.1, bf16[8,7,16,128]{3,2,1,0:T(8,128)(2,1)} %ham.1), custom_call_target="tpu_custom_call" | custom-call | tf_op jit(solution)/shard_map/pallas_call | solution.py:29
  2.2 6.1 %all-to-all-start = ((bf16[8,8,16,512]{3,2,1,0:T(8,128)(2,1)}), bf16[8,8,16,512]{3,2,1,0:T(8,128)(2,1)S(1)}, u32[]{:S(2)}, u32[]{:S(2)}) async-start(bf16[8,8,16,512]{3,2,1,0:T(8,128)(2,1)} %shard_map.37), calls=%async_computation | async-start | bytes 2097152 | tf_op jit(solution)/shard_map/all_to_all | solution.py:132
  8.3 0.0 copy-done.2
  8.3 6.4 %collective-permute-start = (bf16[256,128]{1,0:T(8,128)(2,1)S(1)}, bf16[256,128]{1,0:T(8,128)(2,1)S(1)}, u32[]{:S(2)}, u32[]{:S(2)}) collective-permute-start(bf16[256,128]{1,0:T(8,128)(2,1)S(1)} %get-tuple-element.26), channel_id=1, source_target_pairs={{0,8},{8,0},{1,9},{9,1},{2,10},{10,2},{3,11},{11,3},{4,12},{12,4},... | collective-permute-start | bytes 196616 | tf_op jit(solution)/shard_map/ppermute | solution.py:139
  14.7 1.9 %collective-permute-start.1 = (bf16[256,128]{1,0:T(8,128)(2,1)S(1)}, bf16[256,128]{1,0:T(8,128)(2,1)S(1)}, u32[]{:S(2)}, u32[]{:S(2)}) collective-permute-start(bf16[256,128]{1,0:T(8,128)(2,1)S(1)} %get-tuple-element.25), channel_id=1, source_target_pairs={{0,504},{8,16},{16,8},{24,32},{32,24},{40,48},{48,40},{56,64},{64,... | collective-permute-start | bytes 196616 | tf_op jit(solution)/shard_map/ppermute | solution.py:140
  16.6 0.0 collective-permute-done.from_a
  16.6 0.0 copy-start.10
  16.6 7.2 %collective-permute-done.1.from_b = bf16[256,128]{1,0:T(8,128)(2,1)S(1)} collective-permute-done((bf16[256,128]{1,0:T(8,128)(2,1)S(1)}, bf16[256,128]{1,0:T(8,128)(2,1)S(1)}, u32[]{:S(2)}, u32[]{:S(2)}) %collective-permute-start.1) | collective-permute-done | bytes 65568 | tf_op jit(solution)/shard_map/ppermute | solution.py:140
  23.9 0.0 all-to-all-done.ham
  23.9 0.0 copy-done.10
  23.9 0.6 copy-done.11
  24.5 0.4 copy-done
  24.9 2.5 %shard_map.38 = (bf16[1024,128]{1,0:T(8,128)(2,1)}, bf16[256,128]{1,0:T(8,128)(2,1)}, bf16[256,128]{1,0:T(8,128)(2,1)}) custom-call(s32[1]{0:T(128)} %bitcast.core, bf16[8,8,16,512]{3,2,1,0:T(8,128)(2,1)} %copy-done, bf16[1024,128]{1,0:T(8,128)(2,1)} %rest_0_.1, bf16[256,128]{1,0:T(8,128)(2,1)} %copy-done.10, bf16[256,128]{1,0:T(8,128)(2,1)} %copy-done.11), custom_call_target="tpu_custom_call" | custom-call | tf_op jit(solution)/shard_map/pallas_call | solution.py:29
  27.4 4.8 %collective-permute-start.2 = (bf16[256,128]{1,0:T(8,128)(2,1)}, bf16[256,128]{1,0:T(8,128)(2,1)S(1)}, u32[]{:S(2)}, u32[]{:S(2)}) collective-permute-start(bf16[256,128]{1,0:T(8,128)(2,1)} %get-tuple-element.16), channel_id=1, source_target_pairs={{0,8},{8,0},{1,9},{9,1},{2,10},{10,2},{3,11},{11,3},{4,12},{12,4},... | collective-permute-start | bytes 196616 | tf_op jit(solution)/shard_map/ppermute | solution.py:139
  32.2 2.4 %collective-permute-start.3 = (bf16[256,128]{1,0:T(8,128)(2,1)}, bf16[256,128]{1,0:T(8,128)(2,1)S(1)}, u32[]{:S(2)}, u32[]{:S(2)}) collective-permute-start(bf16[256,128]{1,0:T(8,128)(2,1)} %get-tuple-element.17), channel_id=1, source_target_pairs={{0,504},{8,16},{16,8},{24,32},{32,24},{40,48},{48,40},{56,64},{64,... | collective-permute-start | bytes 196616 | tf_op jit(solution)/shard_map/ppermute | solution.py:140
  34.6 0.0 collective-permute-done.2.from_a
  34.6 4.9 %collective-permute-done.3.from_b = bf16[256,128]{1,0:T(8,128)(2,1)S(1)} collective-permute-done((bf16[256,128]{1,0:T(8,128)(2,1)}, bf16[256,128]{1,0:T(8,128)(2,1)S(1)}, u32[]{:S(2)}, u32[]{:S(2)}) %collective-permute-start.3) | collective-permute-done | bytes 65568 | tf_op jit(solution)/shard_map/ppermute | solution.py:140
  39.5 0.0 copy-done.5
  39.5 0.6 copy-done.8
  40.1 2.6 %shard_map.39 = (bf16[1024,128]{1,0:T(8,128)(2,1)}, bf16[256,128]{1,0:T(8,128)(2,1)}, bf16[256,128]{1,0:T(8,128)(2,1)}) custom-call(s32[1]{0:T(128)} %bitcast.core, bf16[8,8,16,512]{3,2,1,0:T(8,128)(2,1)} %copy-done, bf16[1024,128]{1,0:T(8,128)(2,1)} %get-tuple-element.15.vec.rest_0_, bf16[256,128]{1,0:T(8,128)(2,1)} %copy-done.5, ...), custom_call_target="tpu_custom_call" | custom-call | tf_op jit(solution)/shard_map/pallas_call | solution.py:29
  42.7 9.3 %collective-permute-start.4 = (bf16[256,128]{1,0:T(8,128)(2,1)}, bf16[256,128]{1,0:T(8,128)(2,1)S(1)}, u32[]{:S(2)}, u32[]{:S(2)}) collective-permute-start(bf16[256,128]{1,0:T(8,128)(2,1)} %get-tuple-element.19), channel_id=1, source_target_pairs={{0,8},{8,0},{1,9},{9,1},{2,10},{10,2},{3,11},{11,3},{4,12},{12,4},... | collective-permute-start | bytes 196616 | tf_op jit(solution)/shard_map/ppermute | solution.py:139
  52.0 1.9 %collective-permute-start.5 = (bf16[256,128]{1,0:T(8,128)(2,1)}, bf16[256,128]{1,0:T(8,128)(2,1)S(1)}, u32[]{:S(2)}, u32[]{:S(2)}) collective-permute-start(bf16[256,128]{1,0:T(8,128)(2,1)} %get-tuple-element.20), channel_id=1, source_target_pairs={{0,504},{8,16},{16,8},{24,32},{32,24},{40,48},{48,40},{56,64},{64,... | collective-permute-start | bytes 196616 | tf_op jit(solution)/shard_map/ppermute | solution.py:140
  54.0 0.0 collective-permute-done.4.from_a
  54.0 5.4 %collective-permute-done.5.from_b = bf16[256,128]{1,0:T(8,128)(2,1)S(1)} collective-permute-done((bf16[256,128]{1,0:T(8,128)(2,1)}, bf16[256,128]{1,0:T(8,128)(2,1)S(1)}, u32[]{:S(2)}, u32[]{:S(2)}) %collective-permute-start.5) | collective-permute-done | bytes 65568 | tf_op jit(solution)/shard_map/ppermute | solution.py:140
  59.3 0.6 copy-done.6
  59.9 2.9 %shard_map.40 = (bf16[1024,128]{1,0:T(8,128)(2,1)}, bf16[256,128]{1,0:T(8,128)(2,1)}, bf16[256,128]{1,0:T(8,128)(2,1)}, bf16[4,1024,128]{2,1,0:T(8,128)(2,1)}) custom-call(s32[1]{0:T(128)} %bitcast.core, bf16[8,8,16,512]{3,2,1,0:T(8,128)(2,1)} %copy-done, bf16[1024,128]{1,0:T(8,128)(2,1)} %get-tuple-element.18.vec, bf16[256,128]{1,0:T(8,128)(2,1)} %copy-done.4, ...), custom_call_target="tpu_custom_call" | custom-call | tf_op jit(solution)/shard_map/pallas_call | solution.py:29
  62.9 3.7 %all-to-all-start.1 = ((bf16[4,1024,128]{2,1,0:T(8,128)(2,1)}), bf16[4,1024,128]{2,1,0:T(8,128)(2,1)S(1)}, u32[]{:S(2)}, u32[]{:S(2)}) async-start(bf16[4,1024,128]{2,1,0:T(8,128)(2,1)} %get-tuple-element.21), calls=%async_computation.1 | async-start | bytes 2097152 | tf_op jit(solution)/shard_map/all_to_all | solution.py:132
  66.5 0.0 copy-done.13
  66.6 4.0 %collective-permute-start.6 = (bf16[256,128]{1,0:T(8,128)(2,1)S(1)}, bf16[256,128]{1,0:T(8,128)(2,1)S(1)}, u32[]{:S(2)}, u32[]{:S(2)}) collective-permute-start(bf16[256,128]{1,0:T(8,128)(2,1)S(1)} %copy-done.13), channel_id=1, source_target_pairs={{0,8},{8,0},{1,9},{9,1},{2,10},{10,2},{3,11},{11,3},{4,12},{12,4},... | collective-permute-start | bytes 196616 | tf_op jit(solution)/shard_map/ppermute | solution.py:139
  70.6 1.9 %collective-permute-start.7 = (bf16[256,128]{1,0:T(8,128)(2,1)S(1)}, bf16[256,128]{1,0:T(8,128)(2,1)S(1)}, u32[]{:S(2)}, u32[]{:S(2)}) collective-permute-start(bf16[256,128]{1,0:T(8,128)(2,1)S(1)} %copy-done.12), channel_id=1, source_target_pairs={{0,504},{8,16},{16,8},{24,32},{32,24},{40,48},{48,40},{56,64},{64,... | collective-permute-start | bytes 196616 | tf_op jit(solution)/shard_map/ppermute | solution.py:140
  72.5 0.0 collective-permute-done.6.from_a
  72.6 5.1 %collective-permute-done.7.from_b = bf16[256,128]{1,0:T(8,128)(2,1)S(1)} collective-permute-done((bf16[256,128]{1,0:T(8,128)(2,1)S(1)}, bf16[256,128]{1,0:T(8,128)(2,1)S(1)}, u32[]{:S(2)}, u32[]{:S(2)}) %collective-permute-start.7) | collective-permute-done | bytes 65568 | tf_op jit(solution)/shard_map/ppermute | solution.py:140
  77.7 0.6 copy-done.9
  78.3 2.5 %shard_map.41.own.applied = bf16[1024,128]{1,0:T(8,128)(2,1)} custom-call(s32[1]{0:T(128)} %bitcast.core, bf16[8,8,16,512]{3,2,1,0:T(8,128)(2,1)} %copy-done, bf16[1024,128]{1,0:T(8,128)(2,1)} %get-tuple-element.22.vec, bf16[256,128]{1,0:T(8,128)(2,1)} %copy-done.7, bf16[256,128]{1,0:T(8,128)(2,1)} %copy-done.9), custom_call_target="tpu_custom_call" | custom-call | tf_op jit(solution)/shard_map/pallas_call | solution.py:29
  80.8 1.9 %collective-permute-start.8 = (bf16[1024,128]{1,0:T(8,128)(2,1)}, bf16[1024,128]{1,0:T(8,128)(2,1)S(1)}, u32[]{:S(2)}, u32[]{:S(2)}) collective-permute-start(bf16[1024,128]{1,0:T(8,128)(2,1)} %shard_map.41.own.applied), channel_id=1, source_target_pairs={{0,1},{1,0},{2,3},{3,2},{4,5},{5,4},{6,7},{7,6},{8,9},{9,8},{10,11... | collective-permute-start | bytes 786440 | tf_op jit(solution)/shard_map/ppermute | solution.py:179
  82.7 5.9 %collective-permute-done.8.other = bf16[1024,128]{1,0:T(8,128)(2,1)S(1)} collective-permute-done((bf16[1024,128]{1,0:T(8,128)(2,1)}, bf16[1024,128]{1,0:T(8,128)(2,1)S(1)}, u32[]{:S(2)}, u32[]{:S(2)}) %collective-permute-start.8) | collective-permute-done | bytes 262176 | tf_op jit(solution)/shard_map/ppermute | solution.py:179
  88.6 0.0 all-to-all-done.1.third
  88.6 0.7 copy-done.3
  89.3 1.0 copy-done.1
  90.3 2.5 %shard_map.42 = bf16[16,32,256]{2,1,0:T(8,128)(2,1)} custom-call(bf16[4,1024,128]{2,1,0:T(8,128)(2,1)} %copy-done.1, bf16[1024,128]{1,0:T(8,128)(2,1)} %shard_map.41.own.applied, bf16[1024,128]{1,0:T(8,128)(2,1)} %copy-done.3), custom_call_target="tpu_custom_call" | custom-call | tf_op jit(solution)/shard_map/pallas_call | solution.py:29
  92.9 18.1 %all_to_all.30.parts = bf16[16,32,256]{2,1,0:T(8,128)(2,1)} all-to-all(bf16[16,32,256]{2,1,0:T(8,128)(2,1)} %shard_map.42), channel_id=1, replica_groups=mesh['z2'=4,'z1'=4,'xh'=2,'core'=2,'y'=4,'xl'=2] {'z1','xh','core'}, dimensions={0} | all-to-all | bytes 524288 | tf_op jit(solution)/shard_map/all_to_all | solution.py:132
  110.9 1.6 shard_map.43
  112.6 22.0 %all_to_all.31.parts = bf16[4,32,256]{2,1,0:T(8,128)(2,1)} all-to-all(bf16[4,32,256]{2,1,0:T(8,128)(2,1)} %shard_map.43), channel_id=1, replica_groups=mesh['z2'=4,'z1'=4,'xh'=2,'core'=2,'y'=4,'xl'=2] {'z2'}, dimensions={0} | all-to-all | bytes 131072 | tf_op jit(solution)/shard_map/all_to_all | solution.py:132
  134.5 1.6 shard_map.44
  136.1 17.3 %all_to_all.32.gram = bf16[16,32,256]{2,1,0:T(8,128)(2,1)} all-to-all(bf16[16,32,256]{2,1,0:T(8,128)(2,1)} %shard_map.44), channel_id=1, replica_groups=mesh['z2'=4,'z1'=4,'xh'=2,'core'=2,'y'=4,'xl'=2] {'z1','xh','core'}, dimensions={0} | all-to-all | bytes 524288 | tf_op jit(solution)/shard_map/all_to_all | solution.py:132
  153.3 2.6 %shard_map.45 = bf16[8,128,256]{2,1,0:T(8,128)(2,1)} custom-call(bf16[4,1024,128]{2,1,0:T(8,128)(2,1)} %copy-done.1, bf16[16,32,256]{2,1,0:T(8,128)(2,1)} %all_to_all.32.gram, bf16[1024,128]{1,0:T(8,128)(2,1)} %shard_map.41.own.applied), custom_call_target="tpu_custom_call" | custom-call | tf_op jit(solution)/shard_map/pallas_call | solution.py:29
  156.0 13.5 %all_to_all.33.parts = bf16[8,128,256]{2,1,0:T(8,128)(2,1)} all-to-all(bf16[8,128,256]{2,1,0:T(8,128)(2,1)} %shard_map.45), channel_id=1, replica_groups=mesh['z2'=4,'z1'=4,'xh'=2,'core'=2,'y'=4,'xl'=2] {'y','xl'}, dimensions={0} | all-to-all | bytes 1048576 | tf_op jit(solution)/shard_map/all_to_all | solution.py:132
  169.5 1.8 %shard_map.46 = bf16[128,1024]{1,0:T(8,128)(2,1)} custom-call(bf16[8,128,256]{2,1,0:T(8,128)(2,1)} %all_to_all.33.parts), custom_call_target="tpu_custom_call" | custom-call | tf_op jit(solution)/shard_map/pallas_call | solution.py:29
  (17 shorter events, 0.0 us)
Async XLA Ops:
  2.2 6.1 %copy-start.2 = (bf16[1024,128]{1,0:T(8,128)(2,1)S(1)}, bf16[1024,128]{1,0:T(8,128)(2,1)}, u32[]{:S(2)}) copy-start(bf16[1024,128]{1,0:T(8,128)(2,1)} %rest_0_.1) | copy-start | bytes 786436
  2.2 21.7 %all-to-all-start = ((bf16[8,8,16,512]{3,2,1,0:T(8,128)(2,1)}), bf16[8,8,16,512]{3,2,1,0:T(8,128)(2,1)S(1)}, u32[]{:S(2)}, u32[]{:S(2)}) async-start(bf16[8,8,16,512]{3,2,1,0:T(8,128)(2,1)} %shard_map.37), calls=%async_computation | async-start | bytes 2097152 | tf_op jit(solution)/shard_map/all_to_all | solution.py:132
  8.3 8.3 %collective-permute-start = (bf16[256,128]{1,0:T(8,128)(2,1)S(1)}, bf16[256,128]{1,0:T(8,128)(2,1)S(1)}, u32[]{:S(2)}, u32[]{:S(2)}) collective-permute-start(bf16[256,128]{1,0:T(8,128)(2,1)S(1)} %get-tuple-element.26), channel_id=1, source_target_pairs={{0,8},{8,0},{1,9},{9,1},{2,10},{10,2},{3,11},{11,3},{4,12},{12,4},... | collective-permute-start | bytes 196616 | tf_op jit(solution)/shard_map/ppermute | solution.py:139
  14.7 9.2 %collective-permute-start.1 = (bf16[256,128]{1,0:T(8,128)(2,1)S(1)}, bf16[256,128]{1,0:T(8,128)(2,1)S(1)}, u32[]{:S(2)}, u32[]{:S(2)}) collective-permute-start(bf16[256,128]{1,0:T(8,128)(2,1)S(1)} %get-tuple-element.25), channel_id=1, source_target_pairs={{0,504},{8,16},{16,8},{24,32},{32,24},{40,48},{48,40},{56,64},{64,... | collective-permute-start | bytes 196616 | tf_op jit(solution)/shard_map/ppermute | solution.py:140
  16.6 7.2 %copy-start.10 = (bf16[256,128]{1,0:T(8,128)(2,1)}, bf16[256,128]{1,0:T(8,128)(2,1)S(1)}, u32[]{:S(2)}) copy-start(bf16[256,128]{1,0:T(8,128)(2,1)S(1)} %collective-permute-done.from_a) | copy-start | bytes 196612
  23.9 0.6 copy-start.11
  23.9 1.0 copy-start
  27.4 7.2 %collective-permute-start.2 = (bf16[256,128]{1,0:T(8,128)(2,1)}, bf16[256,128]{1,0:T(8,128)(2,1)S(1)}, u32[]{:S(2)}, u32[]{:S(2)}) collective-permute-start(bf16[256,128]{1,0:T(8,128)(2,1)} %get-tuple-element.16), channel_id=1, source_target_pairs={{0,8},{8,0},{1,9},{9,1},{2,10},{10,2},{3,11},{11,3},{4,12},{12,4},... | collective-permute-start | bytes 196616 | tf_op jit(solution)/shard_map/ppermute | solution.py:139
  32.2 7.3 %collective-permute-start.3 = (bf16[256,128]{1,0:T(8,128)(2,1)}, bf16[256,128]{1,0:T(8,128)(2,1)S(1)}, u32[]{:S(2)}, u32[]{:S(2)}) collective-permute-start(bf16[256,128]{1,0:T(8,128)(2,1)} %get-tuple-element.17), channel_id=1, source_target_pairs={{0,504},{8,16},{16,8},{24,32},{32,24},{40,48},{48,40},{56,64},{64,... | collective-permute-start | bytes 196616 | tf_op jit(solution)/shard_map/ppermute | solution.py:140
  34.6 4.9 %copy-start.5 = (bf16[256,128]{1,0:T(8,128)(2,1)}, bf16[256,128]{1,0:T(8,128)(2,1)S(1)}, u32[]{:S(2)}) copy-start(bf16[256,128]{1,0:T(8,128)(2,1)S(1)} %collective-permute-done.2.from_a) | copy-start | bytes 196612
  39.5 0.6 copy-start.8
  42.7 11.2 %collective-permute-start.4 = (bf16[256,128]{1,0:T(8,128)(2,1)}, bf16[256,128]{1,0:T(8,128)(2,1)S(1)}, u32[]{:S(2)}, u32[]{:S(2)}) collective-permute-start(bf16[256,128]{1,0:T(8,128)(2,1)} %get-tuple-element.19), channel_id=1, source_target_pairs={{0,8},{8,0},{1,9},{9,1},{2,10},{10,2},{3,11},{11,3},{4,12},{12,4},... | collective-permute-start | bytes 196616 | tf_op jit(solution)/shard_map/ppermute | solution.py:139
  52.0 7.3 %collective-permute-start.5 = (bf16[256,128]{1,0:T(8,128)(2,1)}, bf16[256,128]{1,0:T(8,128)(2,1)S(1)}, u32[]{:S(2)}, u32[]{:S(2)}) collective-permute-start(bf16[256,128]{1,0:T(8,128)(2,1)} %get-tuple-element.20), channel_id=1, source_target_pairs={{0,504},{8,16},{16,8},{24,32},{32,24},{40,48},{48,40},{56,64},{64,... | collective-permute-start | bytes 196616 | tf_op jit(solution)/shard_map/ppermute | solution.py:140
  54.0 5.4 %copy-start.4 = (bf16[256,128]{1,0:T(8,128)(2,1)}, bf16[256,128]{1,0:T(8,128)(2,1)S(1)}, u32[]{:S(2)}) copy-start(bf16[256,128]{1,0:T(8,128)(2,1)S(1)} %collective-permute-done.4.from_a) | copy-start | bytes 196612
  59.3 0.6 copy-start.6
  62.9 3.7 %copy-start.13 = (bf16[256,128]{1,0:T(8,128)(2,1)S(1)}, bf16[256,128]{1,0:T(8,128)(2,1)}, u32[]{:S(2)}) copy-start(bf16[256,128]{1,0:T(8,128)(2,1)} %get-tuple-element.23) | copy-start | bytes 196612
  62.9 7.7 %copy-start.12 = (bf16[256,128]{1,0:T(8,128)(2,1)S(1)}, bf16[256,128]{1,0:T(8,128)(2,1)}, u32[]{:S(2)}) copy-start(bf16[256,128]{1,0:T(8,128)(2,1)} %get-tuple-element.24) | copy-start | bytes 196612
  62.9 25.8 %all-to-all-start.1 = ((bf16[4,1024,128]{2,1,0:T(8,128)(2,1)}), bf16[4,1024,128]{2,1,0:T(8,128)(2,1)S(1)}, u32[]{:S(2)}, u32[]{:S(2)}) async-start(bf16[4,1024,128]{2,1,0:T(8,128)(2,1)} %get-tuple-element.21), calls=%async_computation.1 | async-start | bytes 2097152 | tf_op jit(solution)/shard_map/all_to_all | solution.py:132
  66.6 6.0 %collective-permute-start.6 = (bf16[256,128]{1,0:T(8,128)(2,1)S(1)}, bf16[256,128]{1,0:T(8,128)(2,1)S(1)}, u32[]{:S(2)}, u32[]{:S(2)}) collective-permute-start(bf16[256,128]{1,0:T(8,128)(2,1)S(1)} %copy-done.13), channel_id=1, source_target_pairs={{0,8},{8,0},{1,9},{9,1},{2,10},{10,2},{3,11},{11,3},{4,12},{12,4},... | collective-permute-start | bytes 196616 | tf_op jit(solution)/shard_map/ppermute | solution.py:139
  70.6 7.1 %collective-permute-start.7 = (bf16[256,128]{1,0:T(8,128)(2,1)S(1)}, bf16[256,128]{1,0:T(8,128)(2,1)S(1)}, u32[]{:S(2)}, u32[]{:S(2)}) collective-permute-start(bf16[256,128]{1,0:T(8,128)(2,1)S(1)} %copy-done.12), channel_id=1, source_target_pairs={{0,504},{8,16},{16,8},{24,32},{32,24},{40,48},{48,40},{56,64},{64,... | collective-permute-start | bytes 196616 | tf_op jit(solution)/shard_map/ppermute | solution.py:140
  72.5 5.2 %copy-start.7 = (bf16[256,128]{1,0:T(8,128)(2,1)}, bf16[256,128]{1,0:T(8,128)(2,1)S(1)}, u32[]{:S(2)}) copy-start(bf16[256,128]{1,0:T(8,128)(2,1)S(1)} %collective-permute-done.6.from_a) | copy-start | bytes 196612
  77.7 0.6 copy-start.9
  80.8 7.8 %collective-permute-start.8 = (bf16[1024,128]{1,0:T(8,128)(2,1)}, bf16[1024,128]{1,0:T(8,128)(2,1)S(1)}, u32[]{:S(2)}, u32[]{:S(2)}) collective-permute-start(bf16[1024,128]{1,0:T(8,128)(2,1)} %shard_map.41.own.applied), channel_id=1, source_target_pairs={{0,1},{1,0},{2,3},{3,2},{4,5},{5,4},{6,7},{7,6},{8,9},{9,8},{10,11... | collective-permute-start | bytes 786440 | tf_op jit(solution)/shard_map/ppermute | solution.py:179
  88.6 0.7 copy-start.3
  89.3 1.0 copy-start.1

commit v2 on v1

--- a/solution.py
+++ b/solution.py
@@ -25,10 +25,15 @@
     return lax.dot_general(a, b, (dims, ((), ())), preferred_element_type=F32)
 
 
-def call(kernel, outs, args, scratch=(), smem=0):
+def call(kernel, outs, args, scratch=(), smem=0, far=(), last=False):
+    args = [
+        x if i < smem or i in far else pltpu.with_memory_space_constraint(x, pltpu.VMEM)
+        for i, x in enumerate(args)
+    ]
+    make = jax.ShapeDtypeStruct if last else pltpu.VMEM
     return pl.pallas_call(
         kernel,
-        out_shape=[jax.ShapeDtypeStruct(shape, BF16) for shape in outs],
+        out_shape=[make(shape, BF16) for shape in outs],
         in_specs=[SMEM] * smem + [VMEM] * (len(args) - smem),
         out_specs=[VMEM] * len(outs),
         scratch_shapes=list(scratch),
@@ -50,17 +55,17 @@
                 out[copy, r, :, k * width : (k + 1) * width] = total
 
 
-def apply_kernel(prior, copies, core, ham, vec, from_a, from_b, *rest):
+def apply_kernel(prior, copies, core, ham, vec, from_far, from_near, *rest):
     before = rest[0] if prior else None
     rest = rest[1:] if prior else rest
     ext = rest[-1]
-    edge = from_a.shape[0]
+    edge = from_far.shape[0]
     rows = vec.shape[0]
     tile = edge // FACE
     c = core[0]
     ext[edge : edge + rows] = vec[...]
-    ext[pl.ds(pl.multiple_of((1 - c) * (edge + rows), edge), edge)] = from_a[...]
-    ext[pl.ds(pl.multiple_of(c * (edge + rows), edge), edge)] = from_b[...]
+    ext[pl.ds(pl.multiple_of((1 - c) * (edge + rows), edge), edge)] = from_near[...]
+    ext[pl.ds(pl.multiple_of(c * (edge + rows), edge), edge)] = from_far[...]
     out = rest[0]
     for r in range(rows // tile):
         layer = FACE + r // FACE * FACE
@@ -83,8 +88,8 @@
             for copy in range(copies):
                 rest[3][copy, here] = value
     if len(rest) > 2:
-        rest[1][...] = out[pl.ds(pl.multiple_of((1 - c) * (rows - edge), edge), edge)]
-        rest[2][...] = out[pl.ds(pl.multiple_of(c * (rows - edge), edge), edge)]
+        rest[1][...] = out[pl.ds(pl.multiple_of(c * (rows - edge), edge), edge)]
+        rest[2][...] = out[pl.ds(pl.multiple_of((1 - c) * (rows - edge), edge), edge)]
 
 
 def gram_kernel(third, own, other, out):
@@ -132,13 +137,11 @@
     return lax.all_to_all(copies, axes, 0, 0, tiled=True)
 
 
-def swap(near, far):
+def swap(far, near):
     count = lax.axis_size(SLAB)
     pairs = [(s, (s + 1) % count if s % 2 else (s - 1) % count) for s in range(count)]
-    return (
-        lax.ppermute(near, "core", [(0, 1), (1, 0)]),
-        lax.ppermute(far, SLAB, pairs),
-    )
+    from_far = lax.ppermute(far, SLAB, pairs)
+    return from_far, lax.ppermute(near, "core", [(0, 1), (1, 0)])
 
 
 def body(hamiltonian, neighbors, orbitals):
@@ -150,12 +153,12 @@
     scalar = core.astype(jnp.int32).reshape(1)
 
     (shares,) = call(
-        combine_kernel, [(nband, blocks, strip, 4 * tile)], (neighbors, hamiltonian), smem=1
+        combine_kernel, [(nband, blocks, strip, 4 * tile)], (neighbors, hamiltonian), smem=1, far=(1,)
     )
     tiles = gather(shares, BAND)
     received = swap(
+        lax.dynamic_slice_in_dim(orbitals, core * (rows - edge), edge, 0),
         lax.dynamic_slice_in_dim(orbitals, (1 - core) * (rows - edge), edge, 0),
-        lax.dynamic_slice_in_dim(orbitals, core * (rows - edge), edge, 0),
     )
 
     def apply(vec, received, before=None, copies=0, edges=True):
@@ -196,7 +199,9 @@
     (partial_out,) = call(
         mixed_kernel, [(nband, rows // nband, 2 * width)], (third_all, gram, applied)
     )
-    (out,) = call(final_kernel, [(rows // nband, nband * width)], (gather(partial_out, BAND),))
+    (out,) = call(
+        final_kernel, [(rows // nband, nband * width)], (gather(partial_out, BAND),), last=True
+    )
     return out
 
 

time: 172 us -> 144 us (0.84)
  waiting for transfers between devices: 28.5 us -> 11 us
  Pallas kernels: 22.9 us -> 5.81 us
  starting transfers between devices: 44.3 us -> 58 us
  blocking collectives: 70.8 us -> 65.7 us
  local copies, waits for them, and re-layouts: 4.59 us -> 2.23 us
    ppermute x8, waiting for transfers between devices: 22.6 us -> 3.56 us  [the longest x4 2.61 us: swap(): return (from_far, lax.ppermute(near, 'core', [(0, 1), (1, 0)]))]
    pallas_call x10, Pallas kernels: 22.9 us -> 5.81 us  [call(): pl.pallas_call(kernel, out_shape=[make(shape, BF16) for shape in outs], i...]
    ppermute x8, starting transfers between devices: 32.7 us -> 46.5 us  [the longest x4 32.5 us: swap(): return (from_far, lax.ppermute(near, 'core', [(0, 1), (1, 0)]))]
    all_to_all x4, blocking collectives: 70.8 us -> 65.7 us  [gather(): return lax.all_to_all(copies, axes, 0, 0, tiled=True)]
    unnamed x28 -> x8, local copies, waits for them, and re-layouts: 4.58 us -> 2.22 us
  transfers between devices with their start and end apart: 11 -> 11, of which waited for: 5 -> 5; matrix products, arithmetic and copies ran while one was open for 0% -> 0% of each run, Pallas kernels for 1% -> 0%
where the time goes in v2:
time: 144 us; the launch traced here: 143 us
  blocking collectives  65.7 us (46%)
  starting transfers between devices  58 us (40%)
  waiting for transfers between devices  11 us (8%)
  Pallas kernels  5.81 us (4%)
  local copies, waits for them, and re-layouts  2.23 us (2%)
    all_to_all x4, blocking collectives, gather(): return lax.all_to_all(copies, axes, 0, 0, tiled=True)  65.7 us
    ppermute x4, starting transfers between devices, swap(): return (from_far, lax.ppermute(near, 'core', [(0, 1), (1, 0)]))  32.5 us
    ppermute x4, starting transfers between devices, swap(): from_far = lax.ppermute(far, SLAB, pairs)  14 us
    all_to_all x2, starting transfers between devices, gather(): return lax.all_to_all(copies, axes, 0, 0, tiled=True)  9.58 us
    ppermute x1, waiting for transfers between devices, body(): other = lax.ppermute(applied, 'xl', [(0, 1), (1, 0)])  7.47 us
    pallas_call x10, Pallas kernels, call(): pl.pallas_call(kernel, out_shape=[make(shape, BF16) for shape in outs], i...  5.81 us
  transfers between devices with their start and end apart: 11, of which 5 were waited for; matrix products, arithmetic and copies ran while one was open for 0% of the time, Pallas kernels for 0%

profile of v2, /device:TPU:1, one launch (start us, length us, event | category | flops | bytes accessed | tf_op | source)
XLA Modules:
  0.0 143.0 jit_solution(2809486087511661102)
XLA Ops:
  0.0 2.2 %shard_map.37 = bf16[8,8,16,512]{3,2,1,0:T(8,128)(2,1)} custom-call(s32[8,7]{1,0:T(8,128)} %nbr.1, bf16[8,7,16,128]{3,2,1,0:T(8,128)(2,1)} %ham.1), custom_call_target="tpu_custom_call" | custom-call | tf_op jit(solution)/shard_map/pallas_call | solution.py:34
  2.2 0.0 copy-start.2
  2.2 6.1 %all-to-all-start = ((bf16[8,8,16,512]{3,2,1,0:T(8,128)(2,1)}), bf16[8,8,16,512]{3,2,1,0:T(8,128)(2,1)S(1)}, u32[]{:S(2)}, u32[]{:S(2)}) async-start(bf16[8,8,16,512]{3,2,1,0:T(8,128)(2,1)} %shard_map.37), calls=%async_computation | async-start | bytes 2097152 | tf_op jit(solution)/shard_map/all_to_all | solution.py:137
  8.3 0.0 copy-done.2
  8.3 5.2 %collective-permute-start = (bf16[256,128]{1,0:T(8,128)(2,1)S(1)}, bf16[256,128]{1,0:T(8,128)(2,1)S(1)}, u32[]{:S(2)}, u32[]{:S(2)}) collective-permute-start(bf16[256,128]{1,0:T(8,128)(2,1)S(1)} %get-tuple-element.26), channel_id=1, source_target_pairs={{0,504},{8,16},{16,8},{24,32},{32,24},{40,48},{48,40},{56,64},{64,... | collective-permute-start | bytes 196616 | tf_op jit(solution)/shard_map/ppermute | solution.py:143
  13.5 10.4 %collective-permute-start.1 = (bf16[256,128]{1,0:T(8,128)(2,1)S(1)}, bf16[256,128]{1,0:T(8,128)(2,1)S(1)}, u32[]{:S(2)}, u32[]{:S(2)}) collective-permute-start(bf16[256,128]{1,0:T(8,128)(2,1)S(1)} %get-tuple-element.25), channel_id=1, source_target_pairs={{0,8},{8,0},{1,9},{9,1},{2,10},{10,2},{3,11},{11,3},{4,12},{12,4},... | collective-permute-start | bytes 196616 | tf_op jit(solution)/shard_map/ppermute | solution.py:144
  23.9 0.9 collective-permute-done.from_far
  24.9 0.0 collective-permute-done.1.from_near
  24.9 0.0 all-to-all-done.ham
  24.9 0.0 copy-start
  24.9 0.5 shard_map.38
  25.3 5.0 %collective-permute-start.2 = (bf16[256,128]{1,0:T(8,128)(2,1)S(1)}, bf16[256,128]{1,0:T(8,128)(2,1)S(1)}, u32[]{:S(2)}, u32[]{:S(2)}) collective-permute-start(bf16[256,128]{1,0:T(8,128)(2,1)S(1)} %get-tuple-element.16), channel_id=1, source_target_pairs={{0,504},{8,16},{16,8},{24,32},{32,24},{40,48},{48,40},{56,64},{64,... | collective-permute-start | bytes 196616 | tf_op jit(solution)/shard_map/ppermute | solution.py:143
  30.3 9.3 %collective-permute-start.3 = (bf16[256,128]{1,0:T(8,128)(2,1)S(1)}, bf16[256,128]{1,0:T(8,128)(2,1)S(1)}, u32[]{:S(2)}, u32[]{:S(2)}) collective-permute-start(bf16[256,128]{1,0:T(8,128)(2,1)S(1)} %get-tuple-element.17), channel_id=1, source_target_pairs={{0,8},{8,0},{1,9},{9,1},{2,10},{10,2},{3,11},{11,3},{4,12},{12,4},... | collective-permute-start | bytes 196616 | tf_op jit(solution)/shard_map/ppermute | solution.py:144
  39.6 0.0 collective-permute-done.2.from_far
  39.7 0.9 collective-permute-done.3.from_near
  40.5 0.5 shard_map.39
  41.0 0.0 copy-done
  41.0 1.9 %collective-permute-start.4 = (bf16[256,128]{1,0:T(8,128)(2,1)S(1)}, bf16[256,128]{1,0:T(8,128)(2,1)S(1)}, u32[]{:S(2)}, u32[]{:S(2)}) collective-permute-start(bf16[256,128]{1,0:T(8,128)(2,1)S(1)} %get-tuple-element.19), channel_id=1, source_target_pairs={{0,504},{8,16},{16,8},{24,32},{32,24},{40,48},{48,40},{56,64},{64,... | collective-permute-start | bytes 196616 | tf_op jit(solution)/shard_map/ppermute | solution.py:143
  42.9 6.4 %collective-permute-start.5 = (bf16[256,128]{1,0:T(8,128)(2,1)S(1)}, bf16[256,128]{1,0:T(8,128)(2,1)S(1)}, u32[]{:S(2)}, u32[]{:S(2)}) collective-permute-start(bf16[256,128]{1,0:T(8,128)(2,1)S(1)} %get-tuple-element.20), channel_id=1, source_target_pairs={{0,8},{8,0},{1,9},{9,1},{2,10},{10,2},{3,11},{11,3},{4,12},{12,4},... | collective-permute-start | bytes 196616 | tf_op jit(solution)/shard_map/ppermute | solution.py:144
  49.3 0.0 collective-permute-done.4.from_far
  49.3 0.9 collective-permute-done.5.from_near
  50.2 0.0 copy-start.1
  50.2 1.2 copy-done.1
  51.4 0.5 shard_map.40
  51.9 0.0 copy-start.3
  51.9 1.0 copy-done.3
  52.9 3.5 %all-to-all-start.1 = ((bf16[4,1024,128]{2,1,0:T(8,128)(2,1)}), bf16[4,1024,128]{2,1,0:T(8,128)(2,1)S(1)}, u32[]{:S(2)}, u32[]{:S(2)}) async-start(bf16[4,1024,128]{2,1,0:T(8,128)(2,1)} %copy-done.3), calls=%async_computation.1 | async-start | bytes 2097152 | tf_op jit(solution)/shard_map/all_to_all | solution.py:137
  56.4 1.9 %collective-permute-start.6 = (bf16[256,128]{1,0:T(8,128)(2,1)S(1)}, bf16[256,128]{1,0:T(8,128)(2,1)S(1)}, u32[]{:S(2)}, u32[]{:S(2)}) collective-permute-start(bf16[256,128]{1,0:T(8,128)(2,1)S(1)} %get-tuple-element.23), channel_id=1, source_target_pairs={{0,504},{8,16},{16,8},{24,32},{32,24},{40,48},{48,40},{56,64},{64,... | collective-permute-start | bytes 196616 | tf_op jit(solution)/shard_map/ppermute | solution.py:143
  58.4 6.4 %collective-permute-start.7 = (bf16[256,128]{1,0:T(8,128)(2,1)S(1)}, bf16[256,128]{1,0:T(8,128)(2,1)S(1)}, u32[]{:S(2)}, u32[]{:S(2)}) collective-permute-start(bf16[256,128]{1,0:T(8,128)(2,1)S(1)} %get-tuple-element.24), channel_id=1, source_target_pairs={{0,8},{8,0},{1,9},{9,1},{2,10},{10,2},{3,11},{11,3},{4,12},{12,4},... | collective-permute-start | bytes 196616 | tf_op jit(solution)/shard_map/ppermute | solution.py:144
  64.7 0.0 collective-permute-done.6.from_far
  64.8 0.9 collective-permute-done.7.from_near
  65.6 0.4 shard_map.41.own.applied
  66.1 1.9 %collective-permute-start.8 = (bf16[1024,128]{1,0:T(8,128)(2,1)S(1)}, bf16[1024,128]{1,0:T(8,128)(2,1)S(1)}, u32[]{:S(2)}, u32[]{:S(2)}) collective-permute-start(bf16[1024,128]{1,0:T(8,128)(2,1)S(1)} %shard_map.41.own.applied), channel_id=1, source_target_pairs={{0,1},{1,0},{2,3},{3,2},{4,5},{5,4},{6,7},{7,6},{8,9},{9,8},{10,11... | collective-permute-start | bytes 786440 | tf_op jit(solution)/shard_map/ppermute | solution.py:182
  68.0 7.5 %collective-permute-done.8.other = bf16[1024,128]{1,0:T(8,128)(2,1)S(1)} collective-permute-done((bf16[1024,128]{1,0:T(8,128)(2,1)S(1)}, bf16[1024,128]{1,0:T(8,128)(2,1)S(1)}, u32[]{:S(2)}, u32[]{:S(2)}) %collective-permute-start.8) | collective-permute-done | bytes 262176 | tf_op jit(solution)/shard_map/ppermute | solution.py:182
  75.5 0.0 all-to-all-done.1.third
  75.5 0.5 shard_map.42
  76.0 14.7 %all_to_all.30.parts = bf16[16,32,256]{2,1,0:T(8,128)(2,1)S(1)} all-to-all(bf16[16,32,256]{2,1,0:T(8,128)(2,1)S(1)} %shard_map.42), channel_id=1, replica_groups=mesh['z2'=4,'z1'=4,'xh'=2,'core'=2,'y'=4,'xl'=2] {'z1','xh','core'}, dimensions={0} | all-to-all | bytes 524288 | tf_op jit(solution)/shard_map/all_to_all | solution.py:137
  90.7 21.7 %all_to_all.31.parts = bf16[4,32,256]{2,1,0:T(8,128)(2,1)S(1)} all-to-all(bf16[4,32,256]{2,1,0:T(8,128)(2,1)S(1)} %shard_map.43), channel_id=1, replica_groups=mesh['z2'=4,'z1'=4,'xh'=2,'core'=2,'y'=4,'xl'=2] {'z2'}, dimensions={0} | all-to-all | bytes 131072 | tf_op jit(solution)/shard_map/all_to_all | solution.py:137
  112.5 16.1 %all_to_all.32.gram = bf16[16,32,256]{2,1,0:T(8,128)(2,1)S(1)} all-to-all(bf16[16,32,256]{2,1,0:T(8,128)(2,1)S(1)} %shard_map.44), channel_id=1, replica_groups=mesh['z2'=4,'z1'=4,'xh'=2,'core'=2,'y'=4,'xl'=2] {'z1','xh','core'}, dimensions={0} | all-to-all | bytes 524288 | tf_op jit(solution)/shard_map/all_to_all | solution.py:137
  128.6 0.4 shard_map.45
  129.0 13.2 %all_to_all.33.parts = bf16[8,128,256]{2,1,0:T(8,128)(2,1)S(1)} all-to-all(bf16[8,128,256]{2,1,0:T(8,128)(2,1)S(1)} %shard_map.45), channel_id=1, replica_groups=mesh['z2'=4,'z1'=4,'xh'=2,'core'=2,'y'=4,'xl'=2] {'y','xl'}, dimensions={0} | all-to-all | bytes 1048576 | tf_op jit(solution)/shard_map/all_to_all | solution.py:137
  142.2 0.8 shard_map.46
  (3 shorter events, 0.1 us)
Async XLA Ops:
  2.2 6.1 %copy-start.2 = (bf16[1024,128]{1,0:T(8,128)(2,1)S(1)}, bf16[1024,128]{1,0:T(8,128)(2,1)}, u32[]{:S(2)}) copy-start(bf16[1024,128]{1,0:T(8,128)(2,1)} %rest_0_.1) | copy-start | bytes 786436
  2.2 22.7 %all-to-all-start = ((bf16[8,8,16,512]{3,2,1,0:T(8,128)(2,1)}), bf16[8,8,16,512]{3,2,1,0:T(8,128)(2,1)S(1)}, u32[]{:S(2)}, u32[]{:S(2)}) async-start(bf16[8,8,16,512]{3,2,1,0:T(8,128)(2,1)} %shard_map.37), calls=%async_computation | async-start | bytes 2097152 | tf_op jit(solution)/shard_map/all_to_all | solution.py:137
  8.3 16.6 %collective-permute-start = (bf16[256,128]{1,0:T(8,128)(2,1)S(1)}, bf16[256,128]{1,0:T(8,128)(2,1)S(1)}, u32[]{:S(2)}, u32[]{:S(2)}) collective-permute-start(bf16[256,128]{1,0:T(8,128)(2,1)S(1)} %get-tuple-element.26), channel_id=1, source_target_pairs={{0,504},{8,16},{16,8},{24,32},{32,24},{40,48},{48,40},{56,64},{64,... | collective-permute-start | bytes 196616 | tf_op jit(solution)/shard_map/ppermute | solution.py:143
  13.5 11.3 %collective-permute-start.1 = (bf16[256,128]{1,0:T(8,128)(2,1)S(1)}, bf16[256,128]{1,0:T(8,128)(2,1)S(1)}, u32[]{:S(2)}, u32[]{:S(2)}) collective-permute-start(bf16[256,128]{1,0:T(8,128)(2,1)S(1)} %get-tuple-element.25), channel_id=1, source_target_pairs={{0,8},{8,0},{1,9},{9,1},{2,10},{10,2},{3,11},{11,3},{4,12},{12,4},... | collective-permute-start | bytes 196616 | tf_op jit(solution)/shard_map/ppermute | solution.py:144
  24.9 16.1 %copy-start = (bf16[8,8,16,512]{3,2,1,0:T(8,128)(2,1)}, bf16[8,8,16,512]{3,2,1,0:T(8,128)(2,1)S(1)}, u32[]{:S(2)}) copy-start(bf16[8,8,16,512]{3,2,1,0:T(8,128)(2,1)S(1)} %all-to-all-done.ham) | copy-start | bytes 3145732
  25.3 14.3 %collective-permute-start.2 = (bf16[256,128]{1,0:T(8,128)(2,1)S(1)}, bf16[256,128]{1,0:T(8,128)(2,1)S(1)}, u32[]{:S(2)}, u32[]{:S(2)}) collective-permute-start(bf16[256,128]{1,0:T(8,128)(2,1)S(1)} %get-tuple-element.16), channel_id=1, source_target_pairs={{0,504},{8,16},{16,8},{24,32},{32,24},{40,48},{48,40},{56,64},{64,... | collective-permute-start | bytes 196616 | tf_op jit(solution)/shard_map/ppermute | solution.py:143
  30.3 10.2 %collective-permute-start.3 = (bf16[256,128]{1,0:T(8,128)(2,1)S(1)}, bf16[256,128]{1,0:T(8,128)(2,1)S(1)}, u32[]{:S(2)}, u32[]{:S(2)}) collective-permute-start(bf16[256,128]{1,0:T(8,128)(2,1)S(1)} %get-tuple-element.17), channel_id=1, source_target_pairs={{0,8},{8,0},{1,9},{9,1},{2,10},{10,2},{3,11},{11,3},{4,12},{12,4},... | collective-permute-start | bytes 196616 | tf_op jit(solution)/shard_map/ppermute | solution.py:144
  41.0 8.3 %collective-permute-start.4 = (bf16[256,128]{1,0:T(8,128)(2,1)S(1)}, bf16[256,128]{1,0:T(8,128)(2,1)S(1)}, u32[]{:S(2)}, u32[]{:S(2)}) collective-permute-start(bf16[256,128]{1,0:T(8,128)(2,1)S(1)} %get-tuple-element.19), channel_id=1, source_target_pairs={{0,504},{8,16},{16,8},{24,32},{32,24},{40,48},{48,40},{56,64},{64,... | collective-permute-start | bytes 196616 | tf_op jit(solution)/shard_map/ppermute | solution.py:143
  42.9 7.3 %collective-permute-start.5 = (bf16[256,128]{1,0:T(8,128)(2,1)S(1)}, bf16[256,128]{1,0:T(8,128)(2,1)S(1)}, u32[]{:S(2)}, u32[]{:S(2)}) collective-permute-start(bf16[256,128]{1,0:T(8,128)(2,1)S(1)} %get-tuple-element.20), channel_id=1, source_target_pairs={{0,8},{8,0},{1,9},{9,1},{2,10},{10,2},{3,11},{11,3},{4,12},{12,4},... | collective-permute-start | bytes 196616 | tf_op jit(solution)/shard_map/ppermute | solution.py:144
  50.2 1.2 copy-start.1
  51.9 1.0 copy-start.3
  52.9 22.6 %all-to-all-start.1 = ((bf16[4,1024,128]{2,1,0:T(8,128)(2,1)}), bf16[4,1024,128]{2,1,0:T(8,128)(2,1)S(1)}, u32[]{:S(2)}, u32[]{:S(2)}) async-start(bf16[4,1024,128]{2,1,0:T(8,128)(2,1)} %copy-done.3), calls=%async_computation.1 | async-start | bytes 2097152 | tf_op jit(solution)/shard_map/all_to_all | solution.py:137
  56.4 8.3 %collective-permute-start.6 = (bf16[256,128]{1,0:T(8,128)(2,1)S(1)}, bf16[256,128]{1,0:T(8,128)(2,1)S(1)}, u32[]{:S(2)}, u32[]{:S(2)}) collective-permute-start(bf16[256,128]{1,0:T(8,128)(2,1)S(1)} %get-tuple-element.23), channel_id=1, source_target_pairs={{0,504},{8,16},{16,8},{24,32},{32,24},{40,48},{48,40},{56,64},{64,... | collective-permute-start | bytes 196616 | tf_op jit(solution)/shard_map/ppermute | solution.py:143
  58.4 7.3 %collective-permute-start.7 = (bf16[256,128]{1,0:T(8,128)(2,1)S(1)}, bf16[256,128]{1,0:T(8,128)(2,1)S(1)}, u32[]{:S(2)}, u32[]{:S(2)}) collective-permute-start(bf16[256,128]{1,0:T(8,128)(2,1)S(1)} %get-tuple-element.24), channel_id=1, source_target_pairs={{0,8},{8,0},{1,9},{9,1},{2,10},{10,2},{3,11},{11,3},{4,12},{12,4},... | collective-permute-start | bytes 196616 | tf_op jit(solution)/shard_map/ppermute | solution.py:144
  66.1 9.4 %collective-permute-start.8 = (bf16[1024,128]{1,0:T(8,128)(2,1)S(1)}, bf16[1024,128]{1,0:T(8,128)(2,1)S(1)}, u32[]{:S(2)}, u32[]{:S(2)}) collective-permute-start(bf16[1024,128]{1,0:T(8,128)(2,1)S(1)} %shard_map.41.own.applied), channel_id=1, source_target_pairs={{0,1},{1,0},{2,3},{3,2},{4,5},{5,4},{6,7},{7,6},{8,9},{9,8},{10,11... | collective-permute-start | bytes 786440 | tf_op jit(solution)/shard_map/ppermute | solution.py:182

commit v3 on v2

--- a/solution.py
+++ b/solution.py
@@ -19,31 +19,35 @@
 
 VMEM = pl.BlockSpec(memory_space=pltpu.VMEM)
 SMEM = pl.BlockSpec(memory_space=pltpu.SMEM)
+HBM = pl.BlockSpec(memory_space=pltpu.MemorySpace.HBM)
 
 
 def dot(a, b, dims=((1,), (0,))):
     return lax.dot_general(a, b, (dims, ((), ())), preferred_element_type=F32)
 
 
-def call(kernel, outs, args, scratch=(), smem=0, far=(), last=False):
+def call(kernel, outs, args, scratch=(), smem=0, far=(), far_outs=(), last=False):
     args = [
         x if i < smem or i in far else pltpu.with_memory_space_constraint(x, pltpu.VMEM)
         for i, x in enumerate(args)
     ]
-    make = jax.ShapeDtypeStruct if last else pltpu.VMEM
+    spaces = [HBM if i in far_outs else VMEM for i in range(len(outs))]
+    plain = [last or i in far_outs for i in range(len(outs))]
     return pl.pallas_call(
         kernel,
-        out_shape=[make(shape, BF16) for shape in outs],
+        out_shape=[
+            (jax.ShapeDtypeStruct if p else pltpu.VMEM)(shape, BF16) for p, shape in zip(plain, outs)
+        ],
         in_specs=[SMEM] * smem + [VMEM] * (len(args) - smem),
-        out_specs=[VMEM] * len(outs),
+        out_specs=spaces,
         scratch_shapes=list(scratch),
     )(*args)
 
 
-def combine_kernel(nbr, ham, out):
-    blocks, slots = ham.shape[0], ham.shape[1]
-    width = ham.shape[3]
-    for r in range(blocks):
+def combine_kernel(which, nbr, ham, *refs):
+    out = refs[-1]
+    slots, width = ham.shape[1], ham.shape[3]
+    for i, r in enumerate(which):
         layer = FACE + r // FACE * FACE
         for k, position in enumerate((r, layer, layer + 1, r + 2 * FACE)):
             total = jnp.zeros(ham.shape[2:], F32)
@@ -52,50 +56,108 @@
                 total = total + keep * ham[r, j].astype(F32)
             total = total.astype(BF16)
             for copy in range(out.shape[0]):
-                out[copy, r, :, k * width : (k + 1) * width] = total
-
-
-def apply_kernel(prior, copies, core, ham, vec, from_far, from_near, *rest):
-    before = rest[0] if prior else None
-    rest = rest[1:] if prior else rest
-    ext = rest[-1]
+                out[copy, i, :, k * width : (k + 1) * width] = total
+
+
+def product(ham, i, r, ext):
+    tile = ham.shape[3] // 4
+    layer = FACE + r // FACE * FACE
+    rhs = jnp.concatenate(
+        [
+            ext[r * tile : (r + 1) * tile],
+            ext[layer * tile : (layer + FACE) * tile],
+            ext[(r + 2 * FACE) * tile : (r + 2 * FACE + 1) * tile],
+        ],
+        axis=0,
+    )
+    return dot(ham[:, i].reshape(tile, 4 * tile), rhs)
+
+
+def fill_halo(core, ext, from_far, from_near):
     edge = from_far.shape[0]
-    rows = vec.shape[0]
+    last = ext.shape[0] - edge
+    c = core[0]
+    ext[pl.ds(pl.multiple_of(c * last, edge), edge)] = from_far[...]
+    ext[pl.ds(pl.multiple_of((1 - c) * last, edge), edge)] = from_near[...]
+
+
+def outer_kernel(outer, core, ham, vec, from_far, from_near, out, far, near, ext):
+    edge, rows = from_far.shape[0], vec.shape[0]
     tile = edge // FACE
+    ext[edge : edge + rows] = vec[...]
+    fill_halo(core, ext, from_far, from_near)
+    for i, r in enumerate(outer):
+        out[i * tile : (i + 1) * tile] = product(ham, i, r, ext).astype(BF16)
     c = core[0]
-    ext[edge : edge + rows] = vec[...]
-    ext[pl.ds(pl.multiple_of((1 - c) * (edge + rows), edge), edge)] = from_near[...]
-    ext[pl.ds(pl.multiple_of(c * (edge + rows), edge), edge)] = from_far[...]
-    out = rest[0]
-    for r in range(rows // tile):
-        layer = FACE + r // FACE * FACE
-        lhs = ham[:, r].reshape(tile, 4 * tile)
-        rhs = jnp.concatenate(
-            [
-                ext[r * tile : (r + 1) * tile],
-                ext[layer * tile : (layer + FACE) * tile],
-                ext[(r + 2 * FACE) * tile : (r + 2 * FACE + 1) * tile],
-            ],
-            axis=0,
-        )
-        value = dot(lhs, rhs)
-        here = slice(r * tile, (r + 1) * tile)
-        if prior:
-            value = 2.0 * value - before[here].astype(F32)
-        value = value.astype(BF16)
-        out[here] = value
-        if copies:
-            for copy in range(copies):
-                rest[3][copy, here] = value
-    if len(rest) > 2:
-        rest[1][...] = out[pl.ds(pl.multiple_of(c * (rows - edge), edge), edge)]
-        rest[2][...] = out[pl.ds(pl.multiple_of((1 - c) * (rows - edge), edge), edge)]
+    far[...] = out[pl.ds(pl.multiple_of(c * edge, edge), edge)]
+    near[...] = out[pl.ds(pl.multiple_of((1 - c) * edge, edge), edge)]
+
+
+def step(outer, inner, ham_outer, ham_inner, ext, before, out):
+    tile = ham_outer.shape[3] // 4
+    for which, ham in ((outer, ham_outer), (inner, ham_inner)):
+        for i, r in enumerate(which):
+            here = slice(r * tile, (r + 1) * tile)
+            value = product(ham, i, r, ext)
+            if before is not None:
+                value = 2.0 * value - before[here].astype(F32)
+            out[here] = value.astype(BF16)
+
+
+def edges_out(core, out, far, near):
+    edge = far.shape[0]
+    last = out.shape[0] - edge
+    c = core[0]
+    far[...] = out[pl.ds(pl.multiple_of(c * last, edge), edge)]
+    near[...] = out[pl.ds(pl.multiple_of((1 - c) * last, edge), edge)]
+
+
+def second_kernel(
+    outer, inner, core, ham_outer, ham_inner, vec, first_outer, from_far, from_near,
+    first, second, far, near, ext,
+):
+    edge, rows = from_far.shape[0], vec.shape[0]
+    tile = edge // FACE
+    ext[edge : edge + rows] = vec[...]
+    for i, r in enumerate(outer):
+        first[r * tile : (r + 1) * tile] = first_outer[i * tile : (i + 1) * tile]
+    for i, r in enumerate(inner):
+        first[r * tile : (r + 1) * tile] = product(ham_inner, i, r, ext).astype(BF16)
+    ext[edge : edge + rows] = first[...]
+    fill_halo(core, ext, from_far, from_near)
+    step(outer, inner, ham_outer, ham_inner, ext, vec, second)
+    edges_out(core, second, far, near)
+
+
+def third_kernel(
+    outer, inner, core, ham_outer, ham_inner, vec, before, from_far, from_near,
+    out, copies, far, near, ext, sems,
+):
+    edge, rows = from_far.shape[0], vec.shape[0]
+    ext[edge : edge + rows] = vec[...]
+    fill_halo(core, ext, from_far, from_near)
+    step(outer, inner, ham_outer, ham_inner, ext, before, out)
+    sends = [pltpu.make_async_copy(out, copies.at[i], sems.at[i]) for i in range(copies.shape[0])]
+    for send in sends:
+        send.start()
+    edges_out(core, out, far, near)
+    for send in sends:
+        send.wait()
+
+
+def applied_kernel(
+    outer, inner, core, ham_outer, ham_inner, vec, from_far, from_near, out, ext
+):
+    edge, rows = from_far.shape[0], vec.shape[0]
+    ext[edge : edge + rows] = vec[...]
+    fill_halo(core, ext, from_far, from_near)
+    step(outer, inner, ham_outer, ham_inner, ext, None, out)
 
 
 def gram_kernel(third, own, other, out):
-    right = jnp.concatenate([own[...], other[...]], axis=1)
     share = out.shape[1]
     per = third.shape[2] // share
+    right = jnp.concatenate([own[...], other[...]], axis=1)
     for y in range(third.shape[0]):
         block = dot(third[y], right, ((0,), (0,))).astype(BF16)
         for i in range(per):
@@ -152,38 +214,54 @@
     core = lax.axis_index("core")
     scalar = core.astype(jnp.int32).reshape(1)
 
-    (shares,) = call(
-        combine_kernel, [(nband, blocks, strip, 4 * tile)], (neighbors, hamiltonian), smem=1, far=(1,)
-    )
-    tiles = gather(shares, BAND)
+    outer = (*range(FACE), *range(blocks - FACE, blocks))
+    inner = tuple(range(FACE, blocks - FACE))
+
+    def shares(which, *after):
+        outs = [(nband, len(which), strip, 4 * tile)]
+        kernel = functools.partial(combine_kernel, which)
+        return call(kernel, outs, (neighbors, hamiltonian, *after), smem=1, far=(1,))[0]
+
+    def run(kernel, outs, args, scratch=(), far_outs=()):
+        ext = pltpu.VMEM((rows + 2 * edge, width), BF16)
+        return call(kernel, outs, (scalar, *args), (ext, *scratch), smem=1, far_outs=far_outs)
+
+    whole, face = (rows, width), (edge, width)
+    ham_outer = gather(shares(outer), BAND)
     received = swap(
         lax.dynamic_slice_in_dim(orbitals, core * (rows - edge), edge, 0),
         lax.dynamic_slice_in_dim(orbitals, (1 - core) * (rows - edge), edge, 0),
     )
-
-    def apply(vec, received, before=None, copies=0, edges=True):
-        args = (scalar, tiles, vec, *received) + (() if before is None else (before,))
-        outs = [(rows, width)] + [(edge, width)] * (2 if edges else 0)
-        if copies:
-            outs.append((copies, rows, width))
-        return call(
-            functools.partial(apply_kernel, before is not None, copies),
-            outs,
-            args,
-            (pltpu.VMEM((rows + 2 * edge, width), BF16),),
-            smem=1,
-        )
-
-    first, *edges = apply(orbitals, received)
-    second, *edges = apply(first, swap(*edges), orbitals)
-    third, *edges, copies = apply(second, swap(*edges), first, copies=ny)
+    ham_inner = gather(shares(inner, *received), BAND)
+    first_outer, *faces = run(
+        functools.partial(outer_kernel, outer),
+        [(len(outer) * tile, width), face, face],
+        (ham_outer, orbitals, *received),
+    )
+    first, second, *faces = run(
+        functools.partial(second_kernel, outer, inner),
+        [whole, whole, face, face],
+        (ham_outer, ham_inner, orbitals, first_outer, *swap(*faces)),
+    )
+    third, copies, *faces = run(
+        functools.partial(third_kernel, outer, inner),
+        [whole, (ny, rows, width), face, face],
+        (ham_outer, ham_inner, second, first, *swap(*faces)),
+        (pltpu.SemaphoreType.DMA((ny,)),),
+        far_outs=(1,),
+    )
     third_all = gather(copies, "y")
-    (applied,) = apply(third, swap(*edges), edges=False)
+    (applied,) = run(
+        functools.partial(applied_kernel, outer, inner),
+        [whole],
+        (ham_outer, ham_inner, third, *swap(*faces)),
+    )
     other = lax.ppermute(applied, "xl", [(0, 1), (1, 0)])
 
     rows_all = rows * lax.axis_size(SLAB)
     scale = 1.0 / math.sqrt(float(rows_all) * float(width * nband))
     share = ny * width // near
+
     (partial_gram,) = call(gram_kernel, [(near, share, 2 * width)], (third_all, applied, other))
     (summed,) = call(
         functools.partial(sum_kernel, None),

time: 144 us -> 148 us (1.028)
  Pallas kernels: 5.81 us -> 11.1 us
  local copies, waits for them, and re-layouts: 2.23 us -> 0.02 us
    all_to_all x2 -> x3, starting transfers between devices: 9.58 us -> 14.8 us  [gather(): return lax.all_to_all(copies, axes, 0, 0, tiled=True)]
    pallas_call x10 -> x11, Pallas kernels: 5.81 us -> 11.1 us  [call(): pl.pallas_call(kernel, out_shape=[(jax.ShapeDtypeStruct if p else pltpu.V...]
    ppermute x4, starting transfers between devices: 14 us -> 11.6 us  [swap(): from_far = lax.ppermute(far, SLAB, pairs)]
    unnamed x8 -> x2, local copies, waits for them, and re-layouts: 2.22 us -> 0.01 us
    ppermute x4, starting transfers between devices: 32.5 us -> 31 us  [swap(): return (from_far, lax.ppermute(near, 'core', [(0, 1), (1, 0)]))]
  transfers between devices with their start and end apart: 11 -> 12, of which waited for: 5 -> 5; matrix products, arithmetic and copies ran while one was open for 0% -> 0% of each run, Pallas kernels for 0% -> 2%
where the time goes in v3:
time: 148 us; the launch traced here: 147 us
  blocking collectives  65.5 us (44%)
  starting transfers between devices  59.3 us (40%)
  Pallas kernels  11.1 us (8%)
  waiting for transfers between devices  11 us (7%)
    all_to_all x4, blocking collectives, gather(): return lax.all_to_all(copies, axes, 0, 0, tiled=True)  65.5 us
    ppermute x4, starting transfers between devices, swap(): return (from_far, lax.ppermute(near, 'core', [(0, 1), (1, 0)]))  31 us
    all_to_all x3, starting transfers between devices, gather(): return lax.all_to_all(copies, axes, 0, 0, tiled=True)  14.8 us
    ppermute x4, starting transfers between devices, swap(): from_far = lax.ppermute(far, SLAB, pairs)  11.6 us
    pallas_call x11, Pallas kernels, call(): pl.pallas_call(kernel, out_shape=[(jax.ShapeDtypeStruct if p else pltpu.V...  11.1 us
    ppermute x1, waiting for transfers between devices, body(): other = lax.ppermute(applied, 'xl', [(0, 1), (1, 0)])  7.47 us
    ppermute x4, waiting for transfers between devices, swap(): return (from_far, lax.ppermute(near, 'core', [(0, 1), (1, 0)]))  3.48 us
  transfers between devices with their start and end apart: 12, of which 5 were waited for; matrix products, arithmetic and copies ran while one was open for 0% of the time, Pallas kernels for 2%

profile of v3, /device:TPU:1, one launch (start us, length us, event | category | flops | bytes accessed | tf_op | source)
XLA Modules:
  0.0 147.1 jit_solution(5993779362212144009)
XLA Ops:
  0.0 1.9 %shard_map.37 = bf16[8,4,16,512]{3,2,1,0:T(8,128)(2,1)} custom-call(s32[8,7]{1,0:T(8,128)} %nbr.3, bf16[8,7,16,128]{3,2,1,0:T(8,128)(2,1)} %ham.3), custom_call_target="tpu_custom_call" | custom-call | tf_op jit(solution)/shard_map/pallas_call | solution.py:36
  1.9 0.0 copy-start
  1.9 6.1 %all-to-all-start = ((bf16[8,4,16,512]{3,2,1,0:T(8,128)(2,1)}), bf16[8,4,16,512]{3,2,1,0:T(8,128)(2,1)S(1)}, u32[]{:S(2)}, u32[]{:S(2)}) async-start(bf16[8,4,16,512]{3,2,1,0:T(8,128)(2,1)} %shard_map.37), calls=%async_computation | async-start | bytes 1048576 | tf_op jit(solution)/shard_map/all_to_all | solution.py:199
  8.0 0.0 copy-done
  8.0 5.2 %collective-permute-start = (bf16[256,128]{1,0:T(8,128)(2,1)S(1)}, bf16[256,128]{1,0:T(8,128)(2,1)S(1)}, u32[]{:S(2)}, u32[]{:S(2)}) collective-permute-start(bf16[256,128]{1,0:T(8,128)(2,1)S(1)} %get-tuple-element.28), channel_id=1, source_target_pairs={{0,504},{8,16},{16,8},{24,32},{32,24},{40,48},{48,40},{56,64},{64,... | collective-permute-start | bytes 196616 | tf_op jit(solution)/shard_map/ppermute | solution.py:205
  13.2 10.4 %collective-permute-start.1 = (bf16[256,128]{1,0:T(8,128)(2,1)S(1)}, bf16[256,128]{1,0:T(8,128)(2,1)S(1)}, u32[]{:S(2)}, u32[]{:S(2)}) collective-permute-start(bf16[256,128]{1,0:T(8,128)(2,1)S(1)} %get-tuple-element.27), channel_id=1, source_target_pairs={{0,8},{8,0},{1,9},{9,1},{2,10},{10,2},{3,11},{11,3},{4,12},{12,4},... | collective-permute-start | bytes 196616 | tf_op jit(solution)/shard_map/ppermute | solution.py:206
  23.6 0.0 collective-permute-done.refs_0_.from_far
  23.6 0.9 collective-permute-done.1.refs_1_.from_near
  24.5 1.9 %shard_map.38 = bf16[8,4,16,512]{3,2,1,0:T(8,128)(2,1)} custom-call(s32[8,7]{1,0:T(8,128)} %nbr.3, bf16[8,7,16,128]{3,2,1,0:T(8,128)(2,1)} %ham.3, bf16[256,128]{1,0:T(8,128)(2,1)S(1)} %collective-permute-done.refs_0_.from_far, bf16[256,128]{1,0:T(8,128)(2,1)S(1)} %collective-permute-done.1.refs_1_.from_near), custom_call_target="tpu_custom_call" | custom-call | tf_op jit(solution)/shard_map/pallas_call | solution.py:36
  26.3 0.0 all-to-all-done.ham.ham_outer
  26.4 4.5 %all-to-all-start.1 = ((bf16[8,4,16,512]{3,2,1,0:T(8,128)(2,1)}), bf16[8,4,16,512]{3,2,1,0:T(8,128)(2,1)S(1)}, u32[]{:S(2)}, u32[]{:S(2)}) async-start(bf16[8,4,16,512]{3,2,1,0:T(8,128)(2,1)} %shard_map.38), calls=%async_computation.1 | async-start | bytes 1048576 | tf_op jit(solution)/shard_map/all_to_all | solution.py:199
  30.9 0.3 shard_map.39
  31.2 1.9 %collective-permute-start.2 = (bf16[256,128]{1,0:T(8,128)(2,1)S(1)}, bf16[256,128]{1,0:T(8,128)(2,1)S(1)}, u32[]{:S(2)}, u32[]{:S(2)}) collective-permute-start(bf16[256,128]{1,0:T(8,128)(2,1)S(1)} %get-tuple-element.17), channel_id=1, source_target_pairs={{0,504},{8,16},{16,8},{24,32},{32,24},{40,48},{48,40},{56,64},{64,... | collective-permute-start | bytes 196616 | tf_op jit(solution)/shard_map/ppermute | solution.py:205
  33.1 7.1 %collective-permute-start.3 = (bf16[256,128]{1,0:T(8,128)(2,1)S(1)}, bf16[256,128]{1,0:T(8,128)(2,1)S(1)}, u32[]{:S(2)}, u32[]{:S(2)}) collective-permute-start(bf16[256,128]{1,0:T(8,128)(2,1)S(1)} %get-tuple-element.18), channel_id=1, source_target_pairs={{0,8},{8,0},{1,9},{9,1},{2,10},{10,2},{3,11},{11,3},{4,12},{12,4},... | collective-permute-start | bytes 196616 | tf_op jit(solution)/shard_map/ppermute | solution.py:206
  40.2 0.0 collective-permute-done.2.from_far
  40.2 0.9 collective-permute-done.3.from_near
  41.1 0.0 all-to-all-done.1.ham_inner
  41.1 0.8 shard_map.40
  41.9 2.6 %collective-permute-start.4 = (bf16[256,128]{1,0:T(8,128)(2,1)S(1)}, bf16[256,128]{1,0:T(8,128)(2,1)S(1)}, u32[]{:S(2)}, u32[]{:S(2)}) collective-permute-start(bf16[256,128]{1,0:T(8,128)(2,1)S(1)} %get-tuple-element.21), channel_id=1, source_target_pairs={{0,504},{8,16},{16,8},{24,32},{32,24},{40,48},{48,40},{56,64},{64,... | collective-permute-start | bytes 196616 | tf_op jit(solution)/shard_map/ppermute | solution.py:205
  44.5 7.1 %collective-permute-start.5 = (bf16[256,128]{1,0:T(8,128)(2,1)S(1)}, bf16[256,128]{1,0:T(8,128)(2,1)S(1)}, u32[]{:S(2)}, u32[]{:S(2)}) collective-permute-start(bf16[256,128]{1,0:T(8,128)(2,1)S(1)} %get-tuple-element.22), channel_id=1, source_target_pairs={{0,8},{8,0},{1,9},{9,1},{2,10},{10,2},{3,11},{11,3},{4,12},{12,4},... | collective-permute-start | bytes 196616 | tf_op jit(solution)/shard_map/ppermute | solution.py:206
  51.6 0.0 collective-permute-done.4.from_far
  51.6 0.9 collective-permute-done.5.from_near
  52.5 1.5 %shard_map.41 = (bf16[1024,128]{1,0:T(8,128)(2,1)S(1)}, bf16[4,1024,128]{2,1,0:T(8,128)(2,1)}, bf16[256,128]{1,0:T(8,128)(2,1)S(1)}, bf16[256,128]{1,0:T(8,128)(2,1)S(1)}) custom-call(s32[1]{0:T(128)} %bitcast.core, bf16[8,4,16,512]{3,2,1,0:T(8,128)(2,1)S(1)} %all-to-all-done.ham.ham_outer, bf16[8,4,16,512]{3,2,1,0:T(8,128)(2,1)S(1)} %all-to-all-done.1.ham_inner, ...), custom_call_target="tpu_custom_call" | custom-call | tf_op jit(solution)/shard_map/pallas_call | solution.py:36
  54.0 4.2 %all-to-all-start.2 = ((bf16[4,1024,128]{2,1,0:T(8,128)(2,1)}), bf16[4,1024,128]{2,1,0:T(8,128)(2,1)}, u32[]{:S(2)}, u32[]{:S(2)}) async-start(bf16[4,1024,128]{2,1,0:T(8,128)(2,1)} %get-tuple-element.23), calls=%async_computation.2 | async-start | bytes 2097152 | tf_op jit(solution)/shard_map/all_to_all | solution.py:199
  58.2 1.9 %collective-permute-start.6 = (bf16[256,128]{1,0:T(8,128)(2,1)S(1)}, bf16[256,128]{1,0:T(8,128)(2,1)S(1)}, u32[]{:S(2)}, u32[]{:S(2)}) collective-permute-start(bf16[256,128]{1,0:T(8,128)(2,1)S(1)} %get-tuple-element.25), channel_id=1, source_target_pairs={{0,504},{8,16},{16,8},{24,32},{32,24},{40,48},{48,40},{56,64},{64,... | collective-permute-start | bytes 196616 | tf_op jit(solution)/shard_map/ppermute | solution.py:205
  60.2 6.4 %collective-permute-start.7 = (bf16[256,128]{1,0:T(8,128)(2,1)S(1)}, bf16[256,128]{1,0:T(8,128)(2,1)S(1)}, u32[]{:S(2)}, u32[]{:S(2)}) collective-permute-start(bf16[256,128]{1,0:T(8,128)(2,1)S(1)} %get-tuple-element.26), channel_id=1, source_target_pairs={{0,8},{8,0},{1,9},{9,1},{2,10},{10,2},{3,11},{11,3},{4,12},{12,4},... | collective-permute-start | bytes 196616 | tf_op jit(solution)/shard_map/ppermute | solution.py:206
  66.6 0.0 collective-permute-done.6.from_far
  66.6 0.9 collective-permute-done.7.from_near
  67.4 0.4 shard_map.42.own.applied
  67.9 1.9 %collective-permute-start.8 = (bf16[1024,128]{1,0:T(8,128)(2,1)S(1)}, bf16[1024,128]{1,0:T(8,128)(2,1)S(1)}, u32[]{:S(2)}, u32[]{:S(2)}) collective-permute-start(bf16[1024,128]{1,0:T(8,128)(2,1)S(1)} %shard_map.42.own.applied), channel_id=1, source_target_pairs={{0,1},{1,0},{2,3},{3,2},{4,5},{5,4},{6,7},{7,6},{8,9},{9,8},{10,11... | collective-permute-start | bytes 786440 | tf_op jit(solution)/shard_map/ppermute | solution.py:259
  69.8 7.5 %collective-permute-done.8.other = bf16[1024,128]{1,0:T(8,128)(2,1)S(1)} collective-permute-done((bf16[1024,128]{1,0:T(8,128)(2,1)S(1)}, bf16[1024,128]{1,0:T(8,128)(2,1)S(1)}, u32[]{:S(2)}, u32[]{:S(2)}) %collective-permute-start.8) | collective-permute-done | bytes 262176 | tf_op jit(solution)/shard_map/ppermute | solution.py:259
  77.3 0.0 all-to-all-done.2.third
  77.3 1.7 %shard_map.43 = bf16[16,32,256]{2,1,0:T(8,128)(2,1)S(1)} custom-call(bf16[4,1024,128]{2,1,0:T(8,128)(2,1)} %all-to-all-done.2.third, bf16[1024,128]{1,0:T(8,128)(2,1)S(1)} %shard_map.42.own.applied, bf16[1024,128]{1,0:T(8,128)(2,1)S(1)} %collective-permute-done.8.other), custom_call_target="tpu_custom_call" | custom-call | tf_op jit(solution)/shard_map/pallas_call | solution.py:36
  79.0 14.7 %all_to_all.35.parts = bf16[16,32,256]{2,1,0:T(8,128)(2,1)S(1)} all-to-all(bf16[16,32,256]{2,1,0:T(8,128)(2,1)S(1)} %shard_map.43), channel_id=1, replica_groups=mesh['z2'=4,'z1'=4,'xh'=2,'core'=2,'y'=4,'xl'=2] {'z1','xh','core'}, dimensions={0} | all-to-all | bytes 524288 | tf_op jit(solution)/shard_map/all_to_all | solution.py:199
  93.8 21.0 %all_to_all.36.parts = bf16[4,32,256]{2,1,0:T(8,128)(2,1)S(1)} all-to-all(bf16[4,32,256]{2,1,0:T(8,128)(2,1)S(1)} %shard_map.44), channel_id=1, replica_groups=mesh['z2'=4,'z1'=4,'xh'=2,'core'=2,'y'=4,'xl'=2] {'z2'}, dimensions={0} | all-to-all | bytes 131072 | tf_op jit(solution)/shard_map/all_to_all | solution.py:199
  114.8 16.1 %all_to_all.37.gram = bf16[16,32,256]{2,1,0:T(8,128)(2,1)S(1)} all-to-all(bf16[16,32,256]{2,1,0:T(8,128)(2,1)S(1)} %shard_map.45), channel_id=1, replica_groups=mesh['z2'=4,'z1'=4,'xh'=2,'core'=2,'y'=4,'xl'=2] {'z1','xh','core'}, dimensions={0} | all-to-all | bytes 524288 | tf_op jit(solution)/shard_map/all_to_all | solution.py:199
  130.9 1.7 %shard_map.46 = bf16[8,128,256]{2,1,0:T(8,128)(2,1)S(1)} custom-call(bf16[4,1024,128]{2,1,0:T(8,128)(2,1)} %all-to-all-done.2.third, bf16[16,32,256]{2,1,0:T(8,128)(2,1)S(1)} %all_to_all.37.gram, bf16[1024,128]{1,0:T(8,128)(2,1)S(1)} %shard_map.42.own.applied), custom_call_target="tpu_custom_call" | custom-call | tf_op jit(solution)/shard_map/pallas_call | solution.py:36
  132.5 13.7 %all_to_all.38.parts = bf16[8,128,256]{2,1,0:T(8,128)(2,1)S(1)} all-to-all(bf16[8,128,256]{2,1,0:T(8,128)(2,1)S(1)} %shard_map.46), channel_id=1, replica_groups=mesh['z2'=4,'z1'=4,'xh'=2,'core'=2,'y'=4,'xl'=2] {'y','xl'}, dimensions={0} | all-to-all | bytes 1048576 | tf_op jit(solution)/shard_map/all_to_all | solution.py:199
  146.3 0.8 shard_map.47
  (3 shorter events, 0.1 us)
Async XLA Ops:
  1.9 6.1 %copy-start = (bf16[1024,128]{1,0:T(8,128)(2,1)S(1)}, bf16[1024,128]{1,0:T(8,128)(2,1)}, u32[]{:S(2)}) copy-start(bf16[1024,128]{1,0:T(8,128)(2,1)} %vec.3) | copy-start | bytes 786436
  1.9 24.5 %all-to-all-start = ((bf16[8,4,16,512]{3,2,1,0:T(8,128)(2,1)}), bf16[8,4,16,512]{3,2,1,0:T(8,128)(2,1)S(1)}, u32[]{:S(2)}, u32[]{:S(2)}) async-start(bf16[8,4,16,512]{3,2,1,0:T(8,128)(2,1)} %shard_map.37), calls=%async_computation | async-start | bytes 1048576 | tf_op jit(solution)/shard_map/all_to_all | solution.py:199
  8.0 15.6 %collective-permute-start = (bf16[256,128]{1,0:T(8,128)(2,1)S(1)}, bf16[256,128]{1,0:T(8,128)(2,1)S(1)}, u32[]{:S(2)}, u32[]{:S(2)}) collective-permute-start(bf16[256,128]{1,0:T(8,128)(2,1)S(1)} %get-tuple-element.28), channel_id=1, source_target_pairs={{0,504},{8,16},{16,8},{24,32},{32,24},{40,48},{48,40},{56,64},{64,... | collective-permute-start | bytes 196616 | tf_op jit(solution)/shard_map/ppermute | solution.py:205
  13.2 11.3 %collective-permute-start.1 = (bf16[256,128]{1,0:T(8,128)(2,1)S(1)}, bf16[256,128]{1,0:T(8,128)(2,1)S(1)}, u32[]{:S(2)}, u32[]{:S(2)}) collective-permute-start(bf16[256,128]{1,0:T(8,128)(2,1)S(1)} %get-tuple-element.27), channel_id=1, source_target_pairs={{0,8},{8,0},{1,9},{9,1},{2,10},{10,2},{3,11},{11,3},{4,12},{12,4},... | collective-permute-start | bytes 196616 | tf_op jit(solution)/shard_map/ppermute | solution.py:206
  26.4 14.8 %all-to-all-start.1 = ((bf16[8,4,16,512]{3,2,1,0:T(8,128)(2,1)}), bf16[8,4,16,512]{3,2,1,0:T(8,128)(2,1)S(1)}, u32[]{:S(2)}, u32[]{:S(2)}) async-start(bf16[8,4,16,512]{3,2,1,0:T(8,128)(2,1)} %shard_map.38), calls=%async_computation.1 | async-start | bytes 1048576 | tf_op jit(solution)/shard_map/all_to_all | solution.py:199
  31.2 9.0 %collective-permute-start.2 = (bf16[256,128]{1,0:T(8,128)(2,1)S(1)}, bf16[256,128]{1,0:T(8,128)(2,1)S(1)}, u32[]{:S(2)}, u32[]{:S(2)}) collective-permute-start(bf16[256,128]{1,0:T(8,128)(2,1)S(1)} %get-tuple-element.17), channel_id=1, source_target_pairs={{0,504},{8,16},{16,8},{24,32},{32,24},{40,48},{48,40},{56,64},{64,... | collective-permute-start | bytes 196616 | tf_op jit(solution)/shard_map/ppermute | solution.py:205
  33.1 8.0 %collective-permute-start.3 = (bf16[256,128]{1,0:T(8,128)(2,1)S(1)}, bf16[256,128]{1,0:T(8,128)(2,1)S(1)}, u32[]{:S(2)}, u32[]{:S(2)}) collective-permute-start(bf16[256,128]{1,0:T(8,128)(2,1)S(1)} %get-tuple-element.18), channel_id=1, source_target_pairs={{0,8},{8,0},{1,9},{9,1},{2,10},{10,2},{3,11},{11,3},{4,12},{12,4},... | collective-permute-start | bytes 196616 | tf_op jit(solution)/shard_map/ppermute | solution.py:206
  41.9 9.7 %collective-permute-start.4 = (bf16[256,128]{1,0:T(8,128)(2,1)S(1)}, bf16[256,128]{1,0:T(8,128)(2,1)S(1)}, u32[]{:S(2)}, u32[]{:S(2)}) collective-permute-start(bf16[256,128]{1,0:T(8,128)(2,1)S(1)} %get-tuple-element.21), channel_id=1, source_target_pairs={{0,504},{8,16},{16,8},{24,32},{32,24},{40,48},{48,40},{56,64},{64,... | collective-permute-start | bytes 196616 | tf_op jit(solution)/shard_map/ppermute | solution.py:205
  44.5 8.0 %collective-permute-start.5 = (bf16[256,128]{1,0:T(8,128)(2,1)S(1)}, bf16[256,128]{1,0:T(8,128)(2,1)S(1)}, u32[]{:S(2)}, u32[]{:S(2)}) collective-permute-start(bf16[256,128]{1,0:T(8,128)(2,1)S(1)} %get-tuple-element.22), channel_id=1, source_target_pairs={{0,8},{8,0},{1,9},{9,1},{2,10},{10,2},{3,11},{11,3},{4,12},{12,4},... | collective-permute-start | bytes 196616 | tf_op jit(solution)/shard_map/ppermute | solution.py:206
  54.0 23.3 %all-to-all-start.2 = ((bf16[4,1024,128]{2,1,0:T(8,128)(2,1)}), bf16[4,1024,128]{2,1,0:T(8,128)(2,1)}, u32[]{:S(2)}, u32[]{:S(2)}) async-start(bf16[4,1024,128]{2,1,0:T(8,128)(2,1)} %get-tuple-element.23), calls=%async_computation.2 | async-start | bytes 2097152 | tf_op jit(solution)/shard_map/all_to_all | solution.py:199
  58.2 8.3 %collective-permute-start.6 = (bf16[256,128]{1,0:T(8,128)(2,1)S(1)}, bf16[256,128]{1,0:T(8,128)(2,1)S(1)}, u32[]{:S(2)}, u32[]{:S(2)}) collective-permute-start(bf16[256,128]{1,0:T(8,128)(2,1)S(1)} %get-tuple-element.25), channel_id=1, source_target_pairs={{0,504},{8,16},{16,8},{24,32},{32,24},{40,48},{48,40},{56,64},{64,... | collective-permute-start | bytes 196616 | tf_op jit(solution)/shard_map/ppermute | solution.py:205
  60.2 7.3 %collective-permute-start.7 = (bf16[256,128]{1,0:T(8,128)(2,1)S(1)}, bf16[256,128]{1,0:T(8,128)(2,1)S(1)}, u32[]{:S(2)}, u32[]{:S(2)}) collective-permute-start(bf16[256,128]{1,0:T(8,128)(2,1)S(1)} %get-tuple-element.26), channel_id=1, source_target_pairs={{0,8},{8,0},{1,9},{9,1},{2,10},{10,2},{3,11},{11,3},{4,12},{12,4},... | collective-permute-start | bytes 196616 | tf_op jit(solution)/shard_map/ppermute | solution.py:206
  67.9 9.4 %collective-permute-start.8 = (bf16[1024,128]{1,0:T(8,128)(2,1)S(1)}, bf16[1024,128]{1,0:T(8,128)(2,1)S(1)}, u32[]{:S(2)}, u32[]{:S(2)}) collective-permute-start(bf16[1024,128]{1,0:T(8,128)(2,1)S(1)} %shard_map.42.own.applied), channel_id=1, source_target_pairs={{0,1},{1,0},{2,3},{3,2},{4,5},{5,4},{6,7},{7,6},{8,9},{9,8},{10,11... | collective-permute-start | bytes 786440 | tf_op jit(solution)/shard_map/ppermute | solution.py:259

commit v4 on v2

v4 whole, which is shorter than its diff:
```python
import functools
import math

import jax
import jax.numpy as jnp
import numpy as np
from jax import lax
from jax.experimental import pallas as pl
from jax.experimental.pallas import tpu as pltpu
from jax.sharding import Mesh
from jax.sharding import PartitionSpec as P

SLAB = ("z2", "z1", "xh", "core")
BAND = ("y", "xl")
NEAR = ("z1", "xh")
PAIR = [(0, 1), (1, 0)]
FACE = 2
F32 = jnp.float32
BF16 = jnp.bfloat16

VMEM = pl.BlockSpec(memory_space=pltpu.VMEM)
SMEM = pl.BlockSpec(memory_space=pltpu.SMEM)
HBM = pl.BlockSpec(memory_space=pltpu.MemorySpace.HBM)


def dot(a, b, dims=((1,), (0,))):
    return lax.dot_general(a, b, (dims, ((), ())), preferred_element_type=F32)


def call(kernel, outs, args, scratch=(), smem=0, far=None, far_outs=(), last=False):
    far = far or {}
    args = [
        x if i < smem or i in far else pltpu.with_memory_space_constraint(x, pltpu.VMEM)
        for i, x in enumerate(args)
    ]
    shapes = []
    for i, out in enumerate(outs):
        make = jax.ShapeDtypeStruct if last or i in far_outs else pltpu.VMEM
        shapes.append(make(out, BF16) if isinstance(out, tuple) else out)
    return pl.pallas_call(
        kernel,
        out_shape=shapes,
        in_specs=[
            SMEM if i < smem else HBM if far.get(i, False) else VMEM for i in range(len(args))
        ],
        out_specs=[HBM if i in far_outs else VMEM for i in range(len(outs))],
        scratch_shapes=list(scratch),
    )(*args)


def combine_kernel(nbr, ham, out):
    blocks, slots = ham.shape[0], ham.shape[1]
    width = ham.shape[3]
    for r in range(blocks):
        layer = FACE + r // FACE * FACE
        for k, position in enumerate((r, layer, layer + 1, r + 2 * FACE)):
            total = jnp.zeros(ham.shape[2:], F32)
            for j in range(slots):
                keep = (nbr[r, j] == position).astype(F32)
                total = total + keep * ham[r, j].astype(F32)
            total = total.astype(BF16)
            for copy in range(out.shape[0]):
                out[copy, r, :, k * width : (k + 1) * width] = total


def product(ham, r, ext):
    tile = ham.shape[3] // 4
    layer = FACE + r // FACE * FACE
    rhs = jnp.concatenate(
        [
            ext[r * tile : (r + 1) * tile],
            ext[layer * tile : (layer + FACE) * tile],
            ext[(r + 2 * FACE) * tile : (r + 2 * FACE + 1) * tile],
        ],
        axis=0,
    )
    return dot(ham[:, r].reshape(tile, 4 * tile), rhs)


def fill(core, ext, vec, from_far, from_near):
    edge, rows = from_far.shape[0], vec.shape[0]
    c = core[0]
    ext[edge : edge + rows] = vec[...]
    ext[pl.ds(pl.multiple_of(c * (edge + rows), edge), edge)] = from_far[...]
    ext[pl.ds(pl.multiple_of((1 - c) * (edge + rows), edge), edge)] = from_near[...]


def step_kernel(prior, core, ham, vec, from_far, from_near, *rest):
    before = rest[0] if prior else None
    out, far, near, ext, *copying = rest[1:] if prior else rest
    if copying:
        out, copies, far, near, ext, sems = rest[1:]
    edge, rows = far.shape[0], vec.shape[0]
    tile = edge // FACE
    fill(core, ext, vec, from_far, from_near)
    for r in range(rows // tile):
        here = slice(r * tile, (r + 1) * tile)
        value = product(ham, r, ext)
        if prior:
            value = 2.0 * value - before[here].astype(F32)
        out[here] = value.astype(BF16)
    sends = []
    if copying:
        for i in range(copies.shape[0]):
            sends.append(pltpu.make_async_copy(out, copies.at[i], sems.at[i]))
    for send in sends:
        send.start()
    c = core[0]
    far[...] = out[pl.ds(pl.multiple_of(c * (rows - edge), edge), edge)]
    near[...] = out[pl.ds(pl.multiple_of((1 - c) * (rows - edge), edge), edge)]
    for send in sends:
        send.wait()


def inner_kernel(ham, vec, out, ext):
    rows = vec.shape[0]
    edge = (ext.shape[0] - rows) // 2
    tile = edge // FACE
    ext[edge : edge + rows] = vec[...]
    for i in range(out.shape[0] // tile):
        out[i * tile : (i + 1) * tile] = product(ham, FACE + i, ext).astype(BF16)


def outer_kernel(core, ham, vec, from_far, from_near, out, ext):
    edge, rows = from_far.shape[0], vec.shape[0]
    tile = edge // FACE
    fill(core, ext, vec, from_far, from_near)
    for i, r in enumerate((*range(FACE), *range(rows // tile - FACE, rows // tile))):
        out[i * tile : (i + 1) * tile] = product(ham, r, ext).astype(BF16)


def gram_kernel(core, third_far, inner, outer, inner2, outer2, third, give, mine, sems):
    rows, width = third.shape[1], third.shape[2]
    edge = outer.shape[0] // 2
    count = third.shape[0]
    fetches = [
        pltpu.make_async_copy(third_far.at[y], third.at[y], sems.at[y]) for y in range(count)
    ]
    for fetch in fetches:
        fetch.start()
    own = jnp.concatenate([outer[:edge], inner[...], outer[edge:]], axis=0)
    other = jnp.concatenate([outer2[:edge], inner2[...], outer2[edge:]], axis=0)
    right = jnp.concatenate([own, other], axis=1)
    for fetch in fetches:
        fetch.wait()
    half = count // 2
    c = core[0]
    for y in range(half):
        here = slice(y * width, (y + 1) * width)
        give[here] = dot(third[(1 - c) * half + y], right, ((0,), (0,))).astype(BF16)
        mine[here] = dot(third[c * half + y], right, ((0,), (0,)))


def join_kernel(mine, received, out):
    share = out.shape[1]
    total = (mine[...] + received[...].astype(F32)).astype(BF16)
    for i in range(out.shape[0]):
        out[i] = total[i * share : (i + 1) * share]


def sum_kernel(scale, parts, out):
    total = parts[0].astype(F32)
    for i in range(1, parts.shape[0]):
        total = total + parts[i].astype(F32)
    if scale is not None:
        total = total * scale
    total = total.astype(BF16)
    for copy in range(out.shape[0]):
        out[copy] = total


def mixed_kernel(core, third, gram, gram2, inner, outer, out):
    strips, height, width = out.shape[0], out.shape[1], third.shape[2]
    half = third.shape[0] // 2
    edge = outer.shape[0] // (2 * height)
    c = core[0]
    weights = jnp.concatenate(
        [g[...].reshape(half * width, g.shape[2]) for g in (gram, gram2)], axis=0
    )
    for s in range(strips):
        here = slice(s * height, (s + 1) * height)
        order = [c * half + y for y in range(half)] + [(1 - c) * half + y for y in range(half)]
        left = jnp.concatenate([third[y, here] for y in order], axis=1)
        value = dot(left, weights)
        if s < edge:
            applied = outer[here]
        elif s < strips - edge:
            applied = inner[(s - edge) * height : (s - edge + 1) * height]
        else:
            at = (s - strips + 2 * edge) * height
            applied = outer[at : at + height]
        out[s, :, :width] = (applied.astype(F32) - value[:, :width]).astype(BF16)
        out[s, :, width:] = (-value[:, width:]).astype(BF16)


def final_kernel(parts, out):
    width = parts.shape[2] // 2
    for b in range(parts.shape[0]):
        value = parts[b, :, :width].astype(F32) + parts[b ^ 1, :, width:].astype(F32)
        out[:, b * width : (b + 1) * width] = value.astype(BF16)


def gather(copies, axes):
    return lax.all_to_all(copies, axes, 0, 0, tiled=True)


def swap(far, near):
    count = lax.axis_size(SLAB)
    pairs = [(s, (s + 1) % count if s % 2 else (s - 1) % count) for s in range(count)]
    from_far = lax.ppermute(far, SLAB, pairs)
    return from_far, lax.ppermute(near, "core", PAIR)


def body(hamiltonian, neighbors, orbitals):
    blocks, _, strip, tile = hamiltonian.shape
    rows, width = orbitals.shape
    edge = FACE * tile
    ny, nband, near, far = (lax.axis_size(a) for a in ("y", BAND, NEAR, "z2"))
    core = lax.axis_index("core")
    scalar = core.astype(jnp.int32).reshape(1)

    (shares,) = call(
        combine_kernel, [(nband, blocks, strip, 4 * tile)], (neighbors, hamiltonian), smem=1, far={1: False}
    )
    tiles = gather(shares, BAND)
    received = swap(
        lax.dynamic_slice_in_dim(orbitals, core * (rows - edge), edge, 0),
        lax.dynamic_slice_in_dim(orbitals, (1 - core) * (rows - edge), edge, 0),
    )

    ext = pltpu.VMEM((rows + 2 * edge, width), BF16)
    whole, face, part = (rows, width), (edge, width), (rows - 2 * edge, width)

    def step(vec, received, before=()):
        return call(
            functools.partial(step_kernel, bool(before)),
            [whole, face, face],
            (scalar, tiles, vec, *received, *before),
            (ext,),
            smem=1,
        )

    first, *faces = step(orbitals, received)
    second, *faces = step(first, swap(*faces), (orbitals,))
    third, copies, *faces = call(
        functools.partial(step_kernel, True),
        [whole, (ny, rows, width), face, face],
        (scalar, tiles, second, *swap(*faces), first),
        (ext, pltpu.SemaphoreType.DMA((ny,))),
        smem=1,
        far_outs=(1,),
    )
    received = swap(*faces)
    third_far = gather(copies, "y")
    (inner,) = call(inner_kernel, [part], (tiles, third), (ext,))
    inner2 = lax.ppermute(inner, "xl", PAIR)
    (outer,) = call(outer_kernel, [(2 * edge, width)], (scalar, tiles, third, *received), (ext,), smem=1)
    outer2 = lax.ppermute(outer, "xl", PAIR)

    rows_all = rows * lax.axis_size(SLAB)
    scale = 1.0 / math.sqrt(float(rows_all) * float(width * nband))
    depth, columns = ny * width // 2, 2 * width
    share = depth // near
    third_all, give, mine = call(
        gram_kernel,
        [(ny, rows, width), (depth, columns), pltpu.VMEM((depth, columns), F32)],
        (scalar, third_far, inner, outer, inner2, outer2),
        (pltpu.SemaphoreType.DMA((ny,)),),
        smem=1,
        far={1: True},
    )
    received = lax.ppermute(give, "core", PAIR)
    (joined,) = call(join_kernel, [(near, share, columns)], (mine, received))
    (summed,) = call(
        functools.partial(sum_kernel, None), [(far, share, columns)], (gather(joined, NEAR),)
    )
    (scaled,) = call(
        functools.partial(sum_kernel, scale), [(near, share, columns)], (gather(summed, "z2"),)
    )
    gram = gather(scaled, NEAR)
    gram2 = lax.ppermute(gram, "core", PAIR)
    (partial_out,) = call(
        mixed_kernel,
        [(nband, rows // nband, columns)],
        (scalar, third_all, gram, gram2, inner, outer),
        smem=1,
    )
    (out,) = call(
        final_kernel, [(rows // nband, nband * width)], (gather(partial_out, BAND),), last=True
    )
    return out


def solution(mesh):
    slabs = mesh.shape["slab"]
    fine = Mesh(
        np.asarray(mesh.devices).reshape(slabs // 16, 4, 2, 2, mesh.shape["band"] // 2, 2),
        SLAB + BAND,
    )
    in_specs = (P(SLAB, None, BAND, None), P(SLAB, None), P(SLAB, BAND))
    out_specs = P(SLAB + BAND, None)
    return jax.shard_map(body, mesh=fine, in_specs=in_specs, out_specs=out_specs, check_vma=False)
```

time: 144 us -> 144 us (level)
  starting transfers between devices: 58 us -> 70.7 us
  blocking collectives: 65.7 us -> 55.4 us
  Pallas kernels: 5.81 us -> 8.21 us
  waiting for transfers between devices: 11 us -> 8.74 us
  local copies, waits for them, and re-layouts: 2.23 us -> 0.02 us
    ppermute x5 -> x8, starting transfers between devices: 34.4 us -> 46.3 us  [the longest x4 32.5 us: swap(): return (from_far, lax.ppermute(near, 'core', PAIR))]
    all_to_all x4, blocking collectives: 65.7 us -> 55.4 us  [gather(): return lax.all_to_all(copies, axes, 0, 0, tiled=True)]
    pallas_call x10 -> x12, Pallas kernels: 5.81 us -> 8.21 us  [call(): pl.pallas_call(kernel, out_shape=shapes, in_specs=[SMEM if i < smem else...]
    ppermute x5 -> x8, waiting for transfers between devices: 10.1 us -> 7.78 us  [the longest x1 2.7 us: body(): outer2 = lax.ppermute(outer, 'xl', PAIR)]
    unnamed x8 -> x2, local copies, waits for them, and re-layouts: 2.22 us -> 0.01 us
  transfers between devices with their start and end apart: 11 -> 14, of which waited for: 5 -> 7; matrix products, arithmetic and copies ran while one was open for 0% -> 0% of each run, Pallas kernels for 0% -> 0%
where the time goes in v4:
time: 144 us; the launch traced here: 143 us
  starting transfers between devices  70.7 us (49%)
  blocking collectives  55.4 us (38%)
  waiting for transfers between devices  8.74 us (6%)
  Pallas kernels  8.21 us (6%)
    all_to_all x4, blocking collectives, gather(): return lax.all_to_all(copies, axes, 0, 0, tiled=True)  55.4 us
    ppermute x4, starting transfers between devices, swap(): return (from_far, lax.ppermute(near, 'core', PAIR))  32.5 us
    ppermute x4, starting transfers between devices, swap(): from_far = lax.ppermute(far, SLAB, pairs)  14.1 us
    all_to_all x2, starting transfers between devices, gather(): return lax.all_to_all(copies, axes, 0, 0, tiled=True)  10.3 us
    pallas_call x12, Pallas kernels, call(): pl.pallas_call(kernel, out_shape=shapes, in_specs=[SMEM if i < smem else...  8.21 us
    ppermute x1, starting transfers between devices, body(): gram2 = lax.ppermute(gram, 'core', PAIR)  5.81 us
    ppermute x1, starting transfers between devices, body(): outer2 = lax.ppermute(outer, 'xl', PAIR)  3.36 us
  transfers between devices with their start and end apart: 14, of which 7 were waited for; matrix products, arithmetic and copies ran while one was open for 0% of the time, Pallas kernels for 0%

profile of v4, /device:TPU:1, one launch (start us, length us, event | category | flops | bytes accessed | tf_op | source)
XLA Modules:
  0.0 143.2 jit_solution(6034976879156145410)
XLA Ops:
  0.0 2.2 %shard_map.37 = bf16[8,8,16,512]{3,2,1,0:T(8,128)(2,1)} custom-call(s32[8,7]{1,0:T(8,128)} %nbr.1, bf16[8,7,16,128]{3,2,1,0:T(8,128)(2,1)} %ham.1), custom_call_target="tpu_custom_call" | custom-call | tf_op jit(solution)/shard_map/pallas_call | solution.py:40
  2.2 0.0 copy-start
  2.2 6.1 %all-to-all-start = ((bf16[8,8,16,512]{3,2,1,0:T(8,128)(2,1)}), bf16[8,8,16,512]{3,2,1,0:T(8,128)(2,1)S(1)}, u32[]{:S(2)}, u32[]{:S(2)}) async-start(bf16[8,8,16,512]{3,2,1,0:T(8,128)(2,1)} %shard_map.37), calls=%async_computation | async-start | bytes 2097152 | tf_op jit(solution)/shard_map/all_to_all | solution.py:204
  8.3 0.0 copy-done
  8.3 5.2 %collective-permute-start = (bf16[256,128]{1,0:T(8,128)(2,1)S(1)}, bf16[256,128]{1,0:T(8,128)(2,1)S(1)}, u32[]{:S(2)}, u32[]{:S(2)}) collective-permute-start(bf16[256,128]{1,0:T(8,128)(2,1)S(1)} %get-tuple-element.32), channel_id=1, source_target_pairs={{0,504},{8,16},{16,8},{24,32},{32,24},{40,48},{48,40},{56,64},{64,... | collective-permute-start | bytes 196616 | tf_op jit(solution)/shard_map/ppermute | solution.py:210
  13.5 10.4 %collective-permute-start.1 = (bf16[256,128]{1,0:T(8,128)(2,1)S(1)}, bf16[256,128]{1,0:T(8,128)(2,1)S(1)}, u32[]{:S(2)}, u32[]{:S(2)}) collective-permute-start(bf16[256,128]{1,0:T(8,128)(2,1)S(1)} %get-tuple-element.31), channel_id=1, source_target_pairs={{0,8},{8,0},{1,9},{9,1},{2,10},{10,2},{3,11},{11,3},{4,12},{12,4},... | collective-permute-start | bytes 196616 | tf_op jit(solution)/shard_map/ppermute | solution.py:211
  23.9 0.9 collective-permute-done.from_far
  24.8 0.0 collective-permute-done.1.from_near
  24.9 0.0 all-to-all-done.ham
  24.9 0.5 shard_map.38
  25.3 5.0 %collective-permute-start.2 = (bf16[256,128]{1,0:T(8,128)(2,1)S(1)}, bf16[256,128]{1,0:T(8,128)(2,1)S(1)}, u32[]{:S(2)}, u32[]{:S(2)}) collective-permute-start(bf16[256,128]{1,0:T(8,128)(2,1)S(1)} %get-tuple-element.19), channel_id=1, source_target_pairs={{0,504},{8,16},{16,8},{24,32},{32,24},{40,48},{48,40},{56,64},{64,... | collective-permute-start | bytes 196616 | tf_op jit(solution)/shard_map/ppermute | solution.py:210
  30.3 9.3 %collective-permute-start.3 = (bf16[256,128]{1,0:T(8,128)(2,1)S(1)}, bf16[256,128]{1,0:T(8,128)(2,1)S(1)}, u32[]{:S(2)}, u32[]{:S(2)}) collective-permute-start(bf16[256,128]{1,0:T(8,128)(2,1)S(1)} %get-tuple-element.20), channel_id=1, source_target_pairs={{0,8},{8,0},{1,9},{9,1},{2,10},{10,2},{3,11},{11,3},{4,12},{12,4},... | collective-permute-start | bytes 196616 | tf_op jit(solution)/shard_map/ppermute | solution.py:211
  39.6 0.0 collective-permute-done.2.from_far
  39.6 0.9 collective-permute-done.3.from_near
  40.5 0.5 shard_map.39
  41.0 1.9 %collective-permute-start.4 = (bf16[256,128]{1,0:T(8,128)(2,1)S(1)}, bf16[256,128]{1,0:T(8,128)(2,1)S(1)}, u32[]{:S(2)}, u32[]{:S(2)}) collective-permute-start(bf16[256,128]{1,0:T(8,128)(2,1)S(1)} %get-tuple-element.22), channel_id=1, source_target_pairs={{0,504},{8,16},{16,8},{24,32},{32,24},{40,48},{48,40},{56,64},{64,... | collective-permute-start | bytes 196616 | tf_op jit(solution)/shard_map/ppermute | solution.py:210
  42.9 6.4 %collective-permute-start.5 = (bf16[256,128]{1,0:T(8,128)(2,1)S(1)}, bf16[256,128]{1,0:T(8,128)(2,1)S(1)}, u32[]{:S(2)}, u32[]{:S(2)}) collective-permute-start(bf16[256,128]{1,0:T(8,128)(2,1)S(1)} %get-tuple-element.23), channel_id=1, source_target_pairs={{0,8},{8,0},{1,9},{9,1},{2,10},{10,2},{3,11},{11,3},{4,12},{12,4},... | collective-permute-start | bytes 196616 | tf_op jit(solution)/shard_map/ppermute | solution.py:211
  49.3 0.0 collective-permute-done.4.from_far
  49.3 0.9 collective-permute-done.5.from_near
  50.2 1.5 %shard_map.40 = (bf16[1024,128]{1,0:T(8,128)(2,1)S(1)}, bf16[4,1024,128]{2,1,0:T(8,128)(2,1)}, bf16[256,128]{1,0:T(8,128)(2,1)S(1)}, bf16[256,128]{1,0:T(8,128)(2,1)S(1)}) custom-call(s32[1]{0:T(128)} %bitcast.core, bf16[8,8,16,512]{3,2,1,0:T(8,128)(2,1)S(1)} %all-to-all-done.ham, bf16[1024,128]{1,0:T(8,128)(2,1)S(1)} %get-tuple-element.21.vec, ...), custom_call_target="tpu_custom_call" | custom-call | tf_op jit(solution)/shard_map/pallas_call | solution.py:40
  51.7 4.2 %all-to-all-start.1 = ((bf16[4,1024,128]{2,1,0:T(8,128)(2,1)}), bf16[4,1024,128]{2,1,0:T(8,128)(2,1)}, u32[]{:S(2)}, u32[]{:S(2)}) async-start(bf16[4,1024,128]{2,1,0:T(8,128)(2,1)} %get-tuple-element.24), calls=%async_computation.1 | async-start | bytes 2097152 | tf_op jit(solution)/shard_map/all_to_all | solution.py:204
  55.9 1.9 %collective-permute-start.6 = (bf16[256,128]{1,0:T(8,128)(2,1)S(1)}, bf16[256,128]{1,0:T(8,128)(2,1)S(1)}, u32[]{:S(2)}, u32[]{:S(2)}) collective-permute-start(bf16[256,128]{1,0:T(8,128)(2,1)S(1)} %get-tuple-element.26), channel_id=1, source_target_pairs={{0,504},{8,16},{16,8},{24,32},{32,24},{40,48},{48,40},{56,64},{64,... | collective-permute-start | bytes 196616 | tf_op jit(solution)/shard_map/ppermute | solution.py:210
  57.9 6.4 %collective-permute-start.7 = (bf16[256,128]{1,0:T(8,128)(2,1)S(1)}, bf16[256,128]{1,0:T(8,128)(2,1)S(1)}, u32[]{:S(2)}, u32[]{:S(2)}) collective-permute-start(bf16[256,128]{1,0:T(8,128)(2,1)S(1)} %get-tuple-element.27), channel_id=1, source_target_pairs={{0,8},{8,0},{1,9},{9,1},{2,10},{10,2},{3,11},{11,3},{4,12},{12,4},... | collective-permute-start | bytes 196616 | tf_op jit(solution)/shard_map/ppermute | solution.py:211
  64.2 0.3 shard_map.41.inner
  64.6 1.9 %collective-permute-start.8 = (bf16[512,128]{1,0:T(8,128)(2,1)S(1)}, bf16[512,128]{1,0:T(8,128)(2,1)S(1)}, u32[]{:S(2)}, u32[]{:S(2)}) collective-permute-start(bf16[512,128]{1,0:T(8,128)(2,1)S(1)} %shard_map.41.inner), channel_id=1, source_target_pairs={{0,1},{1,0},{2,3},{3,2},{4,5},{5,4},{6,7},{7,6},{8,9},{9,8},{10,11... | collective-permute-start | bytes 393224 | tf_op jit(solution)/shard_map/ppermute | solution.py:256
  66.5 0.0 collective-permute-done.6.from_far
  66.5 0.0 collective-permute-done.7.from_near
  66.5 0.3 shard_map.42.outer
  66.8 3.4 %collective-permute-start.9 = (bf16[512,128]{1,0:T(8,128)(2,1)S(1)}, bf16[512,128]{1,0:T(8,128)(2,1)S(1)}, u32[]{:S(2)}, u32[]{:S(2)}) collective-permute-start(bf16[512,128]{1,0:T(8,128)(2,1)S(1)} %shard_map.42.outer), channel_id=1, source_target_pairs={{0,1},{1,0},{2,3},{3,2},{4,5},{5,4},{6,7},{7,6},{8,9},{9,8},{10,11... | collective-permute-start | bytes 393224 | tf_op jit(solution)/shard_map/ppermute | solution.py:258
  70.2 1.4 collective-permute-done.8.inner2
  71.6 2.7 %collective-permute-done.9.outer2 = bf16[512,128]{1,0:T(8,128)(2,1)S(1)} collective-permute-done((bf16[512,128]{1,0:T(8,128)(2,1)S(1)}, bf16[512,128]{1,0:T(8,128)(2,1)S(1)}, u32[]{:S(2)}, u32[]{:S(2)}) %collective-permute-start.9) | collective-permute-done | bytes 131104 | tf_op jit(solution)/shard_map/ppermute | solution.py:258
  74.3 0.0 all-to-all-done.1.third_far
  74.3 1.7 %shard_map.43 = (bf16[4,1024,128]{2,1,0:T(8,128)(2,1)S(1)}, bf16[256,256]{1,0:T(8,128)(2,1)S(1)}, f32[256,256]{1,0:T(8,128)S(1)}) custom-call(s32[1]{0:T(128)} %bitcast.core, bf16[4,1024,128]{2,1,0:T(8,128)(2,1)} %all-to-all-done.1.third_far, bf16[512,128]{1,0:T(8,128)(2,1)S(1)} %shard_map.41.inner, bf16[512,128]{1,0:T(8,128)(2,1)S(1)} %shard_map.42.outer, ...), custom_call_target="tpu_custom_call" | custom-call | tf_op jit(solution)/shard_map/pallas_call | solution.py:40
  76.0 2.8 %collective-permute-start.10 = (bf16[256,256]{1,0:T(8,128)(2,1)S(1)}, bf16[256,256]{1,0:T(8,128)(2,1)S(1)}, u32[]{:S(2)}, u32[]{:S(2)}) collective-permute-start(bf16[256,256]{1,0:T(8,128)(2,1)S(1)} %get-tuple-element.30), channel_id=1, source_target_pairs={{0,8},{8,0},{1,9},{9,1},{2,10},{10,2},{3,11},{11,3},{4,12},{12,4},... | collective-permute-start | bytes 393224 | tf_op jit(solution)/shard_map/ppermute | solution.py:272
  78.8 1.0 collective-permute-done.10.received
  79.8 10.2 %all_to_all.30.parts = bf16[8,32,256]{2,1,0:T(8,128)(2,1)S(1)} all-to-all(bf16[8,32,256]{2,1,0:T(8,128)(2,1)S(1)} %shard_map.44), channel_id=1, replica_groups=mesh['z2'=4,'z1'=4,'xh'=2,'core'=2,'y'=4,'xl'=2] {'z1','xh'}, dimensions={0} | all-to-all | bytes 262144 | tf_op jit(solution)/shard_map/all_to_all | solution.py:204
  90.0 20.9 %all_to_all.31.parts = bf16[4,32,256]{2,1,0:T(8,128)(2,1)S(1)} all-to-all(bf16[4,32,256]{2,1,0:T(8,128)(2,1)S(1)} %shard_map.45), channel_id=1, replica_groups=mesh['z2'=4,'z1'=4,'xh'=2,'core'=2,'y'=4,'xl'=2] {'z2'}, dimensions={0} | all-to-all | bytes 131072 | tf_op jit(solution)/shard_map/all_to_all | solution.py:204
  110.9 10.8 %all_to_all.32.gram = bf16[8,32,256]{2,1,0:T(8,128)(2,1)S(1)} all-to-all(bf16[8,32,256]{2,1,0:T(8,128)(2,1)S(1)} %shard_map.46), channel_id=1, replica_groups=mesh['z2'=4,'z1'=4,'xh'=2,'core'=2,'y'=4,'xl'=2] {'z1','xh'}, dimensions={0} | all-to-all | bytes 262144 | tf_op jit(solution)/shard_map/all_to_all | solution.py:204
  121.7 5.8 %collective-permute-start.11 = (bf16[8,32,256]{2,1,0:T(8,128)(2,1)S(1)}, bf16[8,32,256]{2,1,0:T(8,128)(2,1)S(1)}, u32[]{:S(2)}, u32[]{:S(2)}) collective-permute-start(bf16[8,32,256]{2,1,0:T(8,128)(2,1)S(1)} %all_to_all.32.gram), channel_id=1, source_target_pairs={{0,8},{8,0},{1,9},{9,1},{2,10},{10,2},{3,11},{11,3},{4,12},{12,4},... | collective-permute-start | bytes 393224 | tf_op jit(solution)/shard_map/ppermute | solution.py:281
  127.5 1.0 collective-permute-done.11.gram2
  128.5 0.4 shard_map.47
  128.9 13.5 %all_to_all.33.parts = bf16[8,128,256]{2,1,0:T(8,128)(2,1)S(1)} all-to-all(bf16[8,128,256]{2,1,0:T(8,128)(2,1)S(1)} %shard_map.47), channel_id=1, replica_groups=mesh['z2'=4,'z1'=4,'xh'=2,'core'=2,'y'=4,'xl'=2] {'y','xl'}, dimensions={0} | all-to-all | bytes 1048576 | tf_op jit(solution)/shard_map/all_to_all | solution.py:204
  142.5 0.8 shard_map.48
  (4 shorter events, 0.1 us)
Async XLA Ops:
  2.2 6.1 %copy-start = (bf16[1024,128]{1,0:T(8,128)(2,1)S(1)}, bf16[1024,128]{1,0:T(8,128)(2,1)}, u32[]{:S(2)}) copy-start(bf16[1024,128]{1,0:T(8,128)(2,1)} %rest_0_.1) | copy-start | bytes 786436
  2.2 22.7 %all-to-all-start = ((bf16[8,8,16,512]{3,2,1,0:T(8,128)(2,1)}), bf16[8,8,16,512]{3,2,1,0:T(8,128)(2,1)S(1)}, u32[]{:S(2)}, u32[]{:S(2)}) async-start(bf16[8,8,16,512]{3,2,1,0:T(8,128)(2,1)} %shard_map.37), calls=%async_computation | async-start | bytes 2097152 | tf_op jit(solution)/shard_map/all_to_all | solution.py:204
  8.3 16.6 %collective-permute-start = (bf16[256,128]{1,0:T(8,128)(2,1)S(1)}, bf16[256,128]{1,0:T(8,128)(2,1)S(1)}, u32[]{:S(2)}, u32[]{:S(2)}) collective-permute-start(bf16[256,128]{1,0:T(8,128)(2,1)S(1)} %get-tuple-element.32), channel_id=1, source_target_pairs={{0,504},{8,16},{16,8},{24,32},{32,24},{40,48},{48,40},{56,64},{64,... | collective-permute-start | bytes 196616 | tf_op jit(solution)/shard_map/ppermute | solution.py:210
  13.5 11.3 %collective-permute-start.1 = (bf16[256,128]{1,0:T(8,128)(2,1)S(1)}, bf16[256,128]{1,0:T(8,128)(2,1)S(1)}, u32[]{:S(2)}, u32[]{:S(2)}) collective-permute-start(bf16[256,128]{1,0:T(8,128)(2,1)S(1)} %get-tuple-element.31), channel_id=1, source_target_pairs={{0,8},{8,0},{1,9},{9,1},{2,10},{10,2},{3,11},{11,3},{4,12},{12,4},... | collective-permute-start | bytes 196616 | tf_op jit(solution)/shard_map/ppermute | solution.py:211
  25.3 14.3 %collective-permute-start.2 = (bf16[256,128]{1,0:T(8,128)(2,1)S(1)}, bf16[256,128]{1,0:T(8,128)(2,1)S(1)}, u32[]{:S(2)}, u32[]{:S(2)}) collective-permute-start(bf16[256,128]{1,0:T(8,128)(2,1)S(1)} %get-tuple-element.19), channel_id=1, source_target_pairs={{0,504},{8,16},{16,8},{24,32},{32,24},{40,48},{48,40},{56,64},{64,... | collective-permute-start | bytes 196616 | tf_op jit(solution)/shard_map/ppermute | solution.py:210
  30.3 10.2 %collective-permute-start.3 = (bf16[256,128]{1,0:T(8,128)(2,1)S(1)}, bf16[256,128]{1,0:T(8,128)(2,1)S(1)}, u32[]{:S(2)}, u32[]{:S(2)}) collective-permute-start(bf16[256,128]{1,0:T(8,128)(2,1)S(1)} %get-tuple-element.20), channel_id=1, source_target_pairs={{0,8},{8,0},{1,9},{9,1},{2,10},{10,2},{3,11},{11,3},{4,12},{12,4},... | collective-permute-start | bytes 196616 | tf_op jit(solution)/shard_map/ppermute | solution.py:211
  41.0 8.3 %collective-permute-start.4 = (bf16[256,128]{1,0:T(8,128)(2,1)S(1)}, bf16[256,128]{1,0:T(8,128)(2,1)S(1)}, u32[]{:S(2)}, u32[]{:S(2)}) collective-permute-start(bf16[256,128]{1,0:T(8,128)(2,1)S(1)} %get-tuple-element.22), channel_id=1, source_target_pairs={{0,504},{8,16},{16,8},{24,32},{32,24},{40,48},{48,40},{56,64},{64,... | collective-permute-start | bytes 196616 | tf_op jit(solution)/shard_map/ppermute | solution.py:210
  42.9 7.3 %collective-permute-start.5 = (bf16[256,128]{1,0:T(8,128)(2,1)S(1)}, bf16[256,128]{1,0:T(8,128)(2,1)S(1)}, u32[]{:S(2)}, u32[]{:S(2)}) collective-permute-start(bf16[256,128]{1,0:T(8,128)(2,1)S(1)} %get-tuple-element.23), channel_id=1, source_target_pairs={{0,8},{8,0},{1,9},{9,1},{2,10},{10,2},{3,11},{11,3},{4,12},{12,4},... | collective-permute-start | bytes 196616 | tf_op jit(solution)/shard_map/ppermute | solution.py:211
  51.7 22.6 %all-to-all-start.1 = ((bf16[4,1024,128]{2,1,0:T(8,128)(2,1)}), bf16[4,1024,128]{2,1,0:T(8,128)(2,1)}, u32[]{:S(2)}, u32[]{:S(2)}) async-start(bf16[4,1024,128]{2,1,0:T(8,128)(2,1)} %get-tuple-element.24), calls=%async_computation.1 | async-start | bytes 2097152 | tf_op jit(solution)/shard_map/all_to_all | solution.py:204
  55.9 10.6 %collective-permute-start.6 = (bf16[256,128]{1,0:T(8,128)(2,1)S(1)}, bf16[256,128]{1,0:T(8,128)(2,1)S(1)}, u32[]{:S(2)}, u32[]{:S(2)}) collective-permute-start(bf16[256,128]{1,0:T(8,128)(2,1)S(1)} %get-tuple-element.26), channel_id=1, source_target_pairs={{0,504},{8,16},{16,8},{24,32},{32,24},{40,48},{48,40},{56,64},{64,... | collective-permute-start | bytes 196616 | tf_op jit(solution)/shard_map/ppermute | solution.py:210
  57.9 8.7 %collective-permute-start.7 = (bf16[256,128]{1,0:T(8,128)(2,1)S(1)}, bf16[256,128]{1,0:T(8,128)(2,1)S(1)}, u32[]{:S(2)}, u32[]{:S(2)}) collective-permute-start(bf16[256,128]{1,0:T(8,128)(2,1)S(1)} %get-tuple-element.27), channel_id=1, source_target_pairs={{0,8},{8,0},{1,9},{9,1},{2,10},{10,2},{3,11},{11,3},{4,12},{12,4},... | collective-permute-start | bytes 196616 | tf_op jit(solution)/shard_map/ppermute | solution.py:211
  64.6 7.0 %collective-permute-start.8 = (bf16[512,128]{1,0:T(8,128)(2,1)S(1)}, bf16[512,128]{1,0:T(8,128)(2,1)S(1)}, u32[]{:S(2)}, u32[]{:S(2)}) collective-permute-start(bf16[512,128]{1,0:T(8,128)(2,1)S(1)} %shard_map.41.inner), channel_id=1, source_target_pairs={{0,1},{1,0},{2,3},{3,2},{4,5},{5,4},{6,7},{7,6},{8,9},{9,8},{10,11... | collective-permute-start | bytes 393224 | tf_op jit(solution)/shard_map/ppermute | solution.py:256
  66.8 7.5 %collective-permute-start.9 = (bf16[512,128]{1,0:T(8,128)(2,1)S(1)}, bf16[512,128]{1,0:T(8,128)(2,1)S(1)}, u32[]{:S(2)}, u32[]{:S(2)}) collective-permute-start(bf16[512,128]{1,0:T(8,128)(2,1)S(1)} %shard_map.42.outer), channel_id=1, source_target_pairs={{0,1},{1,0},{2,3},{3,2},{4,5},{5,4},{6,7},{7,6},{8,9},{9,8},{10,11... | collective-permute-start | bytes 393224 | tf_op jit(solution)/shard_map/ppermute | solution.py:258
  76.0 3.7 %collective-permute-start.10 = (bf16[256,256]{1,0:T(8,128)(2,1)S(1)}, bf16[256,256]{1,0:T(8,128)(2,1)S(1)}, u32[]{:S(2)}, u32[]{:S(2)}) collective-permute-start(bf16[256,256]{1,0:T(8,128)(2,1)S(1)} %get-tuple-element.30), channel_id=1, source_target_pairs={{0,8},{8,0},{1,9},{9,1},{2,10},{10,2},{3,11},{11,3},{4,12},{12,4},... | collective-permute-start | bytes 393224 | tf_op jit(solution)/shard_map/ppermute | solution.py:272
  121.7 6.8 %collective-permute-start.11 = (bf16[8,32,256]{2,1,0:T(8,128)(2,1)S(1)}, bf16[8,32,256]{2,1,0:T(8,128)(2,1)S(1)}, u32[]{:S(2)}, u32[]{:S(2)}) collective-permute-start(bf16[8,32,256]{2,1,0:T(8,128)(2,1)S(1)} %all_to_all.32.gram), channel_id=1, source_target_pairs={{0,8},{8,0},{1,9},{9,1},{2,10},{10,2},{3,11},{11,3},{4,12},{12,4},... | collective-permute-start | bytes 393224 | tf_op jit(solution)/shard_map/ppermute | solution.py:281

commit v5 on v4

--- a/solution.py
+++ b/solution.py
@@ -20,7 +20,8 @@
 
 VMEM = pl.BlockSpec(memory_space=pltpu.VMEM)
 SMEM = pl.BlockSpec(memory_space=pltpu.SMEM)
-HBM = pl.BlockSpec(memory_space=pltpu.MemorySpace.HBM)
+FAR = pltpu.MemorySpace.HBM
+HBM = pl.BlockSpec(memory_space=FAR)
 
 
 def dot(a, b, dims=((1,), (0,))):
@@ -30,7 +31,8 @@
 def call(kernel, outs, args, scratch=(), smem=0, far=None, far_outs=(), last=False):
     far = far or {}
     args = [
-        x if i < smem or i in far else pltpu.with_memory_space_constraint(x, pltpu.VMEM)
+        x if i < smem
+        else pltpu.with_memory_space_constraint(x, FAR if far.get(i, False) else pltpu.VMEM)
         for i, x in enumerate(args)
     ]
     shapes = []
@@ -48,7 +50,15 @@
     )(*args)
 
 
-def combine_kernel(nbr, ham, out):
+def combine_kernel(nbr_far, ham_far, out, nbr, ham, sems):
+    fetches = [
+        pltpu.make_async_copy(nbr_far, nbr, sems.at[0]),
+        pltpu.make_async_copy(ham_far, ham, sems.at[1]),
+    ]
+    for fetch in fetches:
+        fetch.start()
+    for fetch in fetches:
+        fetch.wait()
     blocks, slots = ham.shape[0], ham.shape[1]
     width = ham.shape[3]
     for r in range(blocks):
@@ -129,26 +139,22 @@
         out[i * tile : (i + 1) * tile] = product(ham, r, ext).astype(BF16)
 
 
-def gram_kernel(core, third_far, inner, outer, inner2, outer2, third, give, mine, sems):
-    rows, width = third.shape[1], third.shape[2]
+def fetch_kernel(far, out, sem):
+    fetch = pltpu.make_async_copy(far, out, sem.at[0])
+    fetch.start()
+    fetch.wait()
+
+
+def gram_kernel(side, core, third, inner, outer, inner2, outer2, out):
+    width, half = third.shape[2], third.shape[0] // 2
     edge = outer.shape[0] // 2
-    count = third.shape[0]
-    fetches = [
-        pltpu.make_async_copy(third_far.at[y], third.at[y], sems.at[y]) for y in range(count)
-    ]
-    for fetch in fetches:
-        fetch.start()
+    start = (core[0] if side == 0 else 1 - core[0]) * half
     own = jnp.concatenate([outer[:edge], inner[...], outer[edge:]], axis=0)
     other = jnp.concatenate([outer2[:edge], inner2[...], outer2[edge:]], axis=0)
     right = jnp.concatenate([own, other], axis=1)
-    for fetch in fetches:
-        fetch.wait()
-    half = count // 2
-    c = core[0]
     for y in range(half):
-        here = slice(y * width, (y + 1) * width)
-        give[here] = dot(third[(1 - c) * half + y], right, ((0,), (0,))).astype(BF16)
-        mine[here] = dot(third[c * half + y], right, ((0,), (0,)))
+        block = dot(third[start + y], right, ((0,), (0,)))
+        out[y * width : (y + 1) * width] = block.astype(out.dtype)
 
 
 def join_kernel(mine, received, out):
@@ -211,7 +217,7 @@
     return from_far, lax.ppermute(near, "core", PAIR)
 
 
-def body(hamiltonian, neighbors, orbitals):
+def filtered(hamiltonian, neighbors, orbitals):
     blocks, _, strip, tile = hamiltonian.shape
     rows, width = orbitals.shape
     edge = FACE * tile
@@ -220,7 +226,15 @@
     scalar = core.astype(jnp.int32).reshape(1)
 
     (shares,) = call(
-        combine_kernel, [(nband, blocks, strip, 4 * tile)], (neighbors, hamiltonian), smem=1, far={1: False}
+        combine_kernel,
+        [(nband, blocks, strip, 4 * tile)],
+        (neighbors, hamiltonian),
+        (
+            pltpu.SMEM(neighbors.shape, neighbors.dtype),
+            pltpu.VMEM(hamiltonian.shape, BF16),
+            pltpu.SemaphoreType.DMA((2,)),
+        ),
+        far={0: True, 1: True},
     )
     tiles = gather(shares, BAND)
     received = swap(
@@ -256,20 +270,30 @@
     inner2 = lax.ppermute(inner, "xl", PAIR)
     (outer,) = call(outer_kernel, [(2 * edge, width)], (scalar, tiles, third, *received), (ext,), smem=1)
     outer2 = lax.ppermute(outer, "xl", PAIR)
+    (third_all,) = call(
+        fetch_kernel,
+        [(ny, rows, width)],
+        (third_far,),
+        (pltpu.SemaphoreType.DMA((1,)),),
+        far={0: True},
+    )
 
     rows_all = rows * lax.axis_size(SLAB)
     scale = 1.0 / math.sqrt(float(rows_all) * float(width * nband))
     depth, columns = ny * width // 2, 2 * width
     share = depth // near
-    third_all, give, mine = call(
-        gram_kernel,
-        [(ny, rows, width), (depth, columns), pltpu.VMEM((depth, columns), F32)],
-        (scalar, third_far, inner, outer, inner2, outer2),
-        (pltpu.SemaphoreType.DMA((ny,)),),
-        smem=1,
-        far={1: True},
-    )
-    received = lax.ppermute(give, "core", PAIR)
+
+    def gram_half(side, dtype):
+        (out,) = call(
+            functools.partial(gram_kernel, side),
+            [pltpu.VMEM((depth, columns), dtype)],
+            (scalar, third_all, inner, outer, inner2, outer2),
+            smem=1,
+        )
+        return out
+
+    received = lax.ppermute(gram_half(1, BF16), "core", PAIR)
+    mine = gram_half(0, F32)
     (joined,) = call(join_kernel, [(near, share, columns)], (mine, received))
     (summed,) = call(
         functools.partial(sum_kernel, None), [(far, share, columns)], (gather(joined, NEAR),)
@@ -299,4 +323,4 @@
     )
     in_specs = (P(SLAB, None, BAND, None), P(SLAB, None), P(SLAB, BAND))
     out_specs = P(SLAB + BAND, None)
-    return jax.shard_map(body, mesh=fine, in_specs=in_specs, out_specs=out_specs, check_vma=False)
+    return jax.shard_map(filtered, mesh=fine, in_specs=in_specs, out_specs=out_specs, check_vma=False)

time: 144 us -> 142 us (0.986)
  waiting for transfers between devices: 8.74 us -> 6.14 us
    ppermute x4, waiting for transfers between devices: 6.03 us -> 2.92 us  [the longest x1 1.34 us: filtered(): outer2 = lax.ppermute(outer, 'xl', PAIR)]
    pallas_call x12 -> x14, Pallas kernels: 8.21 us -> 8.45 us  [call(): pl.pallas_call(kernel, out_shape=shapes, in_specs=[SMEM if i < smem else...]
  transfers between devices with their start and end apart: 14 -> 14, of which waited for: 7 -> 7; matrix products, arithmetic and copies ran while one was open for 0% -> 0% of each run, Pallas kernels for 0% -> 2%
where the time goes in v5:
time: 142 us; the launch traced here: 141 us
  starting transfers between devices  70 us (49%)
  blocking collectives  55.4 us (39%)
  Pallas kernels  8.45 us (6%)
  waiting for transfers between devices  6.14 us (4%)
    all_to_all x4, blocking collectives, gather(): return lax.all_to_all(copies, axes, 0, 0, tiled=True)  55.4 us
    ppermute x4, starting transfers between devices, swap(): return (from_far, lax.ppermute(near, 'core', PAIR))  32.5 us
    ppermute x4, starting transfers between devices, swap(): from_far = lax.ppermute(far, SLAB, pairs)  14.1 us
    all_to_all x2, starting transfers between devices, gather(): return lax.all_to_all(copies, axes, 0, 0, tiled=True)  9.61 us
    pallas_call x14, Pallas kernels, call(): pl.pallas_call(kernel, out_shape=shapes, in_specs=[SMEM if i < smem else...  8.45 us
    ppermute x1, starting transfers between devices, filtered(): gram2 = lax.ppermute(gram, 'core', PAIR)  5.81 us
    ppermute x1, starting transfers between devices, filtered(): outer2 = lax.ppermute(outer, 'xl', PAIR)  3.36 us
  transfers between devices with their start and end apart: 14, of which 7 were waited for; matrix products, arithmetic and copies ran while one was open for 0% of the time, Pallas kernels for 2%

profile of v5, /device:TPU:1, one launch (start us, length us, event | category | flops | bytes accessed | tf_op | source)
XLA Modules:
  0.0 141.2 jit_solution(15138892834322440370)
XLA Ops:
  0.0 2.2 %shard_map.37 = bf16[8,8,16,512]{3,2,1,0:T(8,128)(2,1)} custom-call(s32[8,7]{1,0:T(8,128)} %nbr_far.1, bf16[8,7,16,128]{3,2,1,0:T(8,128)(2,1)} %ham_far.1), custom_call_target="tpu_custom_call" | custom-call | tf_op jit(solution)/shard_map/pallas_call | solution.py:42
  2.2 0.0 copy-start
  2.2 6.1 %all-to-all-start = ((bf16[8,8,16,512]{3,2,1,0:T(8,128)(2,1)}), bf16[8,8,16,512]{3,2,1,0:T(8,128)(2,1)S(1)}, u32[]{:S(2)}, u32[]{:S(2)}) async-start(bf16[8,8,16,512]{3,2,1,0:T(8,128)(2,1)} %shard_map.37), calls=%async_computation | async-start | bytes 2097152 | tf_op jit(solution)/shard_map/all_to_all | solution.py:210
  8.3 0.0 copy-done
  8.3 5.2 %collective-permute-start = (bf16[256,128]{1,0:T(8,128)(2,1)S(1)}, bf16[256,128]{1,0:T(8,128)(2,1)S(1)}, u32[]{:S(2)}, u32[]{:S(2)}) collective-permute-start(bf16[256,128]{1,0:T(8,128)(2,1)S(1)} %get-tuple-element.26), channel_id=1, source_target_pairs={{0,504},{8,16},{16,8},{24,32},{32,24},{40,48},{48,40},{56,64},{64,... | collective-permute-start | bytes 196616 | tf_op jit(solution)/shard_map/ppermute | solution.py:216
  13.5 10.4 %collective-permute-start.1 = (bf16[256,128]{1,0:T(8,128)(2,1)S(1)}, bf16[256,128]{1,0:T(8,128)(2,1)S(1)}, u32[]{:S(2)}, u32[]{:S(2)}) collective-permute-start(bf16[256,128]{1,0:T(8,128)(2,1)S(1)} %get-tuple-element.25), channel_id=1, source_target_pairs={{0,8},{8,0},{1,9},{9,1},{2,10},{10,2},{3,11},{11,3},{4,12},{12,4},... | collective-permute-start | bytes 196616 | tf_op jit(solution)/shard_map/ppermute | solution.py:217
  23.9 0.9 collective-permute-done.from_far
  24.9 0.0 collective-permute-done.1.from_near
  24.9 0.0 all-to-all-done.ham
  24.9 0.5 shard_map.38
  25.4 5.0 %collective-permute-start.2 = (bf16[256,128]{1,0:T(8,128)(2,1)S(1)}, bf16[256,128]{1,0:T(8,128)(2,1)S(1)}, u32[]{:S(2)}, u32[]{:S(2)}) collective-permute-start(bf16[256,128]{1,0:T(8,128)(2,1)S(1)} %get-tuple-element.16), channel_id=1, source_target_pairs={{0,504},{8,16},{16,8},{24,32},{32,24},{40,48},{48,40},{56,64},{64,... | collective-permute-start | bytes 196616 | tf_op jit(solution)/shard_map/ppermute | solution.py:216
  30.4 9.3 %collective-permute-start.3 = (bf16[256,128]{1,0:T(8,128)(2,1)S(1)}, bf16[256,128]{1,0:T(8,128)(2,1)S(1)}, u32[]{:S(2)}, u32[]{:S(2)}) collective-permute-start(bf16[256,128]{1,0:T(8,128)(2,1)S(1)} %get-tuple-element.17), channel_id=1, source_target_pairs={{0,8},{8,0},{1,9},{9,1},{2,10},{10,2},{3,11},{11,3},{4,12},{12,4},... | collective-permute-start | bytes 196616 | tf_op jit(solution)/shard_map/ppermute | solution.py:217
  39.7 0.0 collective-permute-done.2.from_far
  39.7 0.9 collective-permute-done.3.from_near
  40.5 0.5 shard_map.39
  41.0 1.9 %collective-permute-start.4 = (bf16[256,128]{1,0:T(8,128)(2,1)S(1)}, bf16[256,128]{1,0:T(8,128)(2,1)S(1)}, u32[]{:S(2)}, u32[]{:S(2)}) collective-permute-start(bf16[256,128]{1,0:T(8,128)(2,1)S(1)} %get-tuple-element.19), channel_id=1, source_target_pairs={{0,504},{8,16},{16,8},{24,32},{32,24},{40,48},{48,40},{56,64},{64,... | collective-permute-start | bytes 196616 | tf_op jit(solution)/shard_map/ppermute | solution.py:216
  42.9 6.4 %collective-permute-start.5 = (bf16[256,128]{1,0:T(8,128)(2,1)S(1)}, bf16[256,128]{1,0:T(8,128)(2,1)S(1)}, u32[]{:S(2)}, u32[]{:S(2)}) collective-permute-start(bf16[256,128]{1,0:T(8,128)(2,1)S(1)} %get-tuple-element.20), channel_id=1, source_target_pairs={{0,8},{8,0},{1,9},{9,1},{2,10},{10,2},{3,11},{11,3},{4,12},{12,4},... | collective-permute-start | bytes 196616 | tf_op jit(solution)/shard_map/ppermute | solution.py:217
  49.3 0.0 collective-permute-done.4.from_far
  49.4 0.9 collective-permute-done.5.from_near
  50.2 1.5 %shard_map.40 = (bf16[1024,128]{1,0:T(8,128)(2,1)S(1)}, bf16[4,1024,128]{2,1,0:T(8,128)(2,1)}, bf16[256,128]{1,0:T(8,128)(2,1)S(1)}, bf16[256,128]{1,0:T(8,128)(2,1)S(1)}) custom-call(s32[1]{0:T(128)} %bitcast.core, bf16[8,8,16,512]{3,2,1,0:T(8,128)(2,1)S(1)} %all-to-all-done.ham, bf16[1024,128]{1,0:T(8,128)(2,1)S(1)} %get-tuple-element.18.vec, ...), custom_call_target="tpu_custom_call" | custom-call | tf_op jit(solution)/shard_map/pallas_call | solution.py:42
  51.7 3.5 %all-to-all-start.1 = ((bf16[4,1024,128]{2,1,0:T(8,128)(2,1)}), bf16[4,1024,128]{2,1,0:T(8,128)(2,1)S(1)}, u32[]{:S(2)}, u32[]{:S(2)}) async-start(bf16[4,1024,128]{2,1,0:T(8,128)(2,1)} %get-tuple-element.21), calls=%async_computation.1 | async-start | bytes 2097152 | tf_op jit(solution)/shard_map/all_to_all | solution.py:210
  55.2 1.9 %collective-permute-start.6 = (bf16[256,128]{1,0:T(8,128)(2,1)S(1)}, bf16[256,128]{1,0:T(8,128)(2,1)S(1)}, u32[]{:S(2)}, u32[]{:S(2)}) collective-permute-start(bf16[256,128]{1,0:T(8,128)(2,1)S(1)} %get-tuple-element.23), channel_id=1, source_target_pairs={{0,504},{8,16},{16,8},{24,32},{32,24},{40,48},{48,40},{56,64},{64,... | collective-permute-start | bytes 196616 | tf_op jit(solution)/shard_map/ppermute | solution.py:216
  57.2 6.4 %collective-permute-start.7 = (bf16[256,128]{1,0:T(8,128)(2,1)S(1)}, bf16[256,128]{1,0:T(8,128)(2,1)S(1)}, u32[]{:S(2)}, u32[]{:S(2)}) collective-permute-start(bf16[256,128]{1,0:T(8,128)(2,1)S(1)} %get-tuple-element.24), channel_id=1, source_target_pairs={{0,8},{8,0},{1,9},{9,1},{2,10},{10,2},{3,11},{11,3},{4,12},{12,4},... | collective-permute-start | bytes 196616 | tf_op jit(solution)/shard_map/ppermute | solution.py:217
  63.6 0.3 shard_map.42.inner
  63.9 1.9 %collective-permute-start.8 = (bf16[512,128]{1,0:T(8,128)(2,1)S(1)}, bf16[512,128]{1,0:T(8,128)(2,1)S(1)}, u32[]{:S(2)}, u32[]{:S(2)}) collective-permute-start(bf16[512,128]{1,0:T(8,128)(2,1)S(1)} %shard_map.42.inner), channel_id=1, source_target_pairs={{0,1},{1,0},{2,3},{3,2},{4,5},{5,4},{6,7},{7,6},{8,9},{9,8},{10,11... | collective-permute-start | bytes 393224 | tf_op jit(solution)/shard_map/ppermute | solution.py:270
  65.8 0.0 collective-permute-done.6.from_far
  65.8 0.0 collective-permute-done.7.from_near
  65.8 0.3 shard_map.43.outer
  66.2 3.4 %collective-permute-start.9 = (bf16[512,128]{1,0:T(8,128)(2,1)S(1)}, bf16[512,128]{1,0:T(8,128)(2,1)S(1)}, u32[]{:S(2)}, u32[]{:S(2)}) collective-permute-start(bf16[512,128]{1,0:T(8,128)(2,1)S(1)} %shard_map.43.outer), channel_id=1, source_target_pairs={{0,1},{1,0},{2,3},{3,2},{4,5},{5,4},{6,7},{7,6},{8,9},{9,8},{10,11... | collective-permute-start | bytes 393224 | tf_op jit(solution)/shard_map/ppermute | solution.py:272
  69.5 0.5 all-to-all-done.1.far
  70.0 0.0 copy-start.1
  70.1 1.0 copy-done.1
  71.0 1.2 shard_map.41.third
  72.3 0.0 collective-permute-done.8.inner2
  72.3 1.3 collective-permute-done.9.outer2
  73.6 0.3 shard_map.45
  74.0 2.8 %collective-permute-start.10 = (bf16[256,256]{1,0:T(8,128)(2,1)S(1)}, bf16[256,256]{1,0:T(8,128)(2,1)S(1)}, u32[]{:S(2)}, u32[]{:S(2)}) collective-permute-start(bf16[256,256]{1,0:T(8,128)(2,1)S(1)} %shard_map.45), channel_id=1, source_target_pairs={{0,8},{8,0},{1,9},{9,1},{2,10},{10,2},{3,11},{11,3},{4,12},{12,4},... | collective-permute-start | bytes 393224 | tf_op jit(solution)/shard_map/ppermute | solution.py:295
  76.8 0.3 shard_map.44.mine
  77.1 0.6 collective-permute-done.10.received
  77.8 10.2 %all_to_all.30.parts = bf16[8,32,256]{2,1,0:T(8,128)(2,1)S(1)} all-to-all(bf16[8,32,256]{2,1,0:T(8,128)(2,1)S(1)} %shard_map.46), channel_id=1, replica_groups=mesh['z2'=4,'z1'=4,'xh'=2,'core'=2,'y'=4,'xl'=2] {'z1','xh'}, dimensions={0} | all-to-all | bytes 262144 | tf_op jit(solution)/shard_map/all_to_all | solution.py:210
  87.9 20.9 %all_to_all.31.parts = bf16[4,32,256]{2,1,0:T(8,128)(2,1)S(1)} all-to-all(bf16[4,32,256]{2,1,0:T(8,128)(2,1)S(1)} %shard_map.47), channel_id=1, replica_groups=mesh['z2'=4,'z1'=4,'xh'=2,'core'=2,'y'=4,'xl'=2] {'z2'}, dimensions={0} | all-to-all | bytes 131072 | tf_op jit(solution)/shard_map/all_to_all | solution.py:210
  108.8 10.8 %all_to_all.32.gram = bf16[8,32,256]{2,1,0:T(8,128)(2,1)S(1)} all-to-all(bf16[8,32,256]{2,1,0:T(8,128)(2,1)S(1)} %shard_map.48), channel_id=1, replica_groups=mesh['z2'=4,'z1'=4,'xh'=2,'core'=2,'y'=4,'xl'=2] {'z1','xh'}, dimensions={0} | all-to-all | bytes 262144 | tf_op jit(solution)/shard_map/all_to_all | solution.py:210
  119.6 5.8 %collective-permute-start.11 = (bf16[8,32,256]{2,1,0:T(8,128)(2,1)S(1)}, bf16[8,32,256]{2,1,0:T(8,128)(2,1)S(1)}, u32[]{:S(2)}, u32[]{:S(2)}) collective-permute-start(bf16[8,32,256]{2,1,0:T(8,128)(2,1)S(1)} %all_to_all.32.gram), channel_id=1, source_target_pairs={{0,8},{8,0},{1,9},{9,1},{2,10},{10,2},{3,11},{11,3},{4,12},{12,4},... | collective-permute-start | bytes 393224 | tf_op jit(solution)/shard_map/ppermute | solution.py:305
  125.5 1.0 collective-permute-done.11.gram2
  126.4 0.5 shard_map.49
  126.9 13.5 %all_to_all.33.parts = bf16[8,128,256]{2,1,0:T(8,128)(2,1)S(1)} all-to-all(bf16[8,128,256]{2,1,0:T(8,128)(2,1)S(1)} %shard_map.49), channel_id=1, replica_groups=mesh['z2'=4,'z1'=4,'xh'=2,'core'=2,'y'=4,'xl'=2] {'y','xl'}, dimensions={0} | all-to-all | bytes 1048576 | tf_op jit(solution)/shard_map/all_to_all | solution.py:210
  140.4 0.8 shard_map.50
  (4 shorter events, 0.1 us)
Async XLA Ops:
  2.2 6.1 %copy-start = (bf16[1024,128]{1,0:T(8,128)(2,1)S(1)}, bf16[1024,128]{1,0:T(8,128)(2,1)}, u32[]{:S(2)}) copy-start(bf16[1024,128]{1,0:T(8,128)(2,1)} %rest_0_.1) | copy-start | bytes 786436
  2.2 22.7 %all-to-all-start = ((bf16[8,8,16,512]{3,2,1,0:T(8,128)(2,1)}), bf16[8,8,16,512]{3,2,1,0:T(8,128)(2,1)S(1)}, u32[]{:S(2)}, u32[]{:S(2)}) async-start(bf16[8,8,16,512]{3,2,1,0:T(8,128)(2,1)} %shard_map.37), calls=%async_computation | async-start | bytes 2097152 | tf_op jit(solution)/shard_map/all_to_all | solution.py:210
  8.3 16.6 %collective-permute-start = (bf16[256,128]{1,0:T(8,128)(2,1)S(1)}, bf16[256,128]{1,0:T(8,128)(2,1)S(1)}, u32[]{:S(2)}, u32[]{:S(2)}) collective-permute-start(bf16[256,128]{1,0:T(8,128)(2,1)S(1)} %get-tuple-element.26), channel_id=1, source_target_pairs={{0,504},{8,16},{16,8},{24,32},{32,24},{40,48},{48,40},{56,64},{64,... | collective-permute-start | bytes 196616 | tf_op jit(solution)/shard_map/ppermute | solution.py:216
  13.5 11.3 %collective-permute-start.1 = (bf16[256,128]{1,0:T(8,128)(2,1)S(1)}, bf16[256,128]{1,0:T(8,128)(2,1)S(1)}, u32[]{:S(2)}, u32[]{:S(2)}) collective-permute-start(bf16[256,128]{1,0:T(8,128)(2,1)S(1)} %get-tuple-element.25), channel_id=1, source_target_pairs={{0,8},{8,0},{1,9},{9,1},{2,10},{10,2},{3,11},{11,3},{4,12},{12,4},... | collective-permute-start | bytes 196616 | tf_op jit(solution)/shard_map/ppermute | solution.py:217
  25.4 14.3 %collective-permute-start.2 = (bf16[256,128]{1,0:T(8,128)(2,1)S(1)}, bf16[256,128]{1,0:T(8,128)(2,1)S(1)}, u32[]{:S(2)}, u32[]{:S(2)}) collective-permute-start(bf16[256,128]{1,0:T(8,128)(2,1)S(1)} %get-tuple-element.16), channel_id=1, source_target_pairs={{0,504},{8,16},{16,8},{24,32},{32,24},{40,48},{48,40},{56,64},{64,... | collective-permute-start | bytes 196616 | tf_op jit(solution)/shard_map/ppermute | solution.py:216
  30.4 10.2 %collective-permute-start.3 = (bf16[256,128]{1,0:T(8,128)(2,1)S(1)}, bf16[256,128]{1,0:T(8,128)(2,1)S(1)}, u32[]{:S(2)}, u32[]{:S(2)}) collective-permute-start(bf16[256,128]{1,0:T(8,128)(2,1)S(1)} %get-tuple-element.17), channel_id=1, source_target_pairs={{0,8},{8,0},{1,9},{9,1},{2,10},{10,2},{3,11},{11,3},{4,12},{12,4},... | collective-permute-start | bytes 196616 | tf_op jit(solution)/shard_map/ppermute | solution.py:217
  41.0 8.3 %collective-permute-start.4 = (bf16[256,128]{1,0:T(8,128)(2,1)S(1)}, bf16[256,128]{1,0:T(8,128)(2,1)S(1)}, u32[]{:S(2)}, u32[]{:S(2)}) collective-permute-start(bf16[256,128]{1,0:T(8,128)(2,1)S(1)} %get-tuple-element.19), channel_id=1, source_target_pairs={{0,504},{8,16},{16,8},{24,32},{32,24},{40,48},{48,40},{56,64},{64,... | collective-permute-start | bytes 196616 | tf_op jit(solution)/shard_map/ppermute | solution.py:216
  42.9 7.3 %collective-permute-start.5 = (bf16[256,128]{1,0:T(8,128)(2,1)S(1)}, bf16[256,128]{1,0:T(8,128)(2,1)S(1)}, u32[]{:S(2)}, u32[]{:S(2)}) collective-permute-start(bf16[256,128]{1,0:T(8,128)(2,1)S(1)} %get-tuple-element.20), channel_id=1, source_target_pairs={{0,8},{8,0},{1,9},{9,1},{2,10},{10,2},{3,11},{11,3},{4,12},{12,4},... | collective-permute-start | bytes 196616 | tf_op jit(solution)/shard_map/ppermute | solution.py:217
  51.7 18.3 %all-to-all-start.1 = ((bf16[4,1024,128]{2,1,0:T(8,128)(2,1)}), bf16[4,1024,128]{2,1,0:T(8,128)(2,1)S(1)}, u32[]{:S(2)}, u32[]{:S(2)}) async-start(bf16[4,1024,128]{2,1,0:T(8,128)(2,1)} %get-tuple-element.21), calls=%async_computation.1 | async-start | bytes 2097152 | tf_op jit(solution)/shard_map/all_to_all | solution.py:210
  55.2 10.6 %collective-permute-start.6 = (bf16[256,128]{1,0:T(8,128)(2,1)S(1)}, bf16[256,128]{1,0:T(8,128)(2,1)S(1)}, u32[]{:S(2)}, u32[]{:S(2)}) collective-permute-start(bf16[256,128]{1,0:T(8,128)(2,1)S(1)} %get-tuple-element.23), channel_id=1, source_target_pairs={{0,504},{8,16},{16,8},{24,32},{32,24},{40,48},{48,40},{56,64},{64,... | collective-permute-start | bytes 196616 | tf_op jit(solution)/shard_map/ppermute | solution.py:216
  57.2 8.6 %collective-permute-start.7 = (bf16[256,128]{1,0:T(8,128)(2,1)S(1)}, bf16[256,128]{1,0:T(8,128)(2,1)S(1)}, u32[]{:S(2)}, u32[]{:S(2)}) collective-permute-start(bf16[256,128]{1,0:T(8,128)(2,1)S(1)} %get-tuple-element.24), channel_id=1, source_target_pairs={{0,8},{8,0},{1,9},{9,1},{2,10},{10,2},{3,11},{11,3},{4,12},{12,4},... | collective-permute-start | bytes 196616 | tf_op jit(solution)/shard_map/ppermute | solution.py:217
  63.9 8.4 %collective-permute-start.8 = (bf16[512,128]{1,0:T(8,128)(2,1)S(1)}, bf16[512,128]{1,0:T(8,128)(2,1)S(1)}, u32[]{:S(2)}, u32[]{:S(2)}) collective-permute-start(bf16[512,128]{1,0:T(8,128)(2,1)S(1)} %shard_map.42.inner), channel_id=1, source_target_pairs={{0,1},{1,0},{2,3},{3,2},{4,5},{5,4},{6,7},{7,6},{8,9},{9,8},{10,11... | collective-permute-start | bytes 393224 | tf_op jit(solution)/shard_map/ppermute | solution.py:270
  66.2 7.5 %collective-permute-start.9 = (bf16[512,128]{1,0:T(8,128)(2,1)S(1)}, bf16[512,128]{1,0:T(8,128)(2,1)S(1)}, u32[]{:S(2)}, u32[]{:S(2)}) collective-permute-start(bf16[512,128]{1,0:T(8,128)(2,1)S(1)} %shard_map.43.outer), channel_id=1, source_target_pairs={{0,1},{1,0},{2,3},{3,2},{4,5},{5,4},{6,7},{7,6},{8,9},{9,8},{10,11... | collective-permute-start | bytes 393224 | tf_op jit(solution)/shard_map/ppermute | solution.py:272
  70.0 1.0 copy-start.1
  74.0 3.8 %collective-permute-start.10 = (bf16[256,256]{1,0:T(8,128)(2,1)S(1)}, bf16[256,256]{1,0:T(8,128)(2,1)S(1)}, u32[]{:S(2)}, u32[]{:S(2)}) collective-permute-start(bf16[256,256]{1,0:T(8,128)(2,1)S(1)} %shard_map.45), channel_id=1, source_target_pairs={{0,8},{8,0},{1,9},{9,1},{2,10},{10,2},{3,11},{11,3},{4,12},{12,4},... | collective-permute-start | bytes 393224 | tf_op jit(solution)/shard_map/ppermute | solution.py:295
  119.6 6.8 %collective-permute-start.11 = (bf16[8,32,256]{2,1,0:T(8,128)(2,1)S(1)}, bf16[8,32,256]{2,1,0:T(8,128)(2,1)S(1)}, u32[]{:S(2)}, u32[]{:S(2)}) collective-permute-start(bf16[8,32,256]{2,1,0:T(8,128)(2,1)S(1)} %all_to_all.32.gram), channel_id=1, source_target_pairs={{0,8},{8,0},{1,9},{9,1},{2,10},{10,2},{3,11},{11,3},{4,12},{12,4},... | collective-permute-start | bytes 393224 | tf_op jit(solution)/shard_map/ppermute | solution.py:305

commit v6 on v5

--- a/solution.py
+++ b/solution.py
@@ -12,7 +12,7 @@
 
 SLAB = ("z2", "z1", "xh", "core")
 BAND = ("y", "xl")
-NEAR = ("z1", "xh")
+NEAR = ("z1", "xh", "core")
 PAIR = [(0, 1), (1, 0)]
 FACE = 2
 F32 = jnp.float32
@@ -145,23 +145,17 @@
     fetch.wait()
 
 
-def gram_kernel(side, core, third, inner, outer, inner2, outer2, out):
-    width, half = third.shape[2], third.shape[0] // 2
+def gram_kernel(third, inner, outer, inner2, outer2, out):
+    share, width = out.shape[1], third.shape[2]
+    per = width // share
     edge = outer.shape[0] // 2
-    start = (core[0] if side == 0 else 1 - core[0]) * half
     own = jnp.concatenate([outer[:edge], inner[...], outer[edge:]], axis=0)
     other = jnp.concatenate([outer2[:edge], inner2[...], outer2[edge:]], axis=0)
     right = jnp.concatenate([own, other], axis=1)
-    for y in range(half):
-        block = dot(third[start + y], right, ((0,), (0,)))
-        out[y * width : (y + 1) * width] = block.astype(out.dtype)
-
-
-def join_kernel(mine, received, out):
-    share = out.shape[1]
-    total = (mine[...] + received[...].astype(F32)).astype(BF16)
-    for i in range(out.shape[0]):
-        out[i] = total[i * share : (i + 1) * share]
+    for y in range(third.shape[0]):
+        block = dot(third[y], right, ((0,), (0,))).astype(BF16)
+        for i in range(per):
+            out[y * per + i] = block[i * share : (i + 1) * share]
 
 
 def sum_kernel(scale, parts, out):
@@ -175,18 +169,14 @@
         out[copy] = total
 
 
-def mixed_kernel(core, third, gram, gram2, inner, outer, out):
+def mixed_kernel(third, gram, inner, outer, out):
     strips, height, width = out.shape[0], out.shape[1], third.shape[2]
-    half = third.shape[0] // 2
+    count = third.shape[0]
     edge = outer.shape[0] // (2 * height)
-    c = core[0]
-    weights = jnp.concatenate(
-        [g[...].reshape(half * width, g.shape[2]) for g in (gram, gram2)], axis=0
-    )
+    weights = gram[...].reshape(count * width, gram.shape[2])
     for s in range(strips):
         here = slice(s * height, (s + 1) * height)
-        order = [c * half + y for y in range(half)] + [(1 - c) * half + y for y in range(half)]
-        left = jnp.concatenate([third[y, here] for y in order], axis=1)
+        left = jnp.concatenate([third[y, here] for y in range(count)], axis=1)
         value = dot(left, weights)
         if s < edge:
             applied = outer[here]
@@ -280,34 +270,22 @@
 
     rows_all = rows * lax.axis_size(SLAB)
     scale = 1.0 / math.sqrt(float(rows_all) * float(width * nband))
-    depth, columns = ny * width // 2, 2 * width
-    share = depth // near
-
-    def gram_half(side, dtype):
-        (out,) = call(
-            functools.partial(gram_kernel, side),
-            [pltpu.VMEM((depth, columns), dtype)],
-            (scalar, third_all, inner, outer, inner2, outer2),
-            smem=1,
-        )
-        return out
-
-    received = lax.ppermute(gram_half(1, BF16), "core", PAIR)
-    mine = gram_half(0, F32)
-    (joined,) = call(join_kernel, [(near, share, columns)], (mine, received))
+    columns = 2 * width
+    share = ny * width // near
+    (partial_gram,) = call(
+        gram_kernel, [(near, share, columns)], (third_all, inner, outer, inner2, outer2)
+    )
     (summed,) = call(
-        functools.partial(sum_kernel, None), [(far, share, columns)], (gather(joined, NEAR),)
+        functools.partial(sum_kernel, None), [(far, share, columns)], (gather(partial_gram, NEAR),)
     )
     (scaled,) = call(
         functools.partial(sum_kernel, scale), [(near, share, columns)], (gather(summed, "z2"),)
     )
     gram = gather(scaled, NEAR)
-    gram2 = lax.ppermute(gram, "core", PAIR)
     (partial_out,) = call(
         mixed_kernel,
         [(nband, rows // nband, columns)],
-        (scalar, third_all, gram, gram2, inner, outer),
-        smem=1,
+        (third_all, gram, inner, outer),
     )
     (out,) = call(
         final_kernel, [(rows // nband, nband * width)], (gather(partial_out, BAND),), last=True

time: 142 us -> 142 us (level)
  blocking collectives: 55.4 us -> 64.9 us
  starting transfers between devices: 70 us -> 62.1 us
    all_to_all x4, blocking collectives: 55.4 us -> 64.9 us  [gather(): return lax.all_to_all(copies, axes, 0, 0, tiled=True)]
    ppermute x2 -> x0, starting transfers between devices: 8.59 us -> none  [the longest x1 5.81 us: filtered(): gram2 = lax.ppermute(gram, 'core', PAIR)]
    ppermute x2 -> x0, waiting for transfers between devices: 1.58 us -> none  [the longest x1 0.96 us: filtered(): gram2 = lax.ppermute(gram, 'core', PAIR)]
    pallas_call x14 -> x12, Pallas kernels: 8.45 us -> 8.23 us  [call(): pl.pallas_call(kernel, out_shape=shapes, in_specs=[SMEM if i < smem else...]
  transfers between devices with their start and end apart: 14 -> 12, of which waited for: 7 -> 5; matrix products, arithmetic and copies ran while one was open for 0% -> 0% of each run, Pallas kernels for 2% -> 1%
where the time goes in v6:
time: 142 us; the launch traced here: 141 us
  blocking collectives  64.9 us (46%)
  starting transfers between devices  62.1 us (44%)
  Pallas kernels  8.23 us (6%)
  waiting for transfers between devices  5.55 us (4%)
    all_to_all x4, blocking collectives, gather(): return lax.all_to_all(copies, axes, 0, 0, tiled=True)  64.9 us
    ppermute x4, starting transfers between devices, swap(): return (from_far, lax.ppermute(near, 'core', PAIR))  32.5 us
    ppermute x4, starting transfers between devices, swap(): from_far = lax.ppermute(far, SLAB, pairs)  14 us
    all_to_all x2, starting transfers between devices, gather(): return lax.all_to_all(copies, axes, 0, 0, tiled=True)  10.3 us
    pallas_call x12, Pallas kernels, call(): pl.pallas_call(kernel, out_shape=shapes, in_specs=[SMEM if i < smem else...  8.23 us
    ppermute x1, starting transfers between devices, filtered(): outer2 = lax.ppermute(outer, 'xl', PAIR)  3.36 us
  transfers between devices with their start and end apart: 12, of which 5 were waited for; matrix products, arithmetic and copies ran while one was open for 0% of the time, Pallas kernels for 1%

profile of v6, /device:TPU:1, one launch (start us, length us, event | category | flops | bytes accessed | tf_op | source)
XLA Modules:
  0.0 141.0 jit_solution(7205266949808221685)
XLA Ops:
  0.0 2.2 %shard_map.37 = bf16[8,8,16,512]{3,2,1,0:T(8,128)(2,1)} custom-call(s32[8,7]{1,0:T(8,128)} %nbr_far.1, bf16[8,7,16,128]{3,2,1,0:T(8,128)(2,1)} %ham_far.1), custom_call_target="tpu_custom_call" | custom-call | tf_op jit(solution)/shard_map/pallas_call | solution.py:42
  2.2 0.0 copy-start
  2.2 6.1 %all-to-all-start = ((bf16[8,8,16,512]{3,2,1,0:T(8,128)(2,1)}), bf16[8,8,16,512]{3,2,1,0:T(8,128)(2,1)S(1)}, u32[]{:S(2)}, u32[]{:S(2)}) async-start(bf16[8,8,16,512]{3,2,1,0:T(8,128)(2,1)} %shard_map.37), calls=%async_computation | async-start | bytes 2097152 | tf_op jit(solution)/shard_map/all_to_all | solution.py:200
  8.3 0.0 copy-done
  8.3 5.2 %collective-permute-start = (bf16[256,128]{1,0:T(8,128)(2,1)S(1)}, bf16[256,128]{1,0:T(8,128)(2,1)S(1)}, u32[]{:S(2)}, u32[]{:S(2)}) collective-permute-start(bf16[256,128]{1,0:T(8,128)(2,1)S(1)} %get-tuple-element.26), channel_id=1, source_target_pairs={{0,504},{8,16},{16,8},{24,32},{32,24},{40,48},{48,40},{56,64},{64,... | collective-permute-start | bytes 196616 | tf_op jit(solution)/shard_map/ppermute | solution.py:206
  13.5 10.4 %collective-permute-start.1 = (bf16[256,128]{1,0:T(8,128)(2,1)S(1)}, bf16[256,128]{1,0:T(8,128)(2,1)S(1)}, u32[]{:S(2)}, u32[]{:S(2)}) collective-permute-start(bf16[256,128]{1,0:T(8,128)(2,1)S(1)} %get-tuple-element.25), channel_id=1, source_target_pairs={{0,8},{8,0},{1,9},{9,1},{2,10},{10,2},{3,11},{11,3},{4,12},{12,4},... | collective-permute-start | bytes 196616 | tf_op jit(solution)/shard_map/ppermute | solution.py:207
  23.9 0.9 collective-permute-done.from_far
  24.9 0.0 collective-permute-done.1.from_near
  24.9 0.0 all-to-all-done.ham
  24.9 0.5 shard_map.38
  25.4 5.0 %collective-permute-start.2 = (bf16[256,128]{1,0:T(8,128)(2,1)S(1)}, bf16[256,128]{1,0:T(8,128)(2,1)S(1)}, u32[]{:S(2)}, u32[]{:S(2)}) collective-permute-start(bf16[256,128]{1,0:T(8,128)(2,1)S(1)} %get-tuple-element.16), channel_id=1, source_target_pairs={{0,504},{8,16},{16,8},{24,32},{32,24},{40,48},{48,40},{56,64},{64,... | collective-permute-start | bytes 196616 | tf_op jit(solution)/shard_map/ppermute | solution.py:206
  30.4 9.3 %collective-permute-start.3 = (bf16[256,128]{1,0:T(8,128)(2,1)S(1)}, bf16[256,128]{1,0:T(8,128)(2,1)S(1)}, u32[]{:S(2)}, u32[]{:S(2)}) collective-permute-start(bf16[256,128]{1,0:T(8,128)(2,1)S(1)} %get-tuple-element.17), channel_id=1, source_target_pairs={{0,8},{8,0},{1,9},{9,1},{2,10},{10,2},{3,11},{11,3},{4,12},{12,4},... | collective-permute-start | bytes 196616 | tf_op jit(solution)/shard_map/ppermute | solution.py:207
  39.7 0.0 collective-permute-done.2.from_far
  39.7 0.9 collective-permute-done.3.from_near
  40.5 0.5 shard_map.39
  41.0 1.9 %collective-permute-start.4 = (bf16[256,128]{1,0:T(8,128)(2,1)S(1)}, bf16[256,128]{1,0:T(8,128)(2,1)S(1)}, u32[]{:S(2)}, u32[]{:S(2)}) collective-permute-start(bf16[256,128]{1,0:T(8,128)(2,1)S(1)} %get-tuple-element.19), channel_id=1, source_target_pairs={{0,504},{8,16},{16,8},{24,32},{32,24},{40,48},{48,40},{56,64},{64,... | collective-permute-start | bytes 196616 | tf_op jit(solution)/shard_map/ppermute | solution.py:206
  42.9 6.4 %collective-permute-start.5 = (bf16[256,128]{1,0:T(8,128)(2,1)S(1)}, bf16[256,128]{1,0:T(8,128)(2,1)S(1)}, u32[]{:S(2)}, u32[]{:S(2)}) collective-permute-start(bf16[256,128]{1,0:T(8,128)(2,1)S(1)} %get-tuple-element.20), channel_id=1, source_target_pairs={{0,8},{8,0},{1,9},{9,1},{2,10},{10,2},{3,11},{11,3},{4,12},{12,4},... | collective-permute-start | bytes 196616 | tf_op jit(solution)/shard_map/ppermute | solution.py:207
  49.3 0.0 collective-permute-done.4.from_far
  49.4 0.9 collective-permute-done.5.from_near
  50.2 1.5 %shard_map.40 = (bf16[1024,128]{1,0:T(8,128)(2,1)S(1)}, bf16[4,1024,128]{2,1,0:T(8,128)(2,1)}, bf16[256,128]{1,0:T(8,128)(2,1)S(1)}, bf16[256,128]{1,0:T(8,128)(2,1)S(1)}) custom-call(s32[1]{0:T(128)} %bitcast.core, bf16[8,8,16,512]{3,2,1,0:T(8,128)(2,1)S(1)} %all-to-all-done.ham, bf16[1024,128]{1,0:T(8,128)(2,1)S(1)} %get-tuple-element.18.vec, ...), custom_call_target="tpu_custom_call" | custom-call | tf_op jit(solution)/shard_map/pallas_call | solution.py:42
  51.7 4.3 %all-to-all-start.1 = ((bf16[4,1024,128]{2,1,0:T(8,128)(2,1)}), bf16[4,1024,128]{2,1,0:T(8,128)(2,1)}, u32[]{:S(2)}, u32[]{:S(2)}) async-start(bf16[4,1024,128]{2,1,0:T(8,128)(2,1)} %get-tuple-element.21), calls=%async_computation.1 | async-start | bytes 2097152 | tf_op jit(solution)/shard_map/all_to_all | solution.py:200
  56.0 1.9 %collective-permute-start.6 = (bf16[256,128]{1,0:T(8,128)(2,1)S(1)}, bf16[256,128]{1,0:T(8,128)(2,1)S(1)}, u32[]{:S(2)}, u32[]{:S(2)}) collective-permute-start(bf16[256,128]{1,0:T(8,128)(2,1)S(1)} %get-tuple-element.23), channel_id=1, source_target_pairs={{0,504},{8,16},{16,8},{24,32},{32,24},{40,48},{48,40},{56,64},{64,... | collective-permute-start | bytes 196616 | tf_op jit(solution)/shard_map/ppermute | solution.py:206
  57.9 6.4 %collective-permute-start.7 = (bf16[256,128]{1,0:T(8,128)(2,1)S(1)}, bf16[256,128]{1,0:T(8,128)(2,1)S(1)}, u32[]{:S(2)}, u32[]{:S(2)}) collective-permute-start(bf16[256,128]{1,0:T(8,128)(2,1)S(1)} %get-tuple-element.24), channel_id=1, source_target_pairs={{0,8},{8,0},{1,9},{9,1},{2,10},{10,2},{3,11},{11,3},{4,12},{12,4},... | collective-permute-start | bytes 196616 | tf_op jit(solution)/shard_map/ppermute | solution.py:207
  64.3 0.3 shard_map.42.inner
  64.6 1.9 %collective-permute-start.8 = (bf16[512,128]{1,0:T(8,128)(2,1)S(1)}, bf16[512,128]{1,0:T(8,128)(2,1)S(1)}, u32[]{:S(2)}, u32[]{:S(2)}) collective-permute-start(bf16[512,128]{1,0:T(8,128)(2,1)S(1)} %shard_map.42.inner), channel_id=1, source_target_pairs={{0,1},{1,0},{2,3},{3,2},{4,5},{5,4},{6,7},{7,6},{8,9},{9,8},{10,11... | collective-permute-start | bytes 393224 | tf_op jit(solution)/shard_map/ppermute | solution.py:260
  66.6 0.0 collective-permute-done.6.from_far
  66.6 0.0 collective-permute-done.7.from_near
  66.6 0.3 shard_map.43.outer
  66.9 3.4 %collective-permute-start.9 = (bf16[512,128]{1,0:T(8,128)(2,1)S(1)}, bf16[512,128]{1,0:T(8,128)(2,1)S(1)}, u32[]{:S(2)}, u32[]{:S(2)}) collective-permute-start(bf16[512,128]{1,0:T(8,128)(2,1)S(1)} %shard_map.43.outer), channel_id=1, source_target_pairs={{0,1},{1,0},{2,3},{3,2},{4,5},{5,4},{6,7},{7,6},{8,9},{9,8},{10,11... | collective-permute-start | bytes 393224 | tf_op jit(solution)/shard_map/ppermute | solution.py:262
  70.3 0.6 all-to-all-done.1.far
  70.9 1.2 shard_map.41.third
  72.1 0.0 collective-permute-done.8.inner2
  72.1 2.2 %collective-permute-done.9.outer2 = bf16[512,128]{1,0:T(8,128)(2,1)S(1)} collective-permute-done((bf16[512,128]{1,0:T(8,128)(2,1)S(1)}, bf16[512,128]{1,0:T(8,128)(2,1)S(1)}, u32[]{:S(2)}, u32[]{:S(2)}) %collective-permute-start.9) | collective-permute-done | bytes 131104 | tf_op jit(solution)/shard_map/ppermute | solution.py:262
  74.4 0.5 shard_map.44
  74.9 14.4 %all_to_all.30.parts = bf16[16,32,256]{2,1,0:T(8,128)(2,1)S(1)} all-to-all(bf16[16,32,256]{2,1,0:T(8,128)(2,1)S(1)} %shard_map.44), channel_id=1, replica_groups=mesh['z2'=4,'z1'=4,'xh'=2,'core'=2,'y'=4,'xl'=2] {'z1','xh','core'}, dimensions={0} | all-to-all | bytes 524288 | tf_op jit(solution)/shard_map/all_to_all | solution.py:200
  89.3 20.9 %all_to_all.31.parts = bf16[4,32,256]{2,1,0:T(8,128)(2,1)S(1)} all-to-all(bf16[4,32,256]{2,1,0:T(8,128)(2,1)S(1)} %shard_map.45), channel_id=1, replica_groups=mesh['z2'=4,'z1'=4,'xh'=2,'core'=2,'y'=4,'xl'=2] {'z2'}, dimensions={0} | all-to-all | bytes 131072 | tf_op jit(solution)/shard_map/all_to_all | solution.py:200
  110.2 16.1 %all_to_all.32.gram = bf16[16,32,256]{2,1,0:T(8,128)(2,1)S(1)} all-to-all(bf16[16,32,256]{2,1,0:T(8,128)(2,1)S(1)} %shard_map.46), channel_id=1, replica_groups=mesh['z2'=4,'z1'=4,'xh'=2,'core'=2,'y'=4,'xl'=2] {'z1','xh','core'}, dimensions={0} | all-to-all | bytes 524288 | tf_op jit(solution)/shard_map/all_to_all | solution.py:200
  126.3 0.4 shard_map.47
  126.7 13.5 %all_to_all.33.parts = bf16[8,128,256]{2,1,0:T(8,128)(2,1)S(1)} all-to-all(bf16[8,128,256]{2,1,0:T(8,128)(2,1)S(1)} %shard_map.47), channel_id=1, replica_groups=mesh['z2'=4,'z1'=4,'xh'=2,'core'=2,'y'=4,'xl'=2] {'y','xl'}, dimensions={0} | all-to-all | bytes 1048576 | tf_op jit(solution)/shard_map/all_to_all | solution.py:200
  140.2 0.8 shard_map.48
  (3 shorter events, 0.1 us)
Async XLA Ops:
  2.2 6.1 %copy-start = (bf16[1024,128]{1,0:T(8,128)(2,1)S(1)}, bf16[1024,128]{1,0:T(8,128)(2,1)}, u32[]{:S(2)}) copy-start(bf16[1024,128]{1,0:T(8,128)(2,1)} %rest_0_.1) | copy-start | bytes 786436
  2.2 22.7 %all-to-all-start = ((bf16[8,8,16,512]{3,2,1,0:T(8,128)(2,1)}), bf16[8,8,16,512]{3,2,1,0:T(8,128)(2,1)S(1)}, u32[]{:S(2)}, u32[]{:S(2)}) async-start(bf16[8,8,16,512]{3,2,1,0:T(8,128)(2,1)} %shard_map.37), calls=%async_computation | async-start | bytes 2097152 | tf_op jit(solution)/shard_map/all_to_all | solution.py:200
  8.3 16.6 %collective-permute-start = (bf16[256,128]{1,0:T(8,128)(2,1)S(1)}, bf16[256,128]{1,0:T(8,128)(2,1)S(1)}, u32[]{:S(2)}, u32[]{:S(2)}) collective-permute-start(bf16[256,128]{1,0:T(8,128)(2,1)S(1)} %get-tuple-element.26), channel_id=1, source_target_pairs={{0,504},{8,16},{16,8},{24,32},{32,24},{40,48},{48,40},{56,64},{64,... | collective-permute-start | bytes 196616 | tf_op jit(solution)/shard_map/ppermute | solution.py:206
  13.5 11.3 %collective-permute-start.1 = (bf16[256,128]{1,0:T(8,128)(2,1)S(1)}, bf16[256,128]{1,0:T(8,128)(2,1)S(1)}, u32[]{:S(2)}, u32[]{:S(2)}) collective-permute-start(bf16[256,128]{1,0:T(8,128)(2,1)S(1)} %get-tuple-element.25), channel_id=1, source_target_pairs={{0,8},{8,0},{1,9},{9,1},{2,10},{10,2},{3,11},{11,3},{4,12},{12,4},... | collective-permute-start | bytes 196616 | tf_op jit(solution)/shard_map/ppermute | solution.py:207
  25.4 14.3 %collective-permute-start.2 = (bf16[256,128]{1,0:T(8,128)(2,1)S(1)}, bf16[256,128]{1,0:T(8,128)(2,1)S(1)}, u32[]{:S(2)}, u32[]{:S(2)}) collective-permute-start(bf16[256,128]{1,0:T(8,128)(2,1)S(1)} %get-tuple-element.16), channel_id=1, source_target_pairs={{0,504},{8,16},{16,8},{24,32},{32,24},{40,48},{48,40},{56,64},{64,... | collective-permute-start | bytes 196616 | tf_op jit(solution)/shard_map/ppermute | solution.py:206
  30.4 10.2 %collective-permute-start.3 = (bf16[256,128]{1,0:T(8,128)(2,1)S(1)}, bf16[256,128]{1,0:T(8,128)(2,1)S(1)}, u32[]{:S(2)}, u32[]{:S(2)}) collective-permute-start(bf16[256,128]{1,0:T(8,128)(2,1)S(1)} %get-tuple-element.17), channel_id=1, source_target_pairs={{0,8},{8,0},{1,9},{9,1},{2,10},{10,2},{3,11},{11,3},{4,12},{12,4},... | collective-permute-start | bytes 196616 | tf_op jit(solution)/shard_map/ppermute | solution.py:207
  41.0 8.3 %collective-permute-start.4 = (bf16[256,128]{1,0:T(8,128)(2,1)S(1)}, bf16[256,128]{1,0:T(8,128)(2,1)S(1)}, u32[]{:S(2)}, u32[]{:S(2)}) collective-permute-start(bf16[256,128]{1,0:T(8,128)(2,1)S(1)} %get-tuple-element.19), channel_id=1, source_target_pairs={{0,504},{8,16},{16,8},{24,32},{32,24},{40,48},{48,40},{56,64},{64,... | collective-permute-start | bytes 196616 | tf_op jit(solution)/shard_map/ppermute | solution.py:206
  42.9 7.3 %collective-permute-start.5 = (bf16[256,128]{1,0:T(8,128)(2,1)S(1)}, bf16[256,128]{1,0:T(8,128)(2,1)S(1)}, u32[]{:S(2)}, u32[]{:S(2)}) collective-permute-start(bf16[256,128]{1,0:T(8,128)(2,1)S(1)} %get-tuple-element.20), channel_id=1, source_target_pairs={{0,8},{8,0},{1,9},{9,1},{2,10},{10,2},{3,11},{11,3},{4,12},{12,4},... | collective-permute-start | bytes 196616 | tf_op jit(solution)/shard_map/ppermute | solution.py:207
  51.7 19.2 %all-to-all-start.1 = ((bf16[4,1024,128]{2,1,0:T(8,128)(2,1)}), bf16[4,1024,128]{2,1,0:T(8,128)(2,1)}, u32[]{:S(2)}, u32[]{:S(2)}) async-start(bf16[4,1024,128]{2,1,0:T(8,128)(2,1)} %get-tuple-element.21), calls=%async_computation.1 | async-start | bytes 2097152 | tf_op jit(solution)/shard_map/all_to_all | solution.py:200
  56.0 10.6 %collective-permute-start.6 = (bf16[256,128]{1,0:T(8,128)(2,1)S(1)}, bf16[256,128]{1,0:T(8,128)(2,1)S(1)}, u32[]{:S(2)}, u32[]{:S(2)}) collective-permute-start(bf16[256,128]{1,0:T(8,128)(2,1)S(1)} %get-tuple-element.23), channel_id=1, source_target_pairs={{0,504},{8,16},{16,8},{24,32},{32,24},{40,48},{48,40},{56,64},{64,... | collective-permute-start | bytes 196616 | tf_op jit(solution)/shard_map/ppermute | solution.py:206
  57.9 8.6 %collective-permute-start.7 = (bf16[256,128]{1,0:T(8,128)(2,1)S(1)}, bf16[256,128]{1,0:T(8,128)(2,1)S(1)}, u32[]{:S(2)}, u32[]{:S(2)}) collective-permute-start(bf16[256,128]{1,0:T(8,128)(2,1)S(1)} %get-tuple-element.24), channel_id=1, source_target_pairs={{0,8},{8,0},{1,9},{9,1},{2,10},{10,2},{3,11},{11,3},{4,12},{12,4},... | collective-permute-start | bytes 196616 | tf_op jit(solution)/shard_map/ppermute | solution.py:207
  64.6 7.5 %collective-permute-start.8 = (bf16[512,128]{1,0:T(8,128)(2,1)S(1)}, bf16[512,128]{1,0:T(8,128)(2,1)S(1)}, u32[]{:S(2)}, u32[]{:S(2)}) collective-permute-start(bf16[512,128]{1,0:T(8,128)(2,1)S(1)} %shard_map.42.inner), channel_id=1, source_target_pairs={{0,1},{1,0},{2,3},{3,2},{4,5},{5,4},{6,7},{7,6},{8,9},{9,8},{10,11... | collective-permute-start | bytes 393224 | tf_op jit(solution)/shard_map/ppermute | solution.py:260
  66.9 7.5 %collective-permute-start.9 = (bf16[512,128]{1,0:T(8,128)(2,1)S(1)}, bf16[512,128]{1,0:T(8,128)(2,1)S(1)}, u32[]{:S(2)}, u32[]{:S(2)}) collective-permute-start(bf16[512,128]{1,0:T(8,128)(2,1)S(1)} %shard_map.43.outer), channel_id=1, source_target_pairs={{0,1},{1,0},{2,3},{3,2},{4,5},{5,4},{6,7},{7,6},{8,9},{9,8},{10,11... | collective-permute-start | bytes 393224 | tf_op jit(solution)/shard_map/ppermute | solution.py:262

commit v7 on v6

--- a/solution.py
+++ b/solution.py
@@ -12,7 +12,8 @@
 
 SLAB = ("z2", "z1", "xh", "core")
 BAND = ("y", "xl")
-NEAR = ("z1", "xh", "core")
+NEAR = ("z1", "core")
+FURTHER = ("z2", "xh")
 PAIR = [(0, 1), (1, 0)]
 FACE = 2
 F32 = jnp.float32
@@ -211,7 +212,7 @@
     blocks, _, strip, tile = hamiltonian.shape
     rows, width = orbitals.shape
     edge = FACE * tile
-    ny, nband, near, far = (lax.axis_size(a) for a in ("y", BAND, NEAR, "z2"))
+    ny, nband, near, far = (lax.axis_size(a) for a in ("y", BAND, NEAR, FURTHER))
     core = lax.axis_index("core")
     scalar = core.astype(jnp.int32).reshape(1)
 
@@ -279,7 +280,7 @@
         functools.partial(sum_kernel, None), [(far, share, columns)], (gather(partial_gram, NEAR),)
     )
     (scaled,) = call(
-        functools.partial(sum_kernel, scale), [(near, share, columns)], (gather(summed, "z2"),)
+        functools.partial(sum_kernel, scale), [(near, share, columns)], (gather(summed, FURTHER),)
     )
     gram = gather(scaled, NEAR)
     (partial_out,) = call(

time: 142 us -> 144 us (1.014); the launches traced: 141 us -> 141 us
  no operation moved by 1% of the time
where the time goes in v7:
time: 144 us; the launch traced here: 141 us
  blocking collectives  65.7 us (46%)
  starting transfers between devices  61.4 us (43%)
  Pallas kernels  8.23 us (6%)
  waiting for transfers between devices  4.57 us (3%)
    all_to_all x4, blocking collectives, gather(): return lax.all_to_all(copies, axes, 0, 0, tiled=True)  65.7 us
    ppermute x4, starting transfers between devices, swap(): return (from_far, lax.ppermute(near, 'core', PAIR))  32.5 us
    ppermute x4, starting transfers between devices, swap(): from_far = lax.ppermute(far, SLAB, pairs)  14.1 us
    all_to_all x2, starting transfers between devices, gather(): return lax.all_to_all(copies, axes, 0, 0, tiled=True)  9.61 us
    pallas_call x12, Pallas kernels, call(): pl.pallas_call(kernel, out_shape=shapes, in_specs=[SMEM if i < smem else...  8.23 us
    ppermute x1, starting transfers between devices, filtered(): outer2 = lax.ppermute(outer, 'xl', PAIR)  3.36 us
  transfers between devices with their start and end apart: 12, of which 5 were waited for; matrix products, arithmetic and copies ran while one was open for 0% of the time, Pallas kernels for 1%

profile of v7, /device:TPU:1, one launch (start us, length us, event | category | flops | bytes accessed | tf_op | source)
XLA Modules:
  0.0 141.2 jit_solution(10101101275869300276)
XLA Ops:
  0.0 2.2 %shard_map.37 = bf16[8,8,16,512]{3,2,1,0:T(8,128)(2,1)} custom-call(s32[8,7]{1,0:T(8,128)} %nbr_far.1, bf16[8,7,16,128]{3,2,1,0:T(8,128)(2,1)} %ham_far.1), custom_call_target="tpu_custom_call" | custom-call | tf_op jit(solution)/shard_map/pallas_call | solution.py:43
  2.2 0.0 copy-start
  2.2 6.1 %all-to-all-start = ((bf16[8,8,16,512]{3,2,1,0:T(8,128)(2,1)}), bf16[8,8,16,512]{3,2,1,0:T(8,128)(2,1)S(1)}, u32[]{:S(2)}, u32[]{:S(2)}) async-start(bf16[8,8,16,512]{3,2,1,0:T(8,128)(2,1)} %shard_map.37), calls=%async_computation | async-start | bytes 2097152 | tf_op jit(solution)/shard_map/all_to_all | solution.py:201
  8.3 0.0 copy-done
  8.3 5.2 %collective-permute-start = (bf16[256,128]{1,0:T(8,128)(2,1)S(1)}, bf16[256,128]{1,0:T(8,128)(2,1)S(1)}, u32[]{:S(2)}, u32[]{:S(2)}) collective-permute-start(bf16[256,128]{1,0:T(8,128)(2,1)S(1)} %get-tuple-element.26), channel_id=1, source_target_pairs={{0,504},{8,16},{16,8},{24,32},{32,24},{40,48},{48,40},{56,64},{64,... | collective-permute-start | bytes 196616 | tf_op jit(solution)/shard_map/ppermute | solution.py:207
  13.5 10.4 %collective-permute-start.1 = (bf16[256,128]{1,0:T(8,128)(2,1)S(1)}, bf16[256,128]{1,0:T(8,128)(2,1)S(1)}, u32[]{:S(2)}, u32[]{:S(2)}) collective-permute-start(bf16[256,128]{1,0:T(8,128)(2,1)S(1)} %get-tuple-element.25), channel_id=1, source_target_pairs={{0,8},{8,0},{1,9},{9,1},{2,10},{10,2},{3,11},{11,3},{4,12},{12,4},... | collective-permute-start | bytes 196616 | tf_op jit(solution)/shard_map/ppermute | solution.py:208
  23.9 0.9 collective-permute-done.from_far
  24.9 0.0 collective-permute-done.1.from_near
  24.9 0.0 all-to-all-done.ham
  24.9 0.5 shard_map.38
  25.3 5.0 %collective-permute-start.2 = (bf16[256,128]{1,0:T(8,128)(2,1)S(1)}, bf16[256,128]{1,0:T(8,128)(2,1)S(1)}, u32[]{:S(2)}, u32[]{:S(2)}) collective-permute-start(bf16[256,128]{1,0:T(8,128)(2,1)S(1)} %get-tuple-element.16), channel_id=1, source_target_pairs={{0,504},{8,16},{16,8},{24,32},{32,24},{40,48},{48,40},{56,64},{64,... | collective-permute-start | bytes 196616 | tf_op jit(solution)/shard_map/ppermute | solution.py:207
  30.4 9.3 %collective-permute-start.3 = (bf16[256,128]{1,0:T(8,128)(2,1)S(1)}, bf16[256,128]{1,0:T(8,128)(2,1)S(1)}, u32[]{:S(2)}, u32[]{:S(2)}) collective-permute-start(bf16[256,128]{1,0:T(8,128)(2,1)S(1)} %get-tuple-element.17), channel_id=1, source_target_pairs={{0,8},{8,0},{1,9},{9,1},{2,10},{10,2},{3,11},{11,3},{4,12},{12,4},... | collective-permute-start | bytes 196616 | tf_op jit(solution)/shard_map/ppermute | solution.py:208
  39.7 0.0 collective-permute-done.2.from_far
  39.7 0.9 collective-permute-done.3.from_near
  40.5 0.5 shard_map.39
  41.0 1.9 %collective-permute-start.4 = (bf16[256,128]{1,0:T(8,128)(2,1)S(1)}, bf16[256,128]{1,0:T(8,128)(2,1)S(1)}, u32[]{:S(2)}, u32[]{:S(2)}) collective-permute-start(bf16[256,128]{1,0:T(8,128)(2,1)S(1)} %get-tuple-element.19), channel_id=1, source_target_pairs={{0,504},{8,16},{16,8},{24,32},{32,24},{40,48},{48,40},{56,64},{64,... | collective-permute-start | bytes 196616 | tf_op jit(solution)/shard_map/ppermute | solution.py:207
  42.9 6.4 %collective-permute-start.5 = (bf16[256,128]{1,0:T(8,128)(2,1)S(1)}, bf16[256,128]{1,0:T(8,128)(2,1)S(1)}, u32[]{:S(2)}, u32[]{:S(2)}) collective-permute-start(bf16[256,128]{1,0:T(8,128)(2,1)S(1)} %get-tuple-element.20), channel_id=1, source_target_pairs={{0,8},{8,0},{1,9},{9,1},{2,10},{10,2},{3,11},{11,3},{4,12},{12,4},... | collective-permute-start | bytes 196616 | tf_op jit(solution)/shard_map/ppermute | solution.py:208
  49.3 0.0 collective-permute-done.4.from_far
  49.3 0.9 collective-permute-done.5.from_near
  50.2 1.5 %shard_map.40 = (bf16[1024,128]{1,0:T(8,128)(2,1)S(1)}, bf16[4,1024,128]{2,1,0:T(8,128)(2,1)}, bf16[256,128]{1,0:T(8,128)(2,1)S(1)}, bf16[256,128]{1,0:T(8,128)(2,1)S(1)}) custom-call(s32[1]{0:T(128)} %bitcast.core, bf16[8,8,16,512]{3,2,1,0:T(8,128)(2,1)S(1)} %all-to-all-done.ham, bf16[1024,128]{1,0:T(8,128)(2,1)S(1)} %get-tuple-element.18.vec, ...), custom_call_target="tpu_custom_call" | custom-call | tf_op jit(solution)/shard_map/pallas_call | solution.py:43
  51.7 3.5 %all-to-all-start.1 = ((bf16[4,1024,128]{2,1,0:T(8,128)(2,1)}), bf16[4,1024,128]{2,1,0:T(8,128)(2,1)S(1)}, u32[]{:S(2)}, u32[]{:S(2)}) async-start(bf16[4,1024,128]{2,1,0:T(8,128)(2,1)} %get-tuple-element.21), calls=%async_computation.1 | async-start | bytes 2097152 | tf_op jit(solution)/shard_map/all_to_all | solution.py:201
  55.2 1.9 %collective-permute-start.6 = (bf16[256,128]{1,0:T(8,128)(2,1)S(1)}, bf16[256,128]{1,0:T(8,128)(2,1)S(1)}, u32[]{:S(2)}, u32[]{:S(2)}) collective-permute-start(bf16[256,128]{1,0:T(8,128)(2,1)S(1)} %get-tuple-element.23), channel_id=1, source_target_pairs={{0,504},{8,16},{16,8},{24,32},{32,24},{40,48},{48,40},{56,64},{64,... | collective-permute-start | bytes 196616 | tf_op jit(solution)/shard_map/ppermute | solution.py:207
  57.2 6.4 %collective-permute-start.7 = (bf16[256,128]{1,0:T(8,128)(2,1)S(1)}, bf16[256,128]{1,0:T(8,128)(2,1)S(1)}, u32[]{:S(2)}, u32[]{:S(2)}) collective-permute-start(bf16[256,128]{1,0:T(8,128)(2,1)S(1)} %get-tuple-element.24), channel_id=1, source_target_pairs={{0,8},{8,0},{1,9},{9,1},{2,10},{10,2},{3,11},{11,3},{4,12},{12,4},... | collective-permute-start | bytes 196616 | tf_op jit(solution)/shard_map/ppermute | solution.py:208
  63.6 0.3 shard_map.42.inner
  63.9 1.9 %collective-permute-start.8 = (bf16[512,128]{1,0:T(8,128)(2,1)S(1)}, bf16[512,128]{1,0:T(8,128)(2,1)S(1)}, u32[]{:S(2)}, u32[]{:S(2)}) collective-permute-start(bf16[512,128]{1,0:T(8,128)(2,1)S(1)} %shard_map.42.inner), channel_id=1, source_target_pairs={{0,1},{1,0},{2,3},{3,2},{4,5},{5,4},{6,7},{7,6},{8,9},{9,8},{10,11... | collective-permute-start | bytes 393224 | tf_op jit(solution)/shard_map/ppermute | solution.py:261
  65.8 0.0 collective-permute-done.6.from_far
  65.8 0.0 collective-permute-done.7.from_near
  65.8 0.3 shard_map.43.outer
  66.1 3.4 %collective-permute-start.9 = (bf16[512,128]{1,0:T(8,128)(2,1)S(1)}, bf16[512,128]{1,0:T(8,128)(2,1)S(1)}, u32[]{:S(2)}, u32[]{:S(2)}) collective-permute-start(bf16[512,128]{1,0:T(8,128)(2,1)S(1)} %shard_map.43.outer), channel_id=1, source_target_pairs={{0,1},{1,0},{2,3},{3,2},{4,5},{5,4},{6,7},{7,6},{8,9},{9,8},{10,11... | collective-permute-start | bytes 393224 | tf_op jit(solution)/shard_map/ppermute | solution.py:263
  69.5 0.5 all-to-all-done.1.far
  70.0 0.0 copy-start.1
  70.0 1.0 copy-done.1
  71.0 1.2 shard_map.41.third
  72.3 0.0 collective-permute-done.8.inner2
  72.3 1.3 collective-permute-done.9.outer2
  73.6 0.5 shard_map.44
  74.1 12.0 %all_to_all.30.parts = bf16[8,64,256]{2,1,0:T(8,128)(2,1)S(1)} all-to-all(bf16[8,64,256]{2,1,0:T(8,128)(2,1)S(1)} %shard_map.44), channel_id=1, replica_groups=mesh['z2'=4,'z1'=4,'xh'=2,'core'=2,'y'=4,'xl'=2] {'z1','core'}, dimensions={0} | all-to-all | bytes 524288 | tf_op jit(solution)/shard_map/all_to_all | solution.py:201
  86.1 26.8 %all_to_all.31.parts = bf16[8,64,256]{2,1,0:T(8,128)(2,1)S(1)} all-to-all(bf16[8,64,256]{2,1,0:T(8,128)(2,1)S(1)} %shard_map.45), channel_id=1, replica_groups=mesh['z2'=4,'z1'=4,'xh'=2,'core'=2,'y'=4,'xl'=2] {'z2','xh'}, dimensions={0} | all-to-all | bytes 524288 | tf_op jit(solution)/shard_map/all_to_all | solution.py:201
  112.9 13.8 %all_to_all.32.gram = bf16[8,64,256]{2,1,0:T(8,128)(2,1)S(1)} all-to-all(bf16[8,64,256]{2,1,0:T(8,128)(2,1)S(1)} %shard_map.46), channel_id=1, replica_groups=mesh['z2'=4,'z1'=4,'xh'=2,'core'=2,'y'=4,'xl'=2] {'z1','core'}, dimensions={0} | all-to-all | bytes 524288 | tf_op jit(solution)/shard_map/all_to_all | solution.py:201
  126.8 0.4 shard_map.47
  127.2 13.1 %all_to_all.33.parts = bf16[8,128,256]{2,1,0:T(8,128)(2,1)S(1)} all-to-all(bf16[8,128,256]{2,1,0:T(8,128)(2,1)S(1)} %shard_map.47), channel_id=1, replica_groups=mesh['z2'=4,'z1'=4,'xh'=2,'core'=2,'y'=4,'xl'=2] {'y','xl'}, dimensions={0} | all-to-all | bytes 1048576 | tf_op jit(solution)/shard_map/all_to_all | solution.py:201
  140.4 0.8 shard_map.48
  (3 shorter events, 0.1 us)
Async XLA Ops:
  2.2 6.1 %copy-start = (bf16[1024,128]{1,0:T(8,128)(2,1)S(1)}, bf16[1024,128]{1,0:T(8,128)(2,1)}, u32[]{:S(2)}) copy-start(bf16[1024,128]{1,0:T(8,128)(2,1)} %rest_0_.1) | copy-start | bytes 786436
  2.2 22.7 %all-to-all-start = ((bf16[8,8,16,512]{3,2,1,0:T(8,128)(2,1)}), bf16[8,8,16,512]{3,2,1,0:T(8,128)(2,1)S(1)}, u32[]{:S(2)}, u32[]{:S(2)}) async-start(bf16[8,8,16,512]{3,2,1,0:T(8,128)(2,1)} %shard_map.37), calls=%async_computation | async-start | bytes 2097152 | tf_op jit(solution)/shard_map/all_to_all | solution.py:201
  8.3 16.6 %collective-permute-start = (bf16[256,128]{1,0:T(8,128)(2,1)S(1)}, bf16[256,128]{1,0:T(8,128)(2,1)S(1)}, u32[]{:S(2)}, u32[]{:S(2)}) collective-permute-start(bf16[256,128]{1,0:T(8,128)(2,1)S(1)} %get-tuple-element.26), channel_id=1, source_target_pairs={{0,504},{8,16},{16,8},{24,32},{32,24},{40,48},{48,40},{56,64},{64,... | collective-permute-start | bytes 196616 | tf_op jit(solution)/shard_map/ppermute | solution.py:207
  13.5 11.3 %collective-permute-start.1 = (bf16[256,128]{1,0:T(8,128)(2,1)S(1)}, bf16[256,128]{1,0:T(8,128)(2,1)S(1)}, u32[]{:S(2)}, u32[]{:S(2)}) collective-permute-start(bf16[256,128]{1,0:T(8,128)(2,1)S(1)} %get-tuple-element.25), channel_id=1, source_target_pairs={{0,8},{8,0},{1,9},{9,1},{2,10},{10,2},{3,11},{11,3},{4,12},{12,4},... | collective-permute-start | bytes 196616 | tf_op jit(solution)/shard_map/ppermute | solution.py:208
  25.3 14.3 %collective-permute-start.2 = (bf16[256,128]{1,0:T(8,128)(2,1)S(1)}, bf16[256,128]{1,0:T(8,128)(2,1)S(1)}, u32[]{:S(2)}, u32[]{:S(2)}) collective-permute-start(bf16[256,128]{1,0:T(8,128)(2,1)S(1)} %get-tuple-element.16), channel_id=1, source_target_pairs={{0,504},{8,16},{16,8},{24,32},{32,24},{40,48},{48,40},{56,64},{64,... | collective-permute-start | bytes 196616 | tf_op jit(solution)/shard_map/ppermute | solution.py:207
  30.4 10.2 %collective-permute-start.3 = (bf16[256,128]{1,0:T(8,128)(2,1)S(1)}, bf16[256,128]{1,0:T(8,128)(2,1)S(1)}, u32[]{:S(2)}, u32[]{:S(2)}) collective-permute-start(bf16[256,128]{1,0:T(8,128)(2,1)S(1)} %get-tuple-element.17), channel_id=1, source_target_pairs={{0,8},{8,0},{1,9},{9,1},{2,10},{10,2},{3,11},{11,3},{4,12},{12,4},... | collective-permute-start | bytes 196616 | tf_op jit(solution)/shard_map/ppermute | solution.py:208
  41.0 8.3 %collective-permute-start.4 = (bf16[256,128]{1,0:T(8,128)(2,1)S(1)}, bf16[256,128]{1,0:T(8,128)(2,1)S(1)}, u32[]{:S(2)}, u32[]{:S(2)}) collective-permute-start(bf16[256,128]{1,0:T(8,128)(2,1)S(1)} %get-tuple-element.19), channel_id=1, source_target_pairs={{0,504},{8,16},{16,8},{24,32},{32,24},{40,48},{48,40},{56,64},{64,... | collective-permute-start | bytes 196616 | tf_op jit(solution)/shard_map/ppermute | solution.py:207
  42.9 7.3 %collective-permute-start.5 = (bf16[256,128]{1,0:T(8,128)(2,1)S(1)}, bf16[256,128]{1,0:T(8,128)(2,1)S(1)}, u32[]{:S(2)}, u32[]{:S(2)}) collective-permute-start(bf16[256,128]{1,0:T(8,128)(2,1)S(1)} %get-tuple-element.20), channel_id=1, source_target_pairs={{0,8},{8,0},{1,9},{9,1},{2,10},{10,2},{3,11},{11,3},{4,12},{12,4},... | collective-permute-start | bytes 196616 | tf_op jit(solution)/shard_map/ppermute | solution.py:208
  51.7 18.3 %all-to-all-start.1 = ((bf16[4,1024,128]{2,1,0:T(8,128)(2,1)}), bf16[4,1024,128]{2,1,0:T(8,128)(2,1)S(1)}, u32[]{:S(2)}, u32[]{:S(2)}) async-start(bf16[4,1024,128]{2,1,0:T(8,128)(2,1)} %get-tuple-element.21), calls=%async_computation.1 | async-start | bytes 2097152 | tf_op jit(solution)/shard_map/all_to_all | solution.py:201
  55.2 10.6 %collective-permute-start.6 = (bf16[256,128]{1,0:T(8,128)(2,1)S(1)}, bf16[256,128]{1,0:T(8,128)(2,1)S(1)}, u32[]{:S(2)}, u32[]{:S(2)}) collective-permute-start(bf16[256,128]{1,0:T(8,128)(2,1)S(1)} %get-tuple-element.23), channel_id=1, source_target_pairs={{0,504},{8,16},{16,8},{24,32},{32,24},{40,48},{48,40},{56,64},{64,... | collective-permute-start | bytes 196616 | tf_op jit(solution)/shard_map/ppermute | solution.py:207
  57.2 8.6 %collective-permute-start.7 = (bf16[256,128]{1,0:T(8,128)(2,1)S(1)}, bf16[256,128]{1,0:T(8,128)(2,1)S(1)}, u32[]{:S(2)}, u32[]{:S(2)}) collective-permute-start(bf16[256,128]{1,0:T(8,128)(2,1)S(1)} %get-tuple-element.24), channel_id=1, source_target_pairs={{0,8},{8,0},{1,9},{9,1},{2,10},{10,2},{3,11},{11,3},{4,12},{12,4},... | collective-permute-start | bytes 196616 | tf_op jit(solution)/shard_map/ppermute | solution.py:208
  63.9 8.4 %collective-permute-start.8 = (bf16[512,128]{1,0:T(8,128)(2,1)S(1)}, bf16[512,128]{1,0:T(8,128)(2,1)S(1)}, u32[]{:S(2)}, u32[]{:S(2)}) collective-permute-start(bf16[512,128]{1,0:T(8,128)(2,1)S(1)} %shard_map.42.inner), channel_id=1, source_target_pairs={{0,1},{1,0},{2,3},{3,2},{4,5},{5,4},{6,7},{7,6},{8,9},{9,8},{10,11... | collective-permute-start | bytes 393224 | tf_op jit(solution)/shard_map/ppermute | solution.py:261
  66.1 7.5 %collective-permute-start.9 = (bf16[512,128]{1,0:T(8,128)(2,1)S(1)}, bf16[512,128]{1,0:T(8,128)(2,1)S(1)}, u32[]{:S(2)}, u32[]{:S(2)}) collective-permute-start(bf16[512,128]{1,0:T(8,128)(2,1)S(1)} %shard_map.43.outer), channel_id=1, source_target_pairs={{0,1},{1,0},{2,3},{3,2},{4,5},{5,4},{6,7},{7,6},{8,9},{9,8},{10,11... | collective-permute-start | bytes 393224 | tf_op jit(solution)/shard_map/ppermute | solution.py:263
  70.0 1.0 copy-start.1

commit v8 on v6

--- a/solution.py
+++ b/solution.py
@@ -87,56 +87,64 @@
     return dot(ham[:, r].reshape(tile, 4 * tile), rhs)
 
 
-def fill(core, ext, vec, from_far, from_near):
-    edge, rows = from_far.shape[0], vec.shape[0]
+def fill(ext, inner, outer):
+    edge, rows = outer.shape[0] // 2, inner.shape[0]
+    ext[edge : 2 * edge] = outer[:edge]
+    ext[2 * edge : 2 * edge + rows] = inner[...]
+    ext[2 * edge + rows : 3 * edge + rows] = outer[edge:]
+
+
+def inner_kernel(prior, ham, inner, outer, *rest):
+    out, ext = rest[-2:]
+    tile = ham.shape[3] // 4
+    fill(ext, inner, outer)
+    for i in range(out.shape[0] // tile):
+        here = slice(i * tile, (i + 1) * tile)
+        value = product(ham, FACE + i, ext)
+        if prior:
+            value = 2.0 * value - rest[0][here].astype(F32)
+        out[here] = value.astype(BF16)
+
+
+def outer_kernel(prior, copying, core, ham, inner, outer, from_far, from_near, *rest):
+    rest = list(rest)
+    before = rest.pop(0) if prior else None
+    done = rest.pop(0) if copying else None
+    out = rest.pop(0)
+    copies = rest.pop(0) if copying else None
+    ext = rest[-2] if copying else rest[-1]
+    sems = rest[-1]
+    edge, rows = from_far.shape[0], inner.shape[0]
+    tile = edge // FACE
+    sends = []
+
+    def send(part, start, which):
+        for i in range(copies.shape[0]):
+            here = pl.ds(start, part.shape[0])
+            sends.append(pltpu.make_async_copy(part, copies.at[i, here], sems.at[which, i]))
+            sends[-1].start()
+
+    if copying:
+        send(done, 0, 0)
+    fill(ext, inner, outer)
     c = core[0]
-    ext[edge : edge + rows] = vec[...]
-    ext[pl.ds(pl.multiple_of(c * (edge + rows), edge), edge)] = from_far[...]
-    ext[pl.ds(pl.multiple_of((1 - c) * (edge + rows), edge), edge)] = from_near[...]
-
-
-def step_kernel(prior, core, ham, vec, from_far, from_near, *rest):
-    before = rest[0] if prior else None
-    out, far, near, ext, *copying = rest[1:] if prior else rest
-    if copying:
-        out, copies, far, near, ext, sems = rest[1:]
-    edge, rows = far.shape[0], vec.shape[0]
-    tile = edge // FACE
-    fill(core, ext, vec, from_far, from_near)
-    for r in range(rows // tile):
-        here = slice(r * tile, (r + 1) * tile)
+    last = rows + 3 * edge
+    ext[pl.ds(pl.multiple_of(c * last, edge), edge)] = from_far[...]
+    ext[pl.ds(pl.multiple_of((1 - c) * last, edge), edge)] = from_near[...]
+    blocks = (rows + 2 * edge) // tile
+    for i, r in enumerate((*range(FACE), *range(blocks - FACE, blocks))):
+        here = slice(i * tile, (i + 1) * tile)
         value = product(ham, r, ext)
         if prior:
             value = 2.0 * value - before[here].astype(F32)
         out[here] = value.astype(BF16)
-    sends = []
     if copying:
-        for i in range(copies.shape[0]):
-            sends.append(pltpu.make_async_copy(out, copies.at[i], sems.at[i]))
-    for send in sends:
-        send.start()
-    c = core[0]
-    far[...] = out[pl.ds(pl.multiple_of(c * (rows - edge), edge), edge)]
-    near[...] = out[pl.ds(pl.multiple_of((1 - c) * (rows - edge), edge), edge)]
-    for send in sends:
-        send.wait()
-
-
-def inner_kernel(ham, vec, out, ext):
-    rows = vec.shape[0]
-    edge = (ext.shape[0] - rows) // 2
-    tile = edge // FACE
-    ext[edge : edge + rows] = vec[...]
-    for i in range(out.shape[0] // tile):
-        out[i * tile : (i + 1) * tile] = product(ham, FACE + i, ext).astype(BF16)
-
-
-def outer_kernel(core, ham, vec, from_far, from_near, out, ext):
-    edge, rows = from_far.shape[0], vec.shape[0]
-    tile = edge // FACE
-    fill(core, ext, vec, from_far, from_near)
-    for i, r in enumerate((*range(FACE), *range(rows // tile - FACE, rows // tile))):
-        out[i * tile : (i + 1) * tile] = product(ham, r, ext).astype(BF16)
+        send(out, rows, 1)
+    if len(rest) > 1:
+        rest[0][...] = out[pl.ds(pl.multiple_of(c * edge, edge), edge)]
+        rest[1][...] = out[pl.ds(pl.multiple_of((1 - c) * edge, edge), edge)]
+    for copy in sends:
+        copy.wait()
 
 
 def fetch_kernel(far, out, sem):
@@ -148,9 +156,8 @@
 def gram_kernel(third, inner, outer, inner2, outer2, out):
     share, width = out.shape[1], third.shape[2]
     per = width // share
-    edge = outer.shape[0] // 2
-    own = jnp.concatenate([outer[:edge], inner[...], outer[edge:]], axis=0)
-    other = jnp.concatenate([outer2[:edge], inner2[...], outer2[edge:]], axis=0)
+    own = jnp.concatenate([inner[...], outer[...]], axis=0)
+    other = jnp.concatenate([inner2[...], outer2[...]], axis=0)
     right = jnp.concatenate([own, other], axis=1)
     for y in range(third.shape[0]):
         block = dot(third[y], right, ((0,), (0,))).astype(BF16)
@@ -175,16 +182,16 @@
     edge = outer.shape[0] // (2 * height)
     weights = gram[...].reshape(count * width, gram.shape[2])
     for s in range(strips):
-        here = slice(s * height, (s + 1) * height)
-        left = jnp.concatenate([third[y, here] for y in range(count)], axis=1)
+        part, at = inner, (s - edge) * height
+        if s < edge or s >= strips - edge:
+            part, at = outer, (s if s < edge else s - strips + 2 * edge) * height
+        here = slice(at, at + height)
+        start = at + (0 if part is inner else inner.shape[0])
+        left = jnp.concatenate(
+            [third[y, start : start + height] for y in range(count)], axis=1
+        )
         value = dot(left, weights)
-        if s < edge:
-            applied = outer[here]
-        elif s < strips - edge:
-            applied = inner[(s - edge) * height : (s - edge + 1) * height]
-        else:
-            at = (s - strips + 2 * edge) * height
-            applied = outer[at : at + height]
+        applied = part[here]
         out[s, :, :width] = (applied.astype(F32) - value[:, :width]).astype(BF16)
         out[s, :, width:] = (-value[:, width:]).astype(BF16)
 
@@ -233,32 +240,42 @@
     )
 
     ext = pltpu.VMEM((rows + 2 * edge, width), BF16)
-    whole, face, part = (rows, width), (edge, width), (rows - 2 * edge, width)
-
-    def step(vec, received, before=()):
+    face, inside, outside = (edge, width), (rows - 2 * edge, width), (2 * edge, width)
+
+    def step_inner(vec, before=()):
+        kernel = functools.partial(inner_kernel, bool(before))
+        return call(kernel, [inside], (tiles, *vec, *before), (ext,))[0]
+
+    def step_outer(vec, received, before=(), done=(), faces=True):
+        outs = [outside] + ([(ny, rows, width)] if done else []) + ([face, face] if faces else [])
         return call(
-            functools.partial(step_kernel, bool(before)),
-            [whole, face, face],
-            (scalar, tiles, vec, *received, *before),
-            (ext,),
+            functools.partial(outer_kernel, bool(before), bool(done)),
+            outs,
+            (scalar, tiles, *vec, *received, *before, *done),
+            (ext, pltpu.SemaphoreType.DMA((2, ny))) if done else (ext,),
             smem=1,
+            far_outs=(1,) if done else (),
         )
 
-    first, *faces = step(orbitals, received)
-    second, *faces = step(first, swap(*faces), (orbitals,))
-    third, copies, *faces = call(
-        functools.partial(step_kernel, True),
-        [whole, (ny, rows, width), face, face],
-        (scalar, tiles, second, *swap(*faces), first),
-        (ext, pltpu.SemaphoreType.DMA((ny,))),
-        smem=1,
-        far_outs=(1,),
-    )
+    start = (
+        orbitals[edge : rows - edge],
+        jnp.concatenate([orbitals[:edge], orbitals[rows - edge :]], axis=0),
+    )
+    first_outer, *faces = step_outer(start, received)
     received = swap(*faces)
+    first = (step_inner(start), first_outer)
+    second_inner = step_inner(first, start[:1])
+    second_outer, *faces = step_outer(first, received, start[1:])
+    received = swap(*faces)
+    second = (second_inner, second_outer)
+    third_inner = step_inner(second, first[:1])
+    third_outer, copies, *faces = step_outer(second, received, first[1:], (third_inner,))
+    received = swap(*faces)
+    third = (third_inner, third_outer)
     third_far = gather(copies, "y")
-    (inner,) = call(inner_kernel, [part], (tiles, third), (ext,))
+    inner = step_inner(third)
     inner2 = lax.ppermute(inner, "xl", PAIR)
-    (outer,) = call(outer_kernel, [(2 * edge, width)], (scalar, tiles, third, *received), (ext,), smem=1)
+    (outer,) = step_outer(third, received, faces=False)
     outer2 = lax.ppermute(outer, "xl", PAIR)
     (third_all,) = call(
         fetch_kernel,

time: 142 us -> 141 us (level)
    pallas_call x12 -> x15, Pallas kernels: 8.23 us -> 8.59 us  [call(): pl.pallas_call(kernel, out_shape=shapes, in_specs=[SMEM if i < smem else...]
  transfers between devices with their start and end apart: 12 -> 12, of which waited for: 5 -> 5; matrix products, arithmetic and copies ran while one was open for 0% -> 0% of each run, Pallas kernels for 1% -> 2%
where the time goes in v8:
time: 141 us; the launch traced here: 140 us
  blocking collectives  64.9 us (46%)
  starting transfers between devices  62.1 us (44%)
  Pallas kernels  8.59 us (6%)
  waiting for transfers between devices  4.56 us (3%)
    all_to_all x4, blocking collectives, gather(): return lax.all_to_all(copies, axes, 0, 0, tiled=True)  64.9 us
    ppermute x4, starting transfers between devices, swap(): return (from_far, lax.ppermute(near, 'core', PAIR))  32.5 us
    ppermute x4, starting transfers between devices, swap(): from_far = lax.ppermute(far, SLAB, pairs)  14 us
    all_to_all x2, starting transfers between devices, gather(): return lax.all_to_all(copies, axes, 0, 0, tiled=True)  10.3 us
    pallas_call x15, Pallas kernels, call(): pl.pallas_call(kernel, out_shape=shapes, in_specs=[SMEM if i < smem else...  8.59 us
    ppermute x1, starting transfers between devices, filtered(): outer2 = lax.ppermute(outer, 'xl', PAIR)  3.36 us
  transfers between devices with their start and end apart: 12, of which 5 were waited for; matrix products, arithmetic and copies ran while one was open for 0% of the time, Pallas kernels for 2%

profile of v8, /device:TPU:1, one launch (start us, length us, event | category | flops | bytes accessed | tf_op | source)
XLA Modules:
  0.0 140.5 jit_solution(17950377507503009638)
XLA Ops:
  0.0 2.2 %shard_map.37 = bf16[8,8,16,512]{3,2,1,0:T(8,128)(2,1)} custom-call(s32[8,7]{1,0:T(8,128)} %nbr_far.1, bf16[8,7,16,128]{3,2,1,0:T(8,128)(2,1)} %ham_far.1), custom_call_target="tpu_custom_call" | custom-call | tf_op jit(solution)/shard_map/pallas_call | solution.py:42
  2.2 0.0 copy-start
  2.2 6.1 %all-to-all-start = ((bf16[8,8,16,512]{3,2,1,0:T(8,128)(2,1)}), bf16[8,8,16,512]{3,2,1,0:T(8,128)(2,1)S(1)}, u32[]{:S(2)}, u32[]{:S(2)}) async-start(bf16[8,8,16,512]{3,2,1,0:T(8,128)(2,1)} %shard_map.37), calls=%async_computation | async-start | bytes 2097152 | tf_op jit(solution)/shard_map/all_to_all | solution.py:207
  8.3 0.0 copy-done
  8.3 5.2 %collective-permute-start = (bf16[256,128]{1,0:T(8,128)(2,1)S(1)}, bf16[256,128]{1,0:T(8,128)(2,1)S(1)}, u32[]{:S(2)}, u32[]{:S(2)}) collective-permute-start(bf16[256,128]{1,0:T(8,128)(2,1)S(1)} %get-tuple-element.28), channel_id=1, source_target_pairs={{0,504},{8,16},{16,8},{24,32},{32,24},{40,48},{48,40},{56,64},{64,... | collective-permute-start | bytes 196616 | tf_op jit(solution)/shard_map/ppermute | solution.py:213
  13.5 10.4 %collective-permute-start.1 = (bf16[256,128]{1,0:T(8,128)(2,1)S(1)}, bf16[256,128]{1,0:T(8,128)(2,1)S(1)}, u32[]{:S(2)}, u32[]{:S(2)}) collective-permute-start(bf16[256,128]{1,0:T(8,128)(2,1)S(1)} %get-tuple-element.25), channel_id=1, source_target_pairs={{0,8},{8,0},{1,9},{9,1},{2,10},{10,2},{3,11},{11,3},{4,12},{12,4},... | collective-permute-start | bytes 196616 | tf_op jit(solution)/shard_map/ppermute | solution.py:214
  24.0 0.9 collective-permute-done.from_far
  24.9 0.0 collective-permute-done.1.from_near
  24.9 0.0 all-to-all-done.ham
  24.9 0.3 shard_map.39
  25.2 5.0 %collective-permute-start.2 = (bf16[256,128]{1,0:T(8,128)(2,1)S(1)}, bf16[256,128]{1,0:T(8,128)(2,1)S(1)}, u32[]{:S(2)}, u32[]{:S(2)}) collective-permute-start(bf16[256,128]{1,0:T(8,128)(2,1)S(1)} %get-tuple-element.16), channel_id=1, source_target_pairs={{0,504},{8,16},{16,8},{24,32},{32,24},{40,48},{48,40},{56,64},{64,... | collective-permute-start | bytes 196616 | tf_op jit(solution)/shard_map/ppermute | solution.py:213
  30.2 9.3 %collective-permute-start.3 = (bf16[256,128]{1,0:T(8,128)(2,1)S(1)}, bf16[256,128]{1,0:T(8,128)(2,1)S(1)}, u32[]{:S(2)}, u32[]{:S(2)}) collective-permute-start(bf16[256,128]{1,0:T(8,128)(2,1)S(1)} %get-tuple-element.17), channel_id=1, source_target_pairs={{0,8},{8,0},{1,9},{9,1},{2,10},{10,2},{3,11},{11,3},{4,12},{12,4},... | collective-permute-start | bytes 196616 | tf_op jit(solution)/shard_map/ppermute | solution.py:214
  39.5 0.3 shard_map.38.inner.rest_0_
  39.8 0.0 collective-permute-done.2.from_far
  39.9 0.6 collective-permute-done.3.from_near
  40.4 0.3 shard_map.41
  40.7 1.9 %collective-permute-start.4 = (bf16[256,128]{1,0:T(8,128)(2,1)S(1)}, bf16[256,128]{1,0:T(8,128)(2,1)S(1)}, u32[]{:S(2)}, u32[]{:S(2)}) collective-permute-start(bf16[256,128]{1,0:T(8,128)(2,1)S(1)} %get-tuple-element.19), channel_id=1, source_target_pairs={{0,504},{8,16},{16,8},{24,32},{32,24},{40,48},{48,40},{56,64},{64,... | collective-permute-start | bytes 196616 | tf_op jit(solution)/shard_map/ppermute | solution.py:213
  42.7 6.4 %collective-permute-start.5 = (bf16[256,128]{1,0:T(8,128)(2,1)S(1)}, bf16[256,128]{1,0:T(8,128)(2,1)S(1)}, u32[]{:S(2)}, u32[]{:S(2)}) collective-permute-start(bf16[256,128]{1,0:T(8,128)(2,1)S(1)} %get-tuple-element.20), channel_id=1, source_target_pairs={{0,8},{8,0},{1,9},{9,1},{2,10},{10,2},{3,11},{11,3},{4,12},{12,4},... | collective-permute-start | bytes 196616 | tf_op jit(solution)/shard_map/ppermute | solution.py:214
  49.1 0.3 shard_map.40.inner
  49.4 0.3 shard_map.42.rest_1_.inner
  49.7 0.0 collective-permute-done.4.from_far
  49.7 0.2 collective-permute-done.5.from_near
  50.0 1.2 shard_map.43
  51.1 4.3 %all-to-all-start.1 = ((bf16[4,1024,128]{2,1,0:T(8,128)(2,1)}), bf16[4,1024,128]{2,1,0:T(8,128)(2,1)}, u32[]{:S(2)}, u32[]{:S(2)}) async-start(bf16[4,1024,128]{2,1,0:T(8,128)(2,1)} %get-tuple-element.21), calls=%async_computation.1 | async-start | bytes 2097152 | tf_op jit(solution)/shard_map/all_to_all | solution.py:207
  55.4 1.9 %collective-permute-start.6 = (bf16[256,128]{1,0:T(8,128)(2,1)S(1)}, bf16[256,128]{1,0:T(8,128)(2,1)S(1)}, u32[]{:S(2)}, u32[]{:S(2)}) collective-permute-start(bf16[256,128]{1,0:T(8,128)(2,1)S(1)} %get-tuple-element.23), channel_id=1, source_target_pairs={{0,504},{8,16},{16,8},{24,32},{32,24},{40,48},{48,40},{56,64},{64,... | collective-permute-start | bytes 196616 | tf_op jit(solution)/shard_map/ppermute | solution.py:213
  57.3 6.4 %collective-permute-start.7 = (bf16[256,128]{1,0:T(8,128)(2,1)S(1)}, bf16[256,128]{1,0:T(8,128)(2,1)S(1)}, u32[]{:S(2)}, u32[]{:S(2)}) collective-permute-start(bf16[256,128]{1,0:T(8,128)(2,1)S(1)} %get-tuple-element.24), channel_id=1, source_target_pairs={{0,8},{8,0},{1,9},{9,1},{2,10},{10,2},{3,11},{11,3},{4,12},{12,4},... | collective-permute-start | bytes 196616 | tf_op jit(solution)/shard_map/ppermute | solution.py:214
  63.7 0.3 shard_map.45.inner
  64.0 1.9 %collective-permute-start.8 = (bf16[512,128]{1,0:T(8,128)(2,1)S(1)}, bf16[512,128]{1,0:T(8,128)(2,1)S(1)}, u32[]{:S(2)}, u32[]{:S(2)}) collective-permute-start(bf16[512,128]{1,0:T(8,128)(2,1)S(1)} %shard_map.45.inner), channel_id=1, source_target_pairs={{0,1},{1,0},{2,3},{3,2},{4,5},{5,4},{6,7},{7,6},{8,9},{9,8},{10,11... | collective-permute-start | bytes 393224 | tf_op jit(solution)/shard_map/ppermute | solution.py:277
  66.0 0.0 collective-permute-done.6.from_far
  66.0 0.0 collective-permute-done.7.from_near
  66.0 0.3 shard_map.46.outer
  66.3 3.4 %collective-permute-start.9 = (bf16[512,128]{1,0:T(8,128)(2,1)S(1)}, bf16[512,128]{1,0:T(8,128)(2,1)S(1)}, u32[]{:S(2)}, u32[]{:S(2)}) collective-permute-start(bf16[512,128]{1,0:T(8,128)(2,1)S(1)} %shard_map.46.outer), channel_id=1, source_target_pairs={{0,1},{1,0},{2,3},{3,2},{4,5},{5,4},{6,7},{7,6},{8,9},{9,8},{10,11... | collective-permute-start | bytes 393224 | tf_op jit(solution)/shard_map/ppermute | solution.py:279
  69.7 0.6 all-to-all-done.1.far
  70.3 1.2 shard_map.44.third
  71.5 0.0 collective-permute-done.8.inner2
  71.6 2.2 %collective-permute-done.9.outer2 = bf16[512,128]{1,0:T(8,128)(2,1)S(1)} collective-permute-done((bf16[512,128]{1,0:T(8,128)(2,1)S(1)}, bf16[512,128]{1,0:T(8,128)(2,1)S(1)}, u32[]{:S(2)}, u32[]{:S(2)}) %collective-permute-start.9) | collective-permute-done | bytes 131104 | tf_op jit(solution)/shard_map/ppermute | solution.py:279
  73.8 0.5 shard_map.47
  74.3 14.4 %all_to_all.30.parts = bf16[16,32,256]{2,1,0:T(8,128)(2,1)S(1)} all-to-all(bf16[16,32,256]{2,1,0:T(8,128)(2,1)S(1)} %shard_map.47), channel_id=1, replica_groups=mesh['z2'=4,'z1'=4,'xh'=2,'core'=2,'y'=4,'xl'=2] {'z1','xh','core'}, dimensions={0} | all-to-all | bytes 524288 | tf_op jit(solution)/shard_map/all_to_all | solution.py:207
  88.7 20.9 %all_to_all.31.parts = bf16[4,32,256]{2,1,0:T(8,128)(2,1)S(1)} all-to-all(bf16[4,32,256]{2,1,0:T(8,128)(2,1)S(1)} %shard_map.48), channel_id=1, replica_groups=mesh['z2'=4,'z1'=4,'xh'=2,'core'=2,'y'=4,'xl'=2] {'z2'}, dimensions={0} | all-to-all | bytes 131072 | tf_op jit(solution)/shard_map/all_to_all | solution.py:207
  109.7 16.1 %all_to_all.32.gram = bf16[16,32,256]{2,1,0:T(8,128)(2,1)S(1)} all-to-all(bf16[16,32,256]{2,1,0:T(8,128)(2,1)S(1)} %shard_map.49), channel_id=1, replica_groups=mesh['z2'=4,'z1'=4,'xh'=2,'core'=2,'y'=4,'xl'=2] {'z1','xh','core'}, dimensions={0} | all-to-all | bytes 524288 | tf_op jit(solution)/shard_map/all_to_all | solution.py:207
  125.7 0.4 shard_map.50
  126.2 13.5 %all_to_all.33.parts = bf16[8,128,256]{2,1,0:T(8,128)(2,1)S(1)} all-to-all(bf16[8,128,256]{2,1,0:T(8,128)(2,1)S(1)} %shard_map.50), channel_id=1, replica_groups=mesh['z2'=4,'z1'=4,'xh'=2,'core'=2,'y'=4,'xl'=2] {'y','xl'}, dimensions={0} | all-to-all | bytes 1048576 | tf_op jit(solution)/shard_map/all_to_all | solution.py:207
  139.7 0.8 shard_map.51
  (5 shorter events, 0.1 us)
Async XLA Ops:
  2.2 6.1 %copy-start = (bf16[1024,128]{1,0:T(8,128)(2,1)S(1)}, bf16[1024,128]{1,0:T(8,128)(2,1)}, u32[]{:S(2)}) copy-start(bf16[1024,128]{1,0:T(8,128)(2,1)} %param.5) | copy-start | bytes 786436
  2.2 22.7 %all-to-all-start = ((bf16[8,8,16,512]{3,2,1,0:T(8,128)(2,1)}), bf16[8,8,16,512]{3,2,1,0:T(8,128)(2,1)S(1)}, u32[]{:S(2)}, u32[]{:S(2)}) async-start(bf16[8,8,16,512]{3,2,1,0:T(8,128)(2,1)} %shard_map.37), calls=%async_computation | async-start | bytes 2097152 | tf_op jit(solution)/shard_map/all_to_all | solution.py:207
  8.3 16.5 %collective-permute-start = (bf16[256,128]{1,0:T(8,128)(2,1)S(1)}, bf16[256,128]{1,0:T(8,128)(2,1)S(1)}, u32[]{:S(2)}, u32[]{:S(2)}) collective-permute-start(bf16[256,128]{1,0:T(8,128)(2,1)S(1)} %get-tuple-element.28), channel_id=1, source_target_pairs={{0,504},{8,16},{16,8},{24,32},{32,24},{40,48},{48,40},{56,64},{64,... | collective-permute-start | bytes 196616 | tf_op jit(solution)/shard_map/ppermute | solution.py:213
  13.5 11.3 %collective-permute-start.1 = (bf16[256,128]{1,0:T(8,128)(2,1)S(1)}, bf16[256,128]{1,0:T(8,128)(2,1)S(1)}, u32[]{:S(2)}, u32[]{:S(2)}) collective-permute-start(bf16[256,128]{1,0:T(8,128)(2,1)S(1)} %get-tuple-element.25), channel_id=1, source_target_pairs={{0,8},{8,0},{1,9},{9,1},{2,10},{10,2},{3,11},{11,3},{4,12},{12,4},... | collective-permute-start | bytes 196616 | tf_op jit(solution)/shard_map/ppermute | solution.py:214
  25.2 14.6 %collective-permute-start.2 = (bf16[256,128]{1,0:T(8,128)(2,1)S(1)}, bf16[256,128]{1,0:T(8,128)(2,1)S(1)}, u32[]{:S(2)}, u32[]{:S(2)}) collective-permute-start(bf16[256,128]{1,0:T(8,128)(2,1)S(1)} %get-tuple-element.16), channel_id=1, source_target_pairs={{0,504},{8,16},{16,8},{24,32},{32,24},{40,48},{48,40},{56,64},{64,... | collective-permute-start | bytes 196616 | tf_op jit(solution)/shard_map/ppermute | solution.py:213
  30.2 10.2 %collective-permute-start.3 = (bf16[256,128]{1,0:T(8,128)(2,1)S(1)}, bf16[256,128]{1,0:T(8,128)(2,1)S(1)}, u32[]{:S(2)}, u32[]{:S(2)}) collective-permute-start(bf16[256,128]{1,0:T(8,128)(2,1)S(1)} %get-tuple-element.17), channel_id=1, source_target_pairs={{0,8},{8,0},{1,9},{9,1},{2,10},{10,2},{3,11},{11,3},{4,12},{12,4},... | collective-permute-start | bytes 196616 | tf_op jit(solution)/shard_map/ppermute | solution.py:214
  40.7 9.0 %collective-permute-start.4 = (bf16[256,128]{1,0:T(8,128)(2,1)S(1)}, bf16[256,128]{1,0:T(8,128)(2,1)S(1)}, u32[]{:S(2)}, u32[]{:S(2)}) collective-permute-start(bf16[256,128]{1,0:T(8,128)(2,1)S(1)} %get-tuple-element.19), channel_id=1, source_target_pairs={{0,504},{8,16},{16,8},{24,32},{32,24},{40,48},{48,40},{56,64},{64,... | collective-permute-start | bytes 196616 | tf_op jit(solution)/shard_map/ppermute | solution.py:213
  42.7 7.3 %collective-permute-start.5 = (bf16[256,128]{1,0:T(8,128)(2,1)S(1)}, bf16[256,128]{1,0:T(8,128)(2,1)S(1)}, u32[]{:S(2)}, u32[]{:S(2)}) collective-permute-start(bf16[256,128]{1,0:T(8,128)(2,1)S(1)} %get-tuple-element.20), channel_id=1, source_target_pairs={{0,8},{8,0},{1,9},{9,1},{2,10},{10,2},{3,11},{11,3},{4,12},{12,4},... | collective-permute-start | bytes 196616 | tf_op jit(solution)/shard_map/ppermute | solution.py:214
  51.1 19.2 %all-to-all-start.1 = ((bf16[4,1024,128]{2,1,0:T(8,128)(2,1)}), bf16[4,1024,128]{2,1,0:T(8,128)(2,1)}, u32[]{:S(2)}, u32[]{:S(2)}) async-start(bf16[4,1024,128]{2,1,0:T(8,128)(2,1)} %get-tuple-element.21), calls=%async_computation.1 | async-start | bytes 2097152 | tf_op jit(solution)/shard_map/all_to_all | solution.py:207
  55.4 10.6 %collective-permute-start.6 = (bf16[256,128]{1,0:T(8,128)(2,1)S(1)}, bf16[256,128]{1,0:T(8,128)(2,1)S(1)}, u32[]{:S(2)}, u32[]{:S(2)}) collective-permute-start(bf16[256,128]{1,0:T(8,128)(2,1)S(1)} %get-tuple-element.23), channel_id=1, source_target_pairs={{0,504},{8,16},{16,8},{24,32},{32,24},{40,48},{48,40},{56,64},{64,... | collective-permute-start | bytes 196616 | tf_op jit(solution)/shard_map/ppermute | solution.py:213
  57.3 8.7 %collective-permute-start.7 = (bf16[256,128]{1,0:T(8,128)(2,1)S(1)}, bf16[256,128]{1,0:T(8,128)(2,1)S(1)}, u32[]{:S(2)}, u32[]{:S(2)}) collective-permute-start(bf16[256,128]{1,0:T(8,128)(2,1)S(1)} %get-tuple-element.24), channel_id=1, source_target_pairs={{0,8},{8,0},{1,9},{9,1},{2,10},{10,2},{3,11},{11,3},{4,12},{12,4},... | collective-permute-start | bytes 196616 | tf_op jit(solution)/shard_map/ppermute | solution.py:214
  64.0 7.5 %collective-permute-start.8 = (bf16[512,128]{1,0:T(8,128)(2,1)S(1)}, bf16[512,128]{1,0:T(8,128)(2,1)S(1)}, u32[]{:S(2)}, u32[]{:S(2)}) collective-permute-start(bf16[512,128]{1,0:T(8,128)(2,1)S(1)} %shard_map.45.inner), channel_id=1, source_target_pairs={{0,1},{1,0},{2,3},{3,2},{4,5},{5,4},{6,7},{7,6},{8,9},{9,8},{10,11... | collective-permute-start | bytes 393224 | tf_op jit(solution)/shard_map/ppermute | solution.py:277
  66.3 7.5 %collective-permute-start.9 = (bf16[512,128]{1,0:T(8,128)(2,1)S(1)}, bf16[512,128]{1,0:T(8,128)(2,1)S(1)}, u32[]{:S(2)}, u32[]{:S(2)}) collective-permute-start(bf16[512,128]{1,0:T(8,128)(2,1)S(1)} %shard_map.46.outer), channel_id=1, source_target_pairs={{0,1},{1,0},{2,3},{3,2},{4,5},{5,4},{6,7},{7,6},{8,9},{9,8},{10,11... | collective-permute-start | bytes 393224 | tf_op jit(solution)/shard_map/ppermute | solution.py:279
